TPU v7x, 32 devices: a whole 2x2x4 slice. The times are simulated.
32 devices in a mesh: sub: 4 (over z), inner: 8 (over y, x, core).
Axes of the slice: x: 2, y: 2, z: 4, core: 2. Of those that a mesh axis runs over, the one named last changes fastest.
Arguments:
- front_leaf: bfloat16 [20480, 1024], P(('sub', 'inner')), may hold values from -6 to 6
- front_mid: bfloat16 [20480, 1024], P(('sub', 'inner')), may hold values from -6 to 6
- front_top: bfloat16 [20480, 1024], P(('sub', 'inner')), may hold values from -6 to 6
- dinv_leaf: bfloat16 [2048, 256], P('sub'), may hold values from -0.046875 to 0.046875
- dinv_mid: bfloat16 [1024, 256], P('sub'), may hold values from -0.046875 to 0.046875
- dinv_top: bfloat16 [512, 256], P('sub'), may hold values from -0.046875 to 0.046875
- live_rows: int32 [3, 32], P(None, ('sub', 'inner')), may hold values from 320 to 640, as said below
- map_leaf: int32 [20480], P(('sub', 'inner')), may hold values from 0 to 1279, as said below
- map_mid: int32 [20480], P(('sub', 'inner')), may hold values from 0 to 1279, as said below
Outputs:
- contribution: bfloat16 [20480, 512], P(('sub', 'inner'))
Inputs may be any that keep to these rules, and one draw needn't show every extreme that they name: `live_rows`: at each level some device block has all 640 rows live. `map_leaf`: within each block of 640 consecutive entries the codes are distinct and exactly half of them are 640 or more. `map_mid`: within each block of 640 consecutive entries the codes are distinct and exactly half of them are 640 or more.
All inputs are finite; a program needn't handle non-finite values.
Results may differ from a plain program's by a relative error of at most 0.0065.
Values may be sent and summed in bfloat16 or wider, within the bound.
No kernel may reach another device: no remote copies, remote signals or barrier semaphores. Data moves between devices by JAX's collectives and lax.ppermute only.
A program may use at most 64 MiB of HBM per device.

v0:
```python
import jax
import jax.numpy as jnp
from jax import lax
from jax.sharding import PartitionSpec as P

PANEL = 512
BLOCK = 256
NEXT = 512


def swapped(value, axis, bit):
    return lax.ppermute(value, axis, [(i, i ^ 1 << bit) for i in range(lax.axis_size(axis))])


def join_halves(mine_part, other_part, bit_index):
    lower_side = lax.axis_index("sub") >> bit_index & 1 == 0
    return jnp.where(
        lower_side,
        jnp.concatenate([mine_part, other_part], 0),
        jnp.concatenate([other_part, mine_part], 0),
    )


def full_inverse(inv_shard, levels):
    whole_part = inv_shard
    for bit_index in range(levels):
        other_part = swapped(whole_part, "sub", bit_index)
        whole_part = join_halves(whole_part, other_part, bit_index)
    return whole_part


def swap_pivots(pivots, bit_index):
    other_part = swapped(pivots, "sub", bit_index)
    return join_halves(pivots, other_part, bit_index)


def factor_level(front_block, inverse, live_count, level_index):
    row_count = front_block.shape[0]
    block_count = PANEL // BLOCK
    panel_part = front_block[:, :PANEL].reshape(row_count, block_count, BLOCK)
    inv_table = inverse.reshape(block_count, BLOCK, BLOCK)
    live_mask = lax.broadcasted_iota(jnp.int32, (row_count, 1), 0) < live_count
    factor = jnp.einsum(
        "rbk,bjk->rbj", panel_part, inv_table, preferred_element_type=jnp.float32
    ).reshape(row_count, PANEL)
    factor = jnp.where(live_mask, factor, 0.0).astype(jnp.bfloat16)
    inner_count = lax.axis_size("inner")
    pivot_count = NEXT // (inner_count << level_index)
    local_pivots = factor[:pivot_count]
    pivots = lax.all_gather(local_pivots, "inner", axis=0, tiled=True)
    for bit_index in range(level_index):
        pivots = swap_pivots(pivots, bit_index)
    product = lax.dot_general(
        factor, pivots, (((1,), (1,)), ((), ())), preferred_element_type=jnp.float32
    )
    update = jnp.where(live_mask, front_block[:, PANEL:].astype(jnp.float32) - product, 0.0)
    return update.astype(jnp.bfloat16)


def extend_add(update, code_map, parent, level_index):
    row_count = update.shape[0]
    col_count = update.shape[1]
    half_rows = row_count // 2
    outward = code_map >= row_count
    own_index = jnp.where(outward, row_count, code_map)
    own_sum = (
        jnp.zeros((row_count, col_count), jnp.float32)
        .at[own_index]
        .add(update.astype(jnp.float32), mode="drop")
    )
    position = jnp.cumsum(outward.astype(jnp.int32)) - 1
    target_slot = jnp.where(outward, position, half_rows)
    picked = (
        jnp.zeros((half_rows,), jnp.int32)
        .at[target_slot]
        .set(lax.iota(jnp.int32, row_count), mode="drop")
    )
    sent_rows = update[picked]
    sent_target = code_map[picked] - row_count
    got_rows, got_target = swapped((sent_rows, sent_target), "sub", level_index)
    far_sum = (
        jnp.zeros((row_count, col_count), jnp.float32)
        .at[got_target]
        .add(got_rows.astype(jnp.float32))
    )
    merged = parent[:, :col_count].astype(jnp.float32) + own_sum + far_sum
    return jnp.concatenate([merged.astype(jnp.bfloat16), parent[:, col_count:]], 1)


def per_device(
    front_leaf, front_mid, front_top, dinv_leaf, dinv_mid, dinv_top, live_rows, map_leaf, map_mid
):
    inverse_mid = full_inverse(dinv_mid, 1)
    inverse_top = full_inverse(dinv_top, 2)
    update = factor_level(front_leaf, dinv_leaf, live_rows[0, 0], 0)
    parent = extend_add(update, map_leaf, front_mid, 0)
    update = factor_level(parent, inverse_mid, live_rows[1, 0], 1)
    parent = extend_add(update, map_mid, front_top, 1)
    return factor_level(parent, inverse_top, live_rows[2, 0], 2)


def solution(mesh):
    placed = (
        P(("sub", "inner"), None),
        P(("sub", "inner"), None),
        P(("sub", "inner"), None),
        P("sub", None),
        P("sub", None),
        P("sub", None),
        P(None, ("sub", "inner")),
        P(("sub", "inner")),
        P(("sub", "inner")),
    )
    return jax.shard_map(
        per_device, mesh=mesh, in_specs=placed, out_specs=P(("sub", "inner"), None), check_vma=False
    )
```

profile of v0, /device:TPU:0, one launch (start us, length us, event | category | flops | bytes accessed | tf_op | source)
XLA Modules:
  0.0 127.4 jit_solution(17495285901685694323)
XLA Ops:
  0.0 1.4 %fusion.40 = (s32[1,1]{0,1:T(1,128)}, s32[1,1]{0,1:T(1,128)}, s32[1,1]{0,1:T(1,128)}) fusion(s32[3,1]{0,1:T(1,128)} %param.15), kind=kLoop, calls=%fused_computation.89 | loop fusion | bytes 24 | tf_op jit(solution)/shard_map/slice | solution.py:99
  3.3 11.5 %all_gather.9 = bf16[512,512]{1,0:T(8,128)(2,1)S(1)} all-gather(bf16[64,512]{1,0:T(8,128)(2,1)S(1)} %slice.74), channel_id=1, replica_groups=mesh['sub'=4,'inner'=8] {'inner'}, dimensions={0}, use_global_device_ids=true | all-gather | bytes 589824 | tf_op jit(solution)/shard_map/all_gather | solution.py:50
  16.1 4.1 %scatter_custom_fusion.1 = s32[320]{0:T(512)S(1)} fusion(s32[640]{0:T(1024)S(1)} %get-tuple-element.7, s32[640]{0:T(1024)S(1)} %iota.25, s32[]{:T(128)} %constant.11.clone.1), kind=kCustom, calls=%fused_computation.85 | custom fusion | bytes 1284 | tf_op jit(solution)/shard_map/scatter | solution.py:76
  20.2 2.0 %gather_fusion.1 = bf16[320,512]{1,0:T(8,128)(2,1)S(1)} fusion(bf16[640,512]{1,0:T(8,128)(2,1)S(1)} %fusion.3, s32[1024]{0:T(1024)S(1)} %pad_clamp_fusion.1), kind=kCustom, calls=%fused_computation.1 | custom fusion | bytes 656640 | tf_op jit(solution)/shard_map/gather | solution.py:78
  22.2 1.6 %collective-permute-start.4 = (bf16[320,512]{1,0:T(8,128)(2,1)S(1)}, bf16[320,512]{1,0:T(8,128)(2,1)S(1)}, u32[]{:S(2)}, u32[]{:S(2)}) collective-permute-start(bf16[320,512]{1,0:T(8,128)(2,1)S(1)} %gather_fusion.1), channel_id=1, source_target_pairs={{0,8},{8,0},{16,24},{24,16},{1,9},{9,1},{17,25},{25,17},{2,10},{10... | collective-permute-start | bytes 983048 | tf_op jit(solution)/shard_map/ppermute | solution.py:12
  23.9 1.7 %gather_fusion = s32[320]{0:T(512)S(1)} fusion(s32[640]{0:T(1024)S(1)} %copy-done.1, s32[1024]{0:T(1024)S(1)} %pad_clamp_fusion.1), kind=kCustom, calls=%fused_computation | custom fusion | bytes 3840 | tf_op jit(solution)/shard_map/gather | solution.py:79
  26.1 1.6 %collective-permute-start.2 = (bf16[256,256]{1,0:T(8,128)(2,1)S(1)}, bf16[256,256]{1,0:T(8,128)(2,1)S(1)}, u32[]{:S(2)}, u32[]{:S(2)}) collective-permute-start(bf16[256,256]{1,0:T(8,128)(2,1)S(1)} %copy-done.6), channel_id=1, source_target_pairs={{0,8},{8,0},{16,24},{24,16},{1,9},{9,1},{17,25},{25,17},{2,10},{10... | collective-permute-start | bytes 393224 | tf_op jit(solution)/shard_map/ppermute | solution.py:12
  28.3 4.1 %scatter_custom_fusion.4 = s32[320]{0:T(512)S(1)} fusion(s32[640]{0:T(1024)S(1)} %get-tuple-element.5, s32[640]{0:T(1024)S(1)} %iota.26, s32[]{:T(128)} %constant.11.clone.1), kind=kCustom, calls=%fused_computation.83 | custom fusion | bytes 1284 | tf_op jit(solution)/shard_map/scatter | solution.py:76
  32.4 1.7 %gather_fusion.2 = s32[320]{0:T(512)S(1)} fusion(s32[640]{0:T(1024)S(1)} %copy-done.2, s32[1024]{0:T(1024)S(1)} %pad_clamp_fusion), kind=kCustom, calls=%fused_computation.2 | custom fusion | bytes 3840 | tf_op jit(solution)/shard_map/gather | solution.py:79
  34.1 2.7 %collective-permute-start.6 = (s32[320]{0:T(512)S(1)}, s32[320]{0:T(512)S(1)}, u32[]{:S(2)}, u32[]{:S(2)}) collective-permute-start(s32[320]{0:T(512)S(1)} %broadcast_add_fusion), channel_id=1, source_target_pairs={{0,16},{8,24},{16,0},{24,8},{1,17},{9,25},{17,1},{25,9},{2,18},{10... | collective-permute-start | bytes 3848 | tf_op jit(solution)/shard_map/ppermute | solution.py:12
  39.6 7.6 %scatter_custom_fusion = f32[640,512]{1,0:T(8,128)S(1)} fusion(f32[640,512]{1,0:T(8,128)S(1)} %slice_convert_fusion, s32[640]{0:T(1024)S(1)} %get-tuple-element.8, bf16[640,512]{1,0:T(8,128)(2,1)S(1)} %fusion.3), kind=kCustom, calls=%fused_computation.25 | custom fusion | flops 655360 | bytes 1966080 | tf_op jit(solution)/shard_map/scatter-add | solution.py:69
  47.9 3.0 %scatter_custom_fusion.2 = f32[640,512]{1,0:T(8,128)S(1)} fusion(s32[320]{0:T(512)} %compare_select_fusion.6, bf16[320,512]{1,0:T(8,128)(2,1)S(1)} %collective-permute-done.4, f32[]{:T(128)} %constant.13.clone.1), kind=kCustom, calls=%fused_computation.36 | custom fusion | flops 327680 | bytes 1638912 | tf_op jit(solution)/shard_map/scatter-add | solution.py:84
  52.2 9.4 %all_gather.10 = bf16[256,512]{1,0:T(8,128)(2,1)S(1)} all-gather(bf16[32,512]{1,0:T(8,128)(2,1)S(1)} %slice.75), channel_id=1, replica_groups=mesh['sub'=4,'inner'=8] {'inner'}, dimensions={0}, use_global_device_ids=true | all-gather | bytes 294912 | tf_op jit(solution)/shard_map/all_gather | solution.py:50
  61.6 1.6 %collective-permute-start.5 = (bf16[256,512]{1,0:T(8,128)(2,1)S(1)}, bf16[256,512]{1,0:T(8,128)(2,1)}, u32[]{:S(2)}, u32[]{:S(2)}) collective-permute-start(bf16[256,512]{1,0:T(8,128)(2,1)S(1)} %all_gather.10), channel_id=1, source_target_pairs={{0,8},{8,0},{16,24},{24,16},{1,9},{9,1},{17,25},{25,17},{2,10},{10... | collective-permute-start | bytes 786440 | tf_op jit(solution)/shard_map/ppermute | solution.py:12
  65.4 6.3 %collective-permute-done.5 = bf16[256,512]{1,0:T(8,128)(2,1)} collective-permute-done((bf16[256,512]{1,0:T(8,128)(2,1)S(1)}, bf16[256,512]{1,0:T(8,128)(2,1)}, u32[]{:S(2)}, u32[]{:S(2)}) %collective-permute-start.5) | collective-permute-done | bytes 262176 | tf_op jit(solution)/shard_map/ppermute | solution.py:12
  71.7 1.8 %fusion.4 = bf16[640,512]{1,0:T(8,128)(2,1)S(1)} fusion(bf16[640,1024]{1,0:T(8,128)(2,1)} %param.10, pred[640]{0:T(1024)(128)(4,1)S(1)} %copy-done.8, bf16[256,512]{1,0:T(8,128)(2,1)} %collective-permute-done.5, bf16[256,512]{1,0:T(8,128)(2,1)S(1)} %all_gather.10, pred[]{:T(512)S(6)} %eq.5, bf16[640,512]{1,0:T(8,128)(2,1)S(1)} %copy.23), kind=kOutput, calls=%fused_computation.17 | convolution fusion | flops 339542016 | bytes 2492417 | tf_op jit(solution)/shard_map/dot_general | solution.py:53
  73.5 2.0 %gather_fusion.3 = bf16[320,512]{1,0:T(8,128)(2,1)S(1)} fusion(bf16[640,512]{1,0:T(8,128)(2,1)S(1)} %fusion.4, s32[1024]{0:T(1024)S(1)} %pad_clamp_fusion), kind=kCustom, calls=%fused_computation.3 | custom fusion | bytes 656640 | tf_op jit(solution)/shard_map/gather | solution.py:78
  76.4 7.4 %scatter_custom_fusion.3 = f32[640,512]{1,0:T(8,128)S(1)} fusion(f32[640,512]{1,0:T(8,128)S(1)} %slice_convert_fusion.1, s32[640]{0:T(1024)S(1)} %get-tuple-element.6, bf16[640,512]{1,0:T(8,128)(2,1)S(1)} %fusion.4), kind=kCustom, calls=%fused_computation.21 | custom fusion | flops 655360 | bytes 1966080 | tf_op jit(solution)/shard_map/scatter-add | solution.py:69
  83.9 8.9 %collective-permute-done.7 = bf16[320,512]{1,0:T(8,128)(2,1)} collective-permute-done((bf16[320,512]{1,0:T(8,128)(2,1)S(1)}, bf16[320,512]{1,0:T(8,128)(2,1)}, u32[]{:S(2)}, u32[]{:S(2)}) %collective-permute-start.7) | collective-permute-done | bytes 327712 | tf_op jit(solution)/shard_map/ppermute | solution.py:12
  92.7 3.5 %scatter_custom_fusion.5 = f32[640,512]{1,0:T(8,128)S(1)} fusion(s32[320]{0:T(512)S(1)} %compare_select_fusion.4, bf16[320,512]{1,0:T(8,128)(2,1)} %collective-permute-done.7, f32[]{:T(128)} %constant.13.clone.1), kind=kCustom, calls=%fused_computation.34 | custom fusion | flops 327680 | bytes 1638404 | tf_op jit(solution)/shard_map/scatter-add | solution.py:84
  97.5 8.4 %all_gather.11 = bf16[128,512]{1,0:T(8,128)(2,1)S(1)} all-gather(bf16[16,512]{1,0:T(8,128)(2,1)S(1)} %slice.76), channel_id=1, replica_groups=mesh['sub'=4,'inner'=8] {'inner'}, dimensions={0}, use_global_device_ids=true | all-gather | bytes 147456 | tf_op jit(solution)/shard_map/all_gather | solution.py:50
  105.8 5.8 %collective-permute-done.8 = bf16[128,512]{1,0:T(8,128)(2,1)S(1)} collective-permute-done((bf16[128,512]{1,0:T(8,128)(2,1)S(1)}, bf16[128,512]{1,0:T(8,128)(2,1)S(1)}, u32[]{:S(2)}, u32[]{:S(2)}) %collective-permute-start.8) | collective-permute-done | bytes 131104 | tf_op jit(solution)/shard_map/ppermute | solution.py:12
  112.2 13.8 %collective-permute-done.9 = bf16[256,512]{1,0:T(8,128)(2,1)S(1)} collective-permute-done((bf16[256,512]{1,0:T(8,128)(2,1)S(1)}, bf16[256,512]{1,0:T(8,128)(2,1)S(1)}, u32[]{:S(2)}, u32[]{:S(2)}) %collective-permute-start.9) | collective-permute-done | bytes 262176 | tf_op jit(solution)/shard_map/ppermute | solution.py:12
  126.0 1.4 %fusion.5 = bf16[640,512]{1,0:T(8,128)(2,1)} fusion(bf16[640,1024]{1,0:T(8,128)(2,1)S(1)} %copy-done.5, pred[640]{0:T(1024)(128)(4,1)S(1)} %iota_compare_fusion.2, bf16[256,512]{1,0:T(8,128)(2,1)S(1)} %collective-permute-done.9, bf16[256,512]{1,0:T(8,128)(2,1)S(1)} %maximum_select_fusion.6, pred[]{:T(512)S(6)} %eq.4, bf16[640,512]{1,0:T(8,128)(2,1)S(1)} %copy.24), kind=kOutput, calls=%fused_computation.18 | convolution fusion | flops 339542016 | bytes 2492417 | tf_op jit(solution)/shard_map/dot_general | solution.py:53
  (79 shorter events, 13.8 us)
Async XLA Ops:
  0.0 2.4 %copy-start = (bf16[512,256]{1,0:T(8,128)(2,1)S(1)}, bf16[512,256]{1,0:T(8,128)(2,1)}, u32[]{:S(2)}) copy-start(bf16[512,256]{1,0:T(8,128)(2,1)} %param.12) | copy-start | bytes 786436
  0.0 2.1 %slice-start = ((bf16[640,1024]{1,0:T(8,128)(2,1)}), bf16[640,512]{1,0:T(8,128)(2,1)S(1)}, s32[]{:S(2)}) async-start(bf16[640,1024]{1,0:T(8,128)(2,1)} %param.9), calls=%async_computation | async-start | bytes 1310720 | tf_op jit(solution)/shard_map/slice | solution.py:40
  3.1 11.7 %copy-start.3 = (bf16[640,1024]{1,0:T(8,128)(2,1)S(1)}, bf16[640,1024]{1,0:T(8,128)(2,1)}, u32[]{:S(2)}) copy-start(bf16[640,1024]{1,0:T(8,128)(2,1)} %param.9) | copy-start | bytes 3932164
  14.8 0.7 copy-start.1
  22.2 3.9 %copy-start.6 = (bf16[256,256]{1,0:T(8,128)(2,1)S(1)}, bf16[256,256]{1,0:T(8,128)(2,1)}, u32[]{:S(2)}) copy-start(bf16[256,256]{1,0:T(8,128)(2,1)} %param.13) | copy-start | bytes 393220
  22.2 5.5 %copy-start.2 = (s32[640]{0:T(1024)S(1)}, s32[640]{0:T(1024)}, u32[]{:S(2)}) copy-start(s32[640]{0:T(1024)} %param.17) | copy-start | bytes 7684
  22.2 25.7 %collective-permute-start.4 = (bf16[320,512]{1,0:T(8,128)(2,1)S(1)}, bf16[320,512]{1,0:T(8,128)(2,1)S(1)}, u32[]{:S(2)}, u32[]{:S(2)}) collective-permute-start(bf16[320,512]{1,0:T(8,128)(2,1)S(1)} %gather_fusion.1), channel_id=1, source_target_pairs={{0,8},{8,0},{16,24},{24,16},{1,9},{9,1},{17,25},{25,17},{2,10},{10... | collective-permute-start | bytes 983048 | tf_op jit(solution)/shard_map/ppermute | solution.py:12
  25.6 11.2 %copy-start.7 = (bf16[128,256]{1,0:T(8,128)(2,1)S(1)}, bf16[128,256]{1,0:T(8,128)(2,1)}, u32[]{:S(2)}) copy-start(bf16[128,256]{1,0:T(8,128)(2,1)} %param.14) | copy-start | bytes 196612
  25.6 21.6 %collective-permute-start.3 = (s32[320]{0:T(512)S(1)}, s32[320]{0:T(512)S(1)}, u32[]{:S(2)}, u32[]{:S(2)}) collective-permute-start(s32[320]{0:T(512)S(1)} %broadcast_add_fusion.1), channel_id=1, source_target_pairs={{0,8},{8,0},{16,24},{24,16},{1,9},{9,1},{17,25},{25,17},{2,10},{10... | collective-permute-start | bytes 3848 | tf_op jit(solution)/shard_map/ppermute | solution.py:12
  26.1 21.7 %collective-permute-start.2 = (bf16[256,256]{1,0:T(8,128)(2,1)S(1)}, bf16[256,256]{1,0:T(8,128)(2,1)S(1)}, u32[]{:S(2)}, u32[]{:S(2)}) collective-permute-start(bf16[256,256]{1,0:T(8,128)(2,1)S(1)} %copy-done.6), channel_id=1, source_target_pairs={{0,8},{8,0},{16,24},{24,16},{1,9},{9,1},{17,25},{25,17},{2,10},{10... | collective-permute-start | bytes 393224 | tf_op jit(solution)/shard_map/ppermute | solution.py:12
  34.1 42.2 %collective-permute-start.6 = (s32[320]{0:T(512)S(1)}, s32[320]{0:T(512)S(1)}, u32[]{:S(2)}, u32[]{:S(2)}) collective-permute-start(s32[320]{0:T(512)S(1)} %broadcast_add_fusion), channel_id=1, source_target_pairs={{0,16},{8,24},{16,0},{24,8},{1,17},{9,25},{17,1},{25,9},{2,18},{10... | collective-permute-start | bytes 3848 | tf_op jit(solution)/shard_map/ppermute | solution.py:12
  36.7 27.3 %collective-permute-start = (bf16[128,256]{1,0:T(8,128)(2,1)S(1)}, bf16[128,256]{1,0:T(8,128)(2,1)}, u32[]{:S(2)}, u32[]{:S(2)}) collective-permute-start(bf16[128,256]{1,0:T(8,128)(2,1)S(1)} %copy-done.7), channel_id=1, source_target_pairs={{0,8},{8,0},{16,24},{24,16},{1,9},{9,1},{17,25},{25,17},{2,10},{10... | collective-permute-start | bytes 196616 | tf_op jit(solution)/shard_map/ppermute | solution.py:12
  51.2 0.7 copy-start.8
  51.9 11.3 %copy-start.4 = (bf16[640,1024]{1,0:T(8,128)(2,1)S(1)}, bf16[640,1024]{1,0:T(8,128)(2,1)}, u32[]{:S(2)}) copy-start(bf16[640,1024]{1,0:T(8,128)(2,1)} %param.11) | copy-start | bytes 3932164
  61.6 10.1 %collective-permute-start.5 = (bf16[256,512]{1,0:T(8,128)(2,1)S(1)}, bf16[256,512]{1,0:T(8,128)(2,1)}, u32[]{:S(2)}, u32[]{:S(2)}) collective-permute-start(bf16[256,512]{1,0:T(8,128)(2,1)S(1)} %all_gather.10), channel_id=1, source_target_pairs={{0,8},{8,0},{16,24},{24,16},{1,9},{9,1},{17,25},{25,17},{2,10},{10... | collective-permute-start | bytes 786440 | tf_op jit(solution)/shard_map/ppermute | solution.py:12
  65.0 11.3 %collective-permute-start.1 = (bf16[256,256]{1,0:T(8,128)(2,1)S(1)}, bf16[256,256]{1,0:T(8,128)(2,1)S(1)}, u32[]{:S(2)}, u32[]{:S(2)}) collective-permute-start(bf16[256,256]{1,0:T(8,128)(2,1)S(1)} %maximum_select_fusion.7), channel_id=1, source_target_pairs={{0,16},{8,24},{16,0},{24,8},{1,17},{9,25},{17,1},{25,9},{2,18},{10... | collective-permute-start | bytes 393224 | tf_op jit(solution)/shard_map/ppermute | solution.py:12
  75.5 17.2 %collective-permute-start.7 = (bf16[320,512]{1,0:T(8,128)(2,1)S(1)}, bf16[320,512]{1,0:T(8,128)(2,1)}, u32[]{:S(2)}, u32[]{:S(2)}) collective-permute-start(bf16[320,512]{1,0:T(8,128)(2,1)S(1)} %gather_fusion.3), channel_id=1, source_target_pairs={{0,16},{8,24},{16,0},{24,8},{1,17},{9,25},{17,1},{25,9},{2,18},{10... | collective-permute-start | bytes 983048 | tf_op jit(solution)/shard_map/ppermute | solution.py:12
  97.2 28.8 %copy-start.5 = (bf16[640,1024]{1,0:T(8,128)(2,1)S(1)}, bf16[640,1024]{1,0:T(8,128)(2,1)}, u32[]{:S(2)}) copy-start(bf16[640,1024]{1,0:T(8,128)(2,1)} %param.11) | copy-start | bytes 3932164
  105.8 5.8 %collective-permute-start.8 = (bf16[128,512]{1,0:T(8,128)(2,1)S(1)}, bf16[128,512]{1,0:T(8,128)(2,1)S(1)}, u32[]{:S(2)}, u32[]{:S(2)}) collective-permute-start(bf16[128,512]{1,0:T(8,128)(2,1)S(1)} %all_gather.11), channel_id=1, source_target_pairs={{0,8},{8,0},{16,24},{24,16},{1,9},{9,1},{17,25},{25,17},{2,10},{10... | collective-permute-start | bytes 393224 | tf_op jit(solution)/shard_map/ppermute | solution.py:12
  111.7 14.3 %collective-permute-start.9 = (bf16[256,512]{1,0:T(8,128)(2,1)S(1)}, bf16[256,512]{1,0:T(8,128)(2,1)S(1)}, u32[]{:S(2)}, u32[]{:S(2)}) collective-permute-start(bf16[256,512]{1,0:T(8,128)(2,1)S(1)} %maximum_select_fusion.6), channel_id=1, source_target_pairs={{0,16},{8,24},{16,0},{24,8},{1,17},{9,25},{17,1},{25,9},{2,18},{10... | collective-permute-start | bytes 786440 | tf_op jit(solution)/shard_map/ppermute | solution.py:12
where the time goes:
time: 128 us; the launch traced here: 127 us
  waiting for transfers between devices  34.8 us (27%)
  other arithmetic  29.3 us (23%)
  blocking collectives  29.3 us (23%)
  local copies, waits for them, and re-layouts  18.7 us (15%)
  starting transfers between devices  10.1 us (8%)
  matrix products  4.91 us (4%)
    ppermute x10, waiting for transfers between devices, swapped(): lax.ppermute(value, axis, [(i, i ^ 1 << bit) for i in range(lax.axis_size...  34.8 us
    all_gather x3, blocking collectives, factor_level(): pivots = lax.all_gather(local_pivots, 'inner', axis=0, tiled=True)  29.3 us
    scatter-add x2, other arithmetic, extend_add(): own_sum = jnp.zeros((row_count, col_count), jnp.float32).at[own_index].ad...  15.1 us
    ppermute x10, starting transfers between devices, swapped(): lax.ppermute(value, axis, [(i, i ^ 1 << bit) for i in range(lax.axis_size...  10.1 us
    scatter x2, local copies, waits for them, and re-layouts, extend_add(): picked = jnp.zeros((half_rows,), jnp.int32).at[target_slot].set(lax.iota(...  8.16 us
    scatter-add x2, other arithmetic, extend_add(): far_sum = jnp.zeros((row_count, col_count), jnp.float32).at[got_target].a...  6.42 us
    gather x2, local copies, waits for them, and re-layouts, extend_add(): sent_rows = update[picked]  4.05 us
    dot_general x3, matrix products, factor_level(): lax.dot_general(factor, pivots, (((1,), (1,)), ((), ())), preferred_eleme...  3.75 us
  transfers between devices with their start and end apart: 10, of which 4 were waited for; matrix products, arithmetic and copies ran while one was open for 28% of the time, Pallas kernels for 0%

commit v1 on v0

v1 whole, which is shorter than its diff:
```python
import jax
import jax.numpy as jnp
from jax import lax
from jax.experimental import pallas as pl
from jax.experimental.pallas import tpu as pltpu
from jax.sharding import PartitionSpec as P

BF = jnp.bfloat16
F32 = jnp.float32
NT = (((1,), (1,)), ((), ()))
NN = (((1,), (0,)), ((), ()))


def dot(a, b, dims):
    return lax.dot_general(a, b, dims, preferred_element_type=F32)


def swap(value, axis, mask):
    return lax.ppermute(value, axis, [(i, i ^ mask) for i in range(lax.axis_size(axis))])


def call(body, out_shape, smem=(), n_in=0, name=None):
    vm = pl.BlockSpec(memory_space=pltpu.VMEM)
    sm = pl.BlockSpec(memory_space=pltpu.SMEM)
    specs = [sm if i in smem else vm for i in range(n_in)]
    outs = [jax.ShapeDtypeStruct(s, d) for s, d in out_shape]
    return pl.pallas_call(
        body, in_specs=specs, out_specs=[vm] * len(outs), out_shape=outs, name=name,
        compiler_params=pltpu.CompilerParams(vmem_limit_bytes=50 * 1024 * 1024),
    )


def one_hot(row, count, offset=0):
    ids = lax.broadcasted_iota(jnp.int32, (count, row.shape[1]), 0) + offset
    return jnp.where(ids == row, 1.0, 0.0).astype(BF)


def slots_of(code, rows):
    outward = code >= rows
    flags = jnp.broadcast_to(jnp.where(outward, 1.0, 0.0).astype(BF), (8, rows))
    a = lax.broadcasted_iota(jnp.int32, (rows, rows), 0)
    b = lax.broadcasted_iota(jnp.int32, (rows, rows), 1)
    upper = jnp.where(a < b, 1.0, 0.0).astype(BF)
    rank = dot(flags, upper, NN)[:1].astype(jnp.int32)
    return jnp.where(outward, rank, -1)


def prep_body(map0, map0_far, map1, map1_far, slot0, target0, slot1, target1):
    rows = map0.shape[1]
    for own, far, slot, target in (
        (map0, map0_far, slot0, target0),
        (map1, map1_far, slot1, target1),
    ):
        slot[...] = slots_of(own[...], rows)
        far_code = far[...]
        pick = one_hot(slots_of(far_code, rows), rows // 2)
        row = far_code - rows
        high = row >> 8
        low = row & 255
        high_row = dot(jnp.broadcast_to(high.astype(F32).astype(BF), (8, rows)), pick, NT)[:1]
        low_row = dot(jnp.broadcast_to(low.astype(F32).astype(BF), (8, rows)), pick, NT)[:1]
        target[...] = high_row.astype(jnp.int32) * 256 + low_row.astype(jnp.int32)


def scaled(panel, inverse):
    block = inverse.shape[1]
    parts = [
        dot(panel[:, b * block:(b + 1) * block], inverse[b * block:(b + 1) * block], NT)
        for b in range(inverse.shape[0] // block)
    ]
    return jnp.concatenate(parts, 1)


def reordered(value, outer, middle):
    rows = value.shape[0]
    part = rows // (outer * middle)
    if middle == 1:
        return value
    if part % 16 == 0:
        return jnp.concatenate(
            [value[(o * middle + m) * part:(o * middle + m + 1) * part]
             for m in range(middle) for o in range(outer)], 0)
    target = lax.broadcasted_iota(jnp.int32, (rows, rows), 0)
    source = lax.broadcasted_iota(jnp.int32, (rows, rows), 1)
    k = target % part
    o = target // part % outer
    m = target // (part * outer)
    return dot(jnp.where((o * middle + m) * part + k == source, 1.0, 0.0).astype(BF), value, NN).astype(BF)


def level_math(panel, rest, gathered, inverse, live, middle, inner):
    rows = panel.shape[0]
    mask = lax.broadcasted_iota(jnp.int32, (rows, 1), 0) < live
    factor = jnp.where(mask, scaled(panel, inverse), 0.0).astype(BF)
    pivots = reordered(scaled(gathered, inverse).astype(BF), inner, middle)
    product = dot(factor, pivots, NT)
    return jnp.where(mask, rest.astype(F32) - product, 0.0).astype(BF)


def sends(update, code, slot, pivot_out, bulk_out):
    rows = update.shape[0]
    n = pivot_out.shape[0] // 2
    pick = jnp.concatenate([one_hot(code, n), one_hot(code, n, rows)], 0) if n % 16 == 0 else None
    if pick is None:
        ids = lax.broadcasted_iota(jnp.int32, (2 * n, rows), 0)
        pick = jnp.where(jnp.where(ids < n, ids, ids - n + rows) == code, 1.0, 0.0).astype(BF)
    pivot_out[...] = dot(pick, update, NN).astype(BF)
    bulk_out[...] = dot(one_hot(slot, bulk_out.shape[0]), update, NN).astype(BF)


def merged_own(update, code, parent):
    return parent.astype(F32) + dot(one_hot(code, update.shape[0]), update, NN)


def per_device(front_leaf, front_mid, front_top, dinv_leaf, dinv_mid, dinv_top, live_rows, map_leaf, map_mid):
    rows = front_leaf.shape[0]
    panel = dinv_leaf.shape[0]
    cols = front_leaf.shape[1] - panel
    inner = lax.axis_size("inner")
    half = rows // 2
    n = [cols // (inner << l) for l in range(3)]
    sub = lax.axis_index("sub")
    low0 = sub & 1 == 0
    low1 = sub & 2 == 0

    def pair(mine, other, low):
        return jnp.where(low, jnp.concatenate([mine, other], 0), jnp.concatenate([other, mine], 0))

    code0 = map_leaf.reshape(1, rows)
    code1 = map_mid.reshape(1, rows)
    raw0 = lax.all_gather(front_leaf[:n[0], :panel], "inner", axis=0, tiled=True)
    far0 = swap(code0, "sub", 1)
    far1 = swap(code1, "sub", 2)
    mid_other = swap(dinv_mid, "sub", 1)
    top_other = swap(dinv_top, "sub", 1)
    inv_mid = pair(dinv_mid, mid_other, low0)
    top_pair = pair(dinv_top, top_other, low0)
    inv_top = pair(top_pair, swap(top_pair, "sub", 2), low1)
    mid_head = front_mid[:n[1], :panel]
    top_head = front_top[:n[2], :panel]
    mid_heads = pair(mid_head, swap(mid_head, "sub", 1), low0)
    top_heads = pair(top_head, swap(top_head, "sub", 1), low0)
    top_heads = pair(top_heads, swap(top_heads, "sub", 2), low1)
    slot0, target0, slot1, target1 = call(
        prep_body, [((1, rows), jnp.int32), ((1, half), jnp.int32)] * 2, n_in=4, name="prep"
    )(code0, far0, code1, far1)

    def level0(live, front, gathered, inverse, code, slot, update_out, pivot_out, bulk_out):
        update = level_math(front[:, :panel], front[:, panel:], gathered[...], inverse[...], live[0, 0], 1, inner)
        update_out[...] = update
        sends(update, code[...], slot[...], pivot_out, bulk_out)

    update0, pivot0, bulk0 = call(
        level0, [((rows, cols), BF), ((2 * n[1], cols), BF), ((half, cols), BF)], smem=(0,), n_in=6, name="level0"
    )(live_rows, front_leaf, raw0, dinv_leaf, code0, slot0)
    pivot0_other = swap(pivot0, "sub", 1)
    bulk0_other = swap(bulk0, "sub", 1)

    def own(update, code, parent, out):
        out[...] = merged_own(update[...], code[...], parent[:, :cols])

    merged0, = call(own, [((rows, cols), F32)], n_in=3, name="own0")(update0, code0, front_mid)
    own_sum = pivot0[:n[1]].astype(F32) + pivot0_other[n[1]:].astype(F32)
    far_sum = pivot0_other[:n[1]].astype(F32) + pivot0[n[1]:].astype(F32)
    raw1 = (mid_heads.astype(F32) + pair(own_sum, far_sum, low0)).astype(BF)
    raw1 = lax.all_gather(raw1, "inner", axis=0, tiled=True)

    def level1(live, front, merged, got, target, gathered, inverse, code, slot, update_out, pivot_out, bulk_out):
        landing = lax.broadcasted_iota(jnp.int32, (rows, half), 0) == target[...]
        assembled = (merged[...] + dot(jnp.where(landing, 1.0, 0.0).astype(BF), got[...], NN)).astype(BF)
        update = level_math(assembled, front[:, panel:], gathered[...], inverse[...], live[1, 0], 2, inner)
        update_out[...] = update
        sends(update, code[...], slot[...], pivot_out, bulk_out)

    update1, pivot1, bulk1 = call(
        level1, [((rows, cols), BF), ((2 * n[2], cols), BF), ((half, cols), BF)], smem=(0,), n_in=9, name="level1"
    )(live_rows, front_mid, merged0, bulk0_other, target0, raw1, inv_mid, code1, slot1)
    pivot1_z = [pivot1] + [swap(pivot1, "sub", m) for m in (1, 2, 3)]
    bulk1_other = swap(bulk1, "sub", 2)
    merged1, = call(own, [((rows, cols), F32)], n_in=3, name="own1")(update1, code1, front_top)
    sums = []
    for m in range(4):
        sums.append(pivot1_z[m][:n[2]].astype(F32) + pivot1_z[m ^ 2][n[2]:].astype(F32))
    raw2 = pair(pair(sums[0], sums[1], low0), pair(sums[2], sums[3], low0), low1)
    raw2 = (top_heads.astype(F32) + raw2).astype(BF)
    raw2 = lax.all_gather(raw2, "inner", axis=0, tiled=True)

    def level2(live, front, merged, got, target, gathered, inverse, out):
        landing = lax.broadcasted_iota(jnp.int32, (rows, half), 0) == target[...]
        assembled = (merged[...] + dot(jnp.where(landing, 1.0, 0.0).astype(BF), got[...], NN)).astype(BF)
        out[...] = level_math(assembled, front[:, panel:], gathered[...], inverse[...], live[2, 0], 4, inner)

    out, = call(level2, [((rows, cols), BF)], smem=(0,), n_in=7, name="level2")(
        live_rows, front_top, merged1, bulk1_other, target1, raw2, inv_top
    )
    return out


def solution(mesh):
    row = P(("sub", "inner"), None)
    placed = (
        row, row, row, P("sub", None), P("sub", None), P("sub", None),
        P(None, ("sub", "inner")), P(("sub", "inner")), P(("sub", "inner")),
    )
    return jax.shard_map(per_device, mesh=mesh, in_specs=placed, out_specs=row, check_vma=False)
```

time: 128 us -> 74 us (0.58)
  other arithmetic: 29.3 us -> 0.36 us
  waiting for transfers between devices: 34.8 us -> 8.29 us
  local copies, waits for them, and re-layouts: 18.7 us -> 6.75 us
  Pallas kernels: 0 us -> 10.4 us
  starting transfers between devices: 10.1 us -> 18.9 us
  matrix products: 4.91 us -> 0 us
    ppermute x10 -> x14, waiting for transfers between devices: 34.8 us -> 8.29 us  [swap(): lax.ppermute(value, axis, [(i, i ^ mask) for i in range(lax.axis_size(axi...]
    scatter-add x4 -> x0, other arithmetic: 21.5 us -> none  [the longest x2 15.1 us: extend_add(): own_sum = jnp.zeros((row_count, col_count), jnp.float32).at[own_index].ad...]
    pallas_call x0 -> x6, Pallas kernels: none -> 10.4 us  [the longest x1 3.17 us: per_device(): call(level1, [((rows, cols), BF), ((2 * n[2], cols), BF), ((half, cols),...]
    ppermute x10 -> x14, starting transfers between devices: 10.1 us -> 18.9 us  [swap(): lax.ppermute(value, axis, [(i, i ^ mask) for i in range(lax.axis_size(axi...]
    scatter x2 -> x0, local copies, waits for them, and re-layouts: 8.16 us -> none  [extend_add(): picked = jnp.zeros((half_rows,), jnp.int32).at[target_slot].set(lax.iota(...]
    gather x4 -> x0, local copies, waits for them, and re-layouts: 7.41 us -> none  [the longest x2 4.05 us: extend_add(): sent_rows = update[picked]]
    dot_general x6 -> x0, matrix products: 4.91 us -> none  [the longest x3 3.75 us: factor_level(): lax.dot_general(factor, pivots, (((1,), (1,)), ((), ())), preferred_eleme...]
    convert_element_type x7 -> x2, other arithmetic: 2.69 us -> 0.06 us  [the longest x1 0.03 us: per_device(): raw2 = (top_heads.astype(F32) + raw2).astype(BF)]
  transfers between devices with their start and end apart: 10 -> 14, of which waited for: 4 -> 3; matrix products, arithmetic and copies ran while one was open for 28% -> 6% of each run, Pallas kernels for 0% -> 10%
where the time goes in v1:
time: 74 us; the launch traced here: 73.5 us
  blocking collectives  28.7 us (39%)
  starting transfers between devices  18.9 us (26%)
  Pallas kernels  10.4 us (14%)
  waiting for transfers between devices  8.29 us (11%)
  local copies, waits for them, and re-layouts  6.75 us (9%)
    ppermute x14, starting transfers between devices, swap(): lax.ppermute(value, axis, [(i, i ^ mask) for i in range(lax.axis_size(axi...  18.9 us
    all_gather x1, blocking collectives, per_device(): lax.all_gather(front_leaf[:n[0], :panel], 'inner', axis=0, tiled=True)  9.97 us
    all_gather x1, blocking collectives, per_device(): raw1 = lax.all_gather(raw1, 'inner', axis=0, tiled=True)  9.83 us
    all_gather x1, blocking collectives, per_device(): raw2 = lax.all_gather(raw2, 'inner', axis=0, tiled=True)  8.88 us
    ppermute x14, waiting for transfers between devices, swap(): lax.ppermute(value, axis, [(i, i ^ mask) for i in range(lax.axis_size(axi...  8.29 us
    pallas_call x1, Pallas kernels, per_device(): call(level1, [((rows, cols), BF), ((2 * n[2], cols), BF), ((half, cols),...  3.17 us
    unnamed x15, local copies, waits for them, and re-layouts  3.05 us
    pallas_call x1, Pallas kernels, per_device(): call(level2, [((rows, cols), BF)], smem=(0,), n_in=7, name='level2')  2.74 us
  transfers between devices with their start and end apart: 14, of which 3 were waited for; matrix products, arithmetic and copies ran while one was open for 6% of the time, Pallas kernels for 10%

profile of v1, /device:TPU:0, one launch (start us, length us, event | category | flops | bytes accessed | tf_op | source)
XLA Modules:
  0.0 73.5 jit_solution(10302668890950089083)
XLA Ops:
  0.7 3.1 %collective-permute-start = (s32[1,640]{1,0:T(1,128)S(1)}, s32[1,640]{1,0:T(1,128)S(1)}, u32[]{:S(2)}, u32[]{:S(2)}) collective-permute-start(s32[1,640]{1,0:T(1,128)S(1)} %reshape.6.map0.code), channel_id=1, source_target_pairs={{0,8},{8,0},{16,24},{24,16},{1,9},{9,1},{17,25},{25,17},{2,10},{10... | collective-permute-start | bytes 7688 | tf_op jit(solution)/shard_map/ppermute | solution.py:19
  4.4 2.6 %collective-permute-start.1 = (s32[1,640]{1,0:T(1,128)S(1)}, s32[1,640]{1,0:T(1,128)S(1)}, u32[]{:S(2)}, u32[]{:S(2)}) collective-permute-start(s32[1,640]{1,0:T(1,128)S(1)} %reshape.7.map1.code), channel_id=1, source_target_pairs={{0,16},{8,24},{16,0},{24,8},{1,17},{9,25},{17,1},{25,9},{2,18},{10... | collective-permute-start | bytes 7688 | tf_op jit(solution)/shard_map/ppermute | solution.py:19
  7.0 0.8 %slice.46 = bf16[32,512]{1,0:T(8,128)(2,1)S(1)} slice(bf16[640,1024]{1,0:T(8,128)(2,1)} %front.4), slice={[0:32], [0:512]} | slice | bytes 65536 | tf_op jit(solution)/shard_map/slice | solution.py:139
  8.2 1.6 %collective-permute-start.5 = (bf16[256,256]{1,0:T(8,128)(2,1)}, bf16[256,256]{1,0:T(8,128)(2,1)S(1)}, u32[]{:S(2)}, u32[]{:S(2)}) collective-permute-start(bf16[256,256]{1,0:T(8,128)(2,1)} %param.13), channel_id=1, source_target_pairs={{0,8},{8,0},{16,24},{24,16},{1,9},{9,1},{17,25},{25,17},{2,10},{10... | collective-permute-start | bytes 393224 | tf_op jit(solution)/shard_map/ppermute | solution.py:19
  11.0 0.8 %slice.45 = bf16[64,512]{1,0:T(8,128)(2,1)S(1)} slice(bf16[640,1024]{1,0:T(8,128)(2,1)} %front.3), slice={[0:64], [0:512]} | slice | bytes 131072 | tf_op jit(solution)/shard_map/slice | solution.py:131
  11.8 10.0 %all_gather.9.gathered = bf16[512,512]{1,0:T(8,128)(2,1)S(1)} all-gather(bf16[64,512]{1,0:T(8,128)(2,1)S(1)} %slice.45), channel_id=1, replica_groups=mesh['sub'=4,'inner'=8] {'inner'}, dimensions={0}, use_global_device_ids=true | all-gather | bytes 589824 | tf_op jit(solution)/shard_map/all_gather | solution.py:131
  21.8 0.7 %copy.12.live = s32[3,1]{1,0:T(4,128)S(1)} copy(s32[3,1]{0,1:T(1,128)} %param.15) | data formatting | bytes 24 | tf_op args[6]
  22.5 1.6 %collective-permute-start.12 = (bf16[128,256]{1,0:T(8,128)(2,1)}, bf16[128,256]{1,0:T(8,128)(2,1)S(1)}, u32[]{:S(2)}, u32[]{:S(2)}) collective-permute-start(bf16[128,256]{1,0:T(8,128)(2,1)} %param.14), channel_id=1, source_target_pairs={{0,8},{8,0},{16,24},{24,16},{1,9},{9,1},{17,25},{25,17},{2,10},{10... | collective-permute-start | bytes 196616 | tf_op jit(solution)/shard_map/ppermute | solution.py:19
  24.1 1.1 %prep.1 = (s32[1,640]{1,0:T(1,128)S(1)}, s32[1,320]{1,0:T(1,128)S(1)}, s32[1,640]{1,0:T(1,128)S(1)}, s32[1,320]{1,0:T(1,128)S(1)}) custom-call(s32[1,640]{1,0:T(1,128)S(1)} %reshape.6.map0.code, s32[1,640]{1,0:T(1,128)S(1)} %collective-permute-done.map0_far, s32[1,640]{1,0:T(1,128)S(1)} %reshape.7.map1.code, s32[1,640]{1,0:T(1,128)S(1)} %collective-permute-done.1.map1_far), custom_call_target="tpu_custom_call" | custom-call | tf_op jit(solution)/shard_map/prep/pallas_call | solution.py:144
  25.3 1.3 %copy-done.3 = bf16[640,1024]{1,0:T(8,128)(2,1)S(1)} copy-done((bf16[640,1024]{1,0:T(8,128)(2,1)S(1)}, bf16[640,1024]{1,0:T(8,128)(2,1)}, u32[]{:S(2)}) %copy-start.3) | copy-done | bytes 1310744
  26.6 0.9 %copy-done.4 = bf16[512,256]{1,0:T(8,128)(2,1)S(1)} copy-done((bf16[512,256]{1,0:T(8,128)(2,1)S(1)}, bf16[512,256]{1,0:T(8,128)(2,1)}, u32[]{:S(2)}) %copy-start.4) | copy-done | bytes 262168
  27.5 2.0 %level0.1 = (bf16[640,512]{1,0:T(8,128)(2,1)S(1)}, bf16[64,512]{1,0:T(8,128)(2,1)S(1)}, bf16[320,512]{1,0:T(8,128)(2,1)S(1)}) custom-call(s32[3,1]{1,0:T(4,128)S(1)} %copy.12.live, bf16[640,1024]{1,0:T(8,128)(2,1)S(1)} %copy-done.3, bf16[512,512]{1,0:T(8,128)(2,1)S(1)} %all_gather.9.gathered, bf16[512,256]{1,0:T(8,128)(2,1)S(1)} %copy-done.4, ...), custom_call_target="tpu_custom_call" | custom-call | tf_op jit(solution)/shard_map/level0/pallas_call | solution.py:153
  30.8 1.6 %collective-permute-start.2 = (bf16[320,512]{1,0:T(8,128)(2,1)S(1)}, bf16[320,512]{1,0:T(8,128)(2,1)S(1)}, u32[]{:S(2)}, u32[]{:S(2)}) collective-permute-start(bf16[320,512]{1,0:T(8,128)(2,1)S(1)} %get-tuple-element.17), channel_id=1, source_target_pairs={{0,8},{8,0},{16,24},{24,16},{1,9},{9,1},{17,25},{25,17},{2,10},{10... | collective-permute-start | bytes 983048 | tf_op jit(solution)/shard_map/ppermute | solution.py:19
  32.9 1.6 %collective-permute-done.4 = bf16[64,512]{1,0:T(8,128)(2,1)S(1)} collective-permute-done((bf16[64,512]{1,0:T(8,128)(2,1)S(1)}, bf16[64,512]{1,0:T(8,128)(2,1)S(1)}, u32[]{:S(2)}, u32[]{:S(2)}) %collective-permute-start.4) | collective-permute-done | bytes 65568 | tf_op jit(solution)/shard_map/ppermute | solution.py:19
  34.5 1.0 %collective-permute-start.13 = (bf16[256,256]{1,0:T(8,128)(2,1)S(1)}, bf16[256,256]{1,0:T(8,128)(2,1)S(1)}, u32[]{:S(2)}, u32[]{:S(2)}) collective-permute-start(bf16[256,256]{1,0:T(8,128)(2,1)S(1)} %maximum_select_fusion.4), channel_id=1, source_target_pairs={{0,16},{8,24},{16,0},{24,8},{1,17},{9,25},{17,1},{25,9},{2,18},{10... | collective-permute-start | bytes 393224 | tf_op jit(solution)/shard_map/ppermute | solution.py:19
  35.6 9.8 %all_gather.10.gathered = bf16[512,512]{1,0:T(8,128)(2,1)S(1)} all-gather(bf16[64,512]{1,0:T(8,128)(2,1)S(1)} %fusion.1), channel_id=1, replica_groups=mesh['sub'=4,'inner'=8] {'inner'}, dimensions={0}, use_global_device_ids=true | all-gather | bytes 589824 | tf_op jit(solution)/shard_map/all_gather | solution.py:166
  45.6 3.2 %level1.1 = (bf16[640,512]{1,0:T(8,128)(2,1)S(1)}, bf16[32,512]{1,0:T(8,128)(2,1)S(1)}, bf16[320,512]{1,0:T(8,128)(2,1)S(1)}) custom-call(s32[3,1]{1,0:T(4,128)S(1)} %copy.12.live, bf16[640,1024]{1,0:T(8,128)(2,1)S(1)} %copy-done, f32[640,512]{1,0:T(8,128)} %copy-done.2, bf16[320,512]{1,0:T(8,128)(2,1)S(1)} %collective-permute-done.2.got, ...), custom_call_target="tpu_custom_call" | custom-call | tf_op jit(solution)/shard_map/level1/pallas_call | solution.py:175
  48.8 2.0 %collective-permute-start.9 = (bf16[32,512]{1,0:T(8,128)(2,1)S(1)}, bf16[32,512]{1,0:T(8,128)(2,1)S(1)}, u32[]{:S(2)}, u32[]{:S(2)}) collective-permute-start(bf16[32,512]{1,0:T(8,128)(2,1)S(1)} %get-tuple-element.24), channel_id=1, source_target_pairs={{0,16},{8,24},{16,0},{24,8},{1,17},{9,25},{17,1},{25,9},{2,18},{10... | collective-permute-start | bytes 98312 | tf_op jit(solution)/shard_map/ppermute | solution.py:19
  51.0 2.5 %collective-permute-start.11 = (bf16[32,512]{1,0:T(8,128)(2,1)S(1)}, bf16[32,512]{1,0:T(8,128)(2,1)S(1)}, u32[]{:S(2)}, u32[]{:S(2)}) collective-permute-start(bf16[32,512]{1,0:T(8,128)(2,1)S(1)} %get-tuple-element.24), channel_id=1, source_target_pairs={{0,24},{8,16},{16,8},{24,0},{1,25},{9,17},{17,9},{25,1},{2,26},{10... | collective-permute-start | bytes 98312 | tf_op jit(solution)/shard_map/ppermute | solution.py:19
  54.1 1.1 %collective-permute-start.6 = (bf16[320,512]{1,0:T(8,128)(2,1)S(1)}, bf16[320,512]{1,0:T(8,128)(2,1)S(1)}, u32[]{:S(2)}, u32[]{:S(2)}) collective-permute-start(bf16[320,512]{1,0:T(8,128)(2,1)S(1)} %get-tuple-element.22), channel_id=1, source_target_pairs={{0,16},{8,24},{16,0},{24,8},{1,17},{9,25},{17,1},{25,9},{2,18},{10... | collective-permute-start | bytes 983048 | tf_op jit(solution)/shard_map/ppermute | solution.py:19
  55.2 1.8 %collective-permute-done.11 = bf16[32,512]{1,0:T(8,128)(2,1)S(1)} collective-permute-done((bf16[32,512]{1,0:T(8,128)(2,1)S(1)}, bf16[32,512]{1,0:T(8,128)(2,1)S(1)}, u32[]{:S(2)}, u32[]{:S(2)}) %collective-permute-start.11) | collective-permute-done | bytes 32800 | tf_op jit(solution)/shard_map/ppermute | solution.py:19
  57.1 8.9 %all_gather.11.gathered = bf16[512,512]{1,0:T(8,128)(2,1)S(1)} all-gather(bf16[64,512]{1,0:T(8,128)(2,1)S(1)} %fusion.3), channel_id=1, replica_groups=mesh['sub'=4,'inner'=8] {'inner'}, dimensions={0}, use_global_device_ids=true | all-gather | bytes 589824 | tf_op jit(solution)/shard_map/all_gather | solution.py:186
  66.0 4.8 %collective-permute-done.6.got = bf16[320,512]{1,0:T(8,128)(2,1)S(1)} collective-permute-done((bf16[320,512]{1,0:T(8,128)(2,1)S(1)}, bf16[320,512]{1,0:T(8,128)(2,1)S(1)}, u32[]{:S(2)}, u32[]{:S(2)}) %collective-permute-start.6) | collective-permute-done | bytes 327712 | tf_op jit(solution)/shard_map/ppermute | solution.py:19
  70.8 2.7 %level2.1 = bf16[640,512]{1,0:T(8,128)(2,1)} custom-call(s32[3,1]{1,0:T(4,128)S(1)} %copy.12.live, bf16[640,1024]{1,0:T(8,128)(2,1)S(1)} %copy-done.1, f32[640,512]{1,0:T(8,128)S(1)} %own1.1.merged, bf16[320,512]{1,0:T(8,128)(2,1)S(1)} %collective-permute-done.6.got, s32[1,320]{1,0:T(1,128)S(1)} %get-tuple-element.23.target, ...), custom_call_target="tpu_custom_call" | custom-call | tf_op jit(solution)/shard_map/level2/pallas_call | solution.py:193
  (43 shorter events, 5.7 us)
Async XLA Ops:
  0.7 21.9 %collective-permute-start = (s32[1,640]{1,0:T(1,128)S(1)}, s32[1,640]{1,0:T(1,128)S(1)}, u32[]{:S(2)}, u32[]{:S(2)}) collective-permute-start(s32[1,640]{1,0:T(1,128)S(1)} %reshape.6.map0.code), channel_id=1, source_target_pairs={{0,8},{8,0},{16,24},{24,16},{1,9},{9,1},{17,25},{25,17},{2,10},{10... | collective-permute-start | bytes 7688 | tf_op jit(solution)/shard_map/ppermute | solution.py:19
  4.4 19.7 %collective-permute-start.1 = (s32[1,640]{1,0:T(1,128)S(1)}, s32[1,640]{1,0:T(1,128)S(1)}, u32[]{:S(2)}, u32[]{:S(2)}) collective-permute-start(s32[1,640]{1,0:T(1,128)S(1)} %reshape.7.map1.code), channel_id=1, source_target_pairs={{0,16},{8,24},{16,0},{24,8},{1,17},{9,25},{17,1},{25,9},{2,18},{10... | collective-permute-start | bytes 7688 | tf_op jit(solution)/shard_map/ppermute | solution.py:19
  7.8 27.8 %collective-permute-start.3 = (bf16[32,512]{1,0:T(8,128)(2,1)S(1)}, bf16[32,512]{1,0:T(8,128)(2,1)S(1)}, u32[]{:S(2)}, u32[]{:S(2)}) collective-permute-start(bf16[32,512]{1,0:T(8,128)(2,1)S(1)} %slice.46), channel_id=1, source_target_pairs={{0,8},{8,0},{16,24},{24,16},{1,9},{9,1},{17,25},{25,17},{2,10},{10... | collective-permute-start | bytes 98312 | tf_op jit(solution)/shard_map/ppermute | solution.py:19
  8.2 37.2 %collective-permute-start.5 = (bf16[256,256]{1,0:T(8,128)(2,1)}, bf16[256,256]{1,0:T(8,128)(2,1)S(1)}, u32[]{:S(2)}, u32[]{:S(2)}) collective-permute-start(bf16[256,256]{1,0:T(8,128)(2,1)} %param.13), channel_id=1, source_target_pairs={{0,8},{8,0},{16,24},{24,16},{1,9},{9,1},{17,25},{25,17},{2,10},{10... | collective-permute-start | bytes 393224 | tf_op jit(solution)/shard_map/ppermute | solution.py:19
  10.5 20.3 %collective-permute-start.7 = (bf16[16,512]{1,0:T(8,128)(2,1)S(1)}, bf16[16,512]{1,0:T(8,128)(2,1)S(1)}, u32[]{:S(2)}, u32[]{:S(2)}) collective-permute-start(bf16[16,512]{1,0:T(8,128)(2,1)S(1)} %slice.51), channel_id=1, source_target_pairs={{0,8},{8,0},{16,24},{24,16},{1,9},{9,1},{17,25},{25,17},{2,10},{10... | collective-permute-start | bytes 49160 | tf_op jit(solution)/shard_map/ppermute | solution.py:19
  11.8 18.3 %copy-start = (bf16[640,1024]{1,0:T(8,128)(2,1)S(1)}, bf16[640,1024]{1,0:T(8,128)(2,1)}, u32[]{:S(2)}) copy-start(bf16[640,1024]{1,0:T(8,128)(2,1)} %front.4) | copy-start | bytes 3932164
  22.5 9.9 %collective-permute-start.12 = (bf16[128,256]{1,0:T(8,128)(2,1)}, bf16[128,256]{1,0:T(8,128)(2,1)S(1)}, u32[]{:S(2)}, u32[]{:S(2)}) collective-permute-start(bf16[128,256]{1,0:T(8,128)(2,1)} %param.14), channel_id=1, source_target_pairs={{0,8},{8,0},{16,24},{24,16},{1,9},{9,1},{17,25},{25,17},{2,10},{10... | collective-permute-start | bytes 196616 | tf_op jit(solution)/shard_map/ppermute | solution.py:19
  25.3 1.3 %copy-start.3 = (bf16[640,1024]{1,0:T(8,128)(2,1)S(1)}, bf16[640,1024]{1,0:T(8,128)(2,1)}, u32[]{:S(2)}) copy-start(bf16[640,1024]{1,0:T(8,128)(2,1)} %front.3) | copy-start | bytes 3932164
  26.6 0.9 %copy-start.4 = (bf16[512,256]{1,0:T(8,128)(2,1)S(1)}, bf16[512,256]{1,0:T(8,128)(2,1)}, u32[]{:S(2)}) copy-start(bf16[512,256]{1,0:T(8,128)(2,1)} %inverse.1) | copy-start | bytes 786436
  29.6 5.0 %collective-permute-start.4 = (bf16[64,512]{1,0:T(8,128)(2,1)S(1)}, bf16[64,512]{1,0:T(8,128)(2,1)S(1)}, u32[]{:S(2)}, u32[]{:S(2)}) collective-permute-start(bf16[64,512]{1,0:T(8,128)(2,1)S(1)} %get-tuple-element.19), channel_id=1, source_target_pairs={{0,8},{8,0},{16,24},{24,16},{1,9},{9,1},{17,25},{25,17},{2,10},{10... | collective-permute-start | bytes 196616 | tf_op jit(solution)/shard_map/ppermute | solution.py:19
  30.1 2.8 %copy-start.6 = (bf16[128,256]{1,0:T(8,128)(2,1)S(1)}, bf16[128,256]{1,0:T(8,128)(2,1)}, u32[]{:S(2)}) copy-start(bf16[128,256]{1,0:T(8,128)(2,1)} %param.14) | copy-start | bytes 196612
  30.8 14.8 %copy-start.2 = (f32[640,512]{1,0:T(8,128)}, f32[640,512]{1,0:T(8,128)S(1)}, u32[]{:S(2)}) copy-start(f32[640,512]{1,0:T(8,128)S(1)} %own0.1.merged) | copy-start | bytes 3932164
  30.8 14.7 %copy-start.5 = (bf16[256,256]{1,0:T(8,128)(2,1)S(1)}, bf16[256,256]{1,0:T(8,128)(2,1)}, u32[]{:S(2)}) copy-start(bf16[256,256]{1,0:T(8,128)(2,1)} %param.13) | copy-start | bytes 393220
  30.8 14.8 %collective-permute-start.2 = (bf16[320,512]{1,0:T(8,128)(2,1)S(1)}, bf16[320,512]{1,0:T(8,128)(2,1)S(1)}, u32[]{:S(2)}, u32[]{:S(2)}) collective-permute-start(bf16[320,512]{1,0:T(8,128)(2,1)S(1)} %get-tuple-element.17), channel_id=1, source_target_pairs={{0,8},{8,0},{16,24},{24,16},{1,9},{9,1},{17,25},{25,17},{2,10},{10... | collective-permute-start | bytes 983048 | tf_op jit(solution)/shard_map/ppermute | solution.py:19
  32.5 24.6 %collective-permute-start.8 = (bf16[32,512]{1,0:T(8,128)(2,1)S(1)}, bf16[32,512]{1,0:T(8,128)(2,1)S(1)}, u32[]{:S(2)}, u32[]{:S(2)}) collective-permute-start(bf16[32,512]{1,0:T(8,128)(2,1)S(1)} %maximum_select_fusion.9), channel_id=1, source_target_pairs={{0,16},{8,24},{16,0},{24,8},{1,17},{9,25},{17,1},{25,9},{2,18},{10... | collective-permute-start | bytes 98312 | tf_op jit(solution)/shard_map/ppermute | solution.py:19
  34.5 16.2 %collective-permute-start.13 = (bf16[256,256]{1,0:T(8,128)(2,1)S(1)}, bf16[256,256]{1,0:T(8,128)(2,1)S(1)}, u32[]{:S(2)}, u32[]{:S(2)}) collective-permute-start(bf16[256,256]{1,0:T(8,128)(2,1)S(1)} %maximum_select_fusion.4), channel_id=1, source_target_pairs={{0,16},{8,24},{16,0},{24,8},{1,17},{9,25},{17,1},{25,9},{2,18},{10... | collective-permute-start | bytes 393224 | tf_op jit(solution)/shard_map/ppermute | solution.py:19
  45.6 7.8 %copy-start.1 = (bf16[640,1024]{1,0:T(8,128)(2,1)S(1)}, bf16[640,1024]{1,0:T(8,128)(2,1)}, u32[]{:S(2)}) copy-start(bf16[640,1024]{1,0:T(8,128)(2,1)} %front.5) | copy-start | bytes 3932164
  48.8 6.4 %collective-permute-start.9 = (bf16[32,512]{1,0:T(8,128)(2,1)S(1)}, bf16[32,512]{1,0:T(8,128)(2,1)S(1)}, u32[]{:S(2)}, u32[]{:S(2)}) collective-permute-start(bf16[32,512]{1,0:T(8,128)(2,1)S(1)} %get-tuple-element.24), channel_id=1, source_target_pairs={{0,16},{8,24},{16,0},{24,8},{1,17},{9,25},{17,1},{25,9},{2,18},{10... | collective-permute-start | bytes 98312 | tf_op jit(solution)/shard_map/ppermute | solution.py:19
  50.9 4.3 %collective-permute-start.10 = (bf16[32,512]{1,0:T(8,128)(2,1)S(1)}, bf16[32,512]{1,0:T(8,128)(2,1)S(1)}, u32[]{:S(2)}, u32[]{:S(2)}) collective-permute-start(bf16[32,512]{1,0:T(8,128)(2,1)S(1)} %get-tuple-element.24), channel_id=1, source_target_pairs={{0,8},{8,0},{16,24},{24,16},{1,9},{9,1},{17,25},{25,17},{2,10},{10... | collective-permute-start | bytes 98312 | tf_op jit(solution)/shard_map/ppermute | solution.py:19
  51.0 6.1 %collective-permute-start.11 = (bf16[32,512]{1,0:T(8,128)(2,1)S(1)}, bf16[32,512]{1,0:T(8,128)(2,1)S(1)}, u32[]{:S(2)}, u32[]{:S(2)}) collective-permute-start(bf16[32,512]{1,0:T(8,128)(2,1)S(1)} %get-tuple-element.24), channel_id=1, source_target_pairs={{0,24},{8,16},{16,8},{24,0},{1,25},{9,17},{17,9},{25,1},{2,26},{10... | collective-permute-start | bytes 98312 | tf_op jit(solution)/shard_map/ppermute | solution.py:19
  54.1 16.7 %collective-permute-start.6 = (bf16[320,512]{1,0:T(8,128)(2,1)S(1)}, bf16[320,512]{1,0:T(8,128)(2,1)S(1)}, u32[]{:S(2)}, u32[]{:S(2)}) collective-permute-start(bf16[320,512]{1,0:T(8,128)(2,1)S(1)} %get-tuple-element.22), channel_id=1, source_target_pairs={{0,16},{8,24},{16,0},{24,8},{1,17},{9,25},{17,1},{25,9},{2,18},{10... | collective-permute-start | bytes 983048 | tf_op jit(solution)/shard_map/ppermute | solution.py:19

commit v2 on v1

v2 whole, which is shorter than its diff:
```python
import jax
import jax.numpy as jnp
from jax import lax
from jax.experimental import pallas as pl
from jax.experimental.pallas import tpu as pltpu
from jax.sharding import PartitionSpec as P


BF = jnp.bfloat16
F32 = jnp.float32
I32 = jnp.int32
NT = (((1,), (1,)), ((), ()))
NN = (((1,), (0,)), ((), ()))
VM = pl.BlockSpec(memory_space=pltpu.VMEM)
SM = pl.BlockSpec(memory_space=pltpu.SMEM)
AN = pl.BlockSpec(memory_space=pltpu.HBM)


def dot(a, b, dims):
    return lax.dot_general(a, b, dims, preferred_element_type=F32)


def swap(value, axis, mask):
    return lax.ppermute(value, axis, [(i, i ^ mask) for i in range(lax.axis_size(axis))])


def later(value, *others):
    return lax.optimization_barrier((value,) + others)[0]


def call(body, in_specs, outs, scratch=(), out_specs=None):
    made = pl.pallas_call(
        body, in_specs=in_specs, out_specs=out_specs or [VM] * len(outs),
        out_shape=[jax.ShapeDtypeStruct(s, d) for s, d in outs], scratch_shapes=scratch,
        compiler_params=pltpu.CompilerParams(vmem_limit_bytes=16 * 1024 * 1024),
    )

    def run(*args):
        return made(*[
            pltpu.with_memory_space_constraint(a, pltpu.HBM) if spec is AN else a
            for a, spec in zip(args, in_specs)
        ])

    return run


def copies(sems, pairs):
    made = [pltpu.make_async_copy(a, b, sems.at[i]) for i, (a, b) in enumerate(pairs)]
    for c in made:
        c.start()
    return made


def one_hot(row, count):
    ids = lax.broadcasted_iota(I32, (count, row.shape[1]), 0)
    return jnp.where(ids == row, 1.0, 0.0).astype(BF)


def slots_of(code, rows):
    outward = code >= rows
    flags = jnp.broadcast_to(jnp.where(outward, 1.0, 0.0).astype(BF), (8, rows))
    a = lax.broadcasted_iota(I32, (rows, rows), 0)
    b = lax.broadcasted_iota(I32, (rows, rows), 1)
    upper = jnp.where(a < b, 1.0, 0.0).astype(BF)
    rank = dot(flags, upper, NN)[:1].astype(I32)
    return jnp.where(outward, rank, -1)


def landing_of(code, rows):
    pick = one_hot(slots_of(code, rows), rows // 2)
    target = one_hot(code - rows, rows)
    return dot(target, pick, NT).astype(BF)


def row_picks(code, live, n):
    rows = code.shape[1]
    alive = lax.broadcasted_iota(I32, (1, rows), 1) < live
    shown = jnp.where(alive, code, -1)
    slot = jnp.where(alive, slots_of(code, rows), -1)
    ids = lax.broadcasted_iota(I32, (2 * n, rows), 0)
    pivot = jnp.where(jnp.where(ids < n, ids, ids + (rows - n)) == shown, 1.0, 0.0).astype(BF)
    bulk = one_hot(slot, rows // 2)
    return jnp.concatenate([pivot, bulk], 0)


def own_pick(code, live):
    rows = code.shape[1]
    return one_hot(jnp.where(lax.broadcasted_iota(I32, (1, rows), 1) < live, code, -1), rows)


def scaled(panel, inverse):
    block = inverse.shape[1]
    parts = [
        dot(panel[:, b * block:(b + 1) * block], inverse[b * block:(b + 1) * block], NT)
        for b in range(inverse.shape[0] // block)
    ]
    return jnp.concatenate(parts, 1)


def factor_of(panel, inverse, live):
    mask = lax.broadcasted_iota(I32, (panel.shape[0], 1), 0) < live
    return jnp.where(mask, scaled(panel, inverse), 0.0).astype(BF)


def reordered(value, outer, middle):
    rows = value.shape[0]
    part = rows // (outer * middle)
    if middle == 1:
        return value
    if part % 16 == 0:
        return jnp.concatenate(
            [value[(o * middle + m) * part:(o * middle + m + 1) * part]
             for m in range(middle) for o in range(outer)], 0)
    target = lax.broadcasted_iota(I32, (rows, rows), 0)
    source = lax.broadcasted_iota(I32, (rows, rows), 1)
    k = target % part
    o = target // part % outer
    m = target // (part * outer)
    return dot(jnp.where((o * middle + m) * part + k == source, 1.0, 0.0).astype(BF), value, NN).astype(BF)


def spread(block):
    if lax.axis_size("inner") != 8 or block.shape[0] % 64:
        return {}
    return {m: swap(block, "inner", m) for m in GATHER_ORDER}


def collect(block, got, *before):
    if not got:
        return [lax.all_gather(block, "inner", axis=0, tiled=True)]
    got = dict(got)
    got[0] = block
    got[1] = swap(block, "inner", 1)
    for m in GATHER_ORDER:
        got[m] = later(got[m], *before)
        got[m + 1] = swap(got[m], "inner", 1)
    return [got[m] for m in range(8)]


GATHER_ORDER = (6, 4, 2)


def pivots_from(blocks, inverse, pivots, middle, inner):
    if len(blocks) == 1:
        pivots[...] = reordered(scaled(blocks[0][...], inverse[...]).astype(BF), inner, middle)
        return
    size = blocks[0].shape[0]
    part = size // middle
    made = scaled(jnp.concatenate([block[...] for block in blocks], 0), inverse[...]).astype(BF)
    for m in range(len(blocks)):
        at = (lax.axis_index("inner") ^ m) * part
        for q in range(middle):
            pivots[pl.ds(pl.multiple_of(q * part * inner + at, part), part), :] = (
                made[m * size + q * part:m * size + (q + 1) * part])


def code_row(ref):
    return jnp.concatenate([ref[i:i + 1] for i in range(ref.shape[0])], 1)


def up16(count):
    return (count + 15) // 16 * 16


def per_device(front_leaf, front_mid, front_top, dinv_leaf, dinv_mid, dinv_top, live_rows, map_leaf, map_mid):
    rows = front_leaf.shape[0]
    panel, block = dinv_leaf.shape
    cols = front_leaf.shape[1] - panel
    inner = lax.axis_size("inner")
    half = rows // 2
    n = [cols // (inner << l) for l in range(3)]

    lanes = 128 if rows % 128 == 0 else rows
    code0 = map_leaf.reshape(rows // lanes, lanes)
    code1 = map_mid.reshape(rows // lanes, lanes)
    live = live_rows.reshape(1, 3)

    mr, tr = dinv_mid.shape[0] // 2, dinv_top.shape[0] // 2
    at_top, at_code, at_mid = 0, tr + up16(n[2]), tr + up16(n[2]) + 16
    small = (tr + up16(n[2]) + 16, panel)
    large = (small[0] + mr + up16(n[1]), panel)

    def pack(code0_ref, code1_ref, mid, top, fmid, ftop, leaf, near, wide, c0v, c1v, head, sems):
        made = []
        for out in (near, wide):
            made += [
                (top.at[:tr], out.at[at_top:at_top + tr, :block]),
                (top.at[tr:], out.at[at_top:at_top + tr, block:]),
                (ftop.at[:n[2], :panel], out.at[tr:tr + n[2]]),
            ]
        made += [
            (mid.at[:mr], near.at[at_mid:at_mid + mr, :block]),
            (mid.at[mr:], near.at[at_mid:at_mid + mr, block:]),
            (fmid.at[:n[1], :panel], near.at[at_mid + mr:at_mid + mr + n[1]]),
        ]
        made = copies(sems, [(code0_ref, c0v), (code1_ref, c1v)] + made + [(leaf.at[:n[0], :panel], head)])
        made[0].wait()
        made[1].wait()
        code = jnp.concatenate([code_row(c0v), code_row(c1v)], 0)
        parts = jnp.concatenate([code >> 8, code & 255, jnp.zeros((4, rows), I32)], 0)
        parts = parts.astype(F32).astype(BF)
        padded = jnp.concatenate([parts, jnp.zeros((8, 2 * panel - rows), BF)], 1)
        packed = jnp.concatenate([padded[:, :panel], padded[:, panel:]], 0)
        near[at_code:at_code + 16] = packed
        wide[at_code:at_code + 16] = packed
        for c in made[2:]:
            c.wait()

    near, wide, code0, code1, block0 = call(
        pack, [AN] * 7,
        [(large, BF), (small, BF), (code0.shape, I32), (code1.shape, I32), ((n[0], panel), BF)],
        scratch=[pltpu.SemaphoreType.DMA((12,))],
    )(code0, code1, dinv_mid, dinv_top, front_mid, front_top, front_leaf)
    got0 = spread(block0)
    near_1 = swap(near, "sub", 1)
    wide_2 = swap(wide, "sub", 2)
    wide_3 = swap(wide, "sub", 3)

    def sent(level):
        return [((2 * n[level] + half, cols), BF)] * 2

    def before0(live_ref, code, front_ref, inverse, mid, fs, cs, factor, iv, front, mid_v, sems):
        made = copies(sems, [(inverse, iv), (front_ref, front), (mid, mid_v)])
        pick = row_picks(code_row(code), live_ref[0, 0], n[1])
        made[0].wait()
        made[1].wait()
        factor[...] = factor_of(front[:, :panel], iv[...], live_ref[0, 0])
        cs[...] = dot(pick, front[:, panel:], NN).astype(BF)
        fs[...] = dot(pick, factor[...], NN).astype(BF)
        made[2].wait()

    fs0, cs0, factor0, inv_leaf, leaf, mid = call(
        before0, [SM, VM, AN, AN, AN],
        sent(1) + [((rows, panel), BF), (dinv_leaf.shape, BF), (front_leaf.shape, BF), (front_mid.shape, BF)],
        scratch=[pltpu.SemaphoreType.DMA((3,))],
    )(live, code0, front_leaf, dinv_leaf, front_mid)
    blocks0 = collect(block0, got0, fs0)

    def chain(middle):
        def body(fs, cs, inverse, *refs):
            blocks, (pivots, out, bulk) = refs[:-3], refs[-3:]
            pivots_from(blocks, inverse, pivots, middle, inner)
            update = (cs[...].astype(F32) - dot(fs[...], pivots[...], NT)).astype(BF)
            out[...] = update[:out.shape[0]]
            bulk[...] = update[out.shape[0]:]

        return body

    def after(level, fs, cs, inverse, blocks):
        return call(
            chain(1 << level), [VM] * (3 + len(blocks)),
            [((cols, panel), BF), ((2 * n[level + 1], cols), BF), ((half, cols), BF)],
        )(fs, cs, inverse, *blocks)

    def own(level, code, factor, front, pivots, parent):
        def body(live_ref, code_ref, factor_ref, front_ref, pivots_ref, parent_ref, out):
            update = (front_ref[:, panel:].astype(F32) - dot(factor_ref[...], pivots_ref[...], NT)).astype(BF)
            pick = own_pick(code_row(code_ref), live_ref[0, level])
            out[...] = parent_ref[:, :cols].astype(F32) + dot(pick, update, NN)

        return call(body, [SM] + [VM] * 5, [((rows, cols), F32)])(
            live, code, factor, front, pivots, parent)[0]

    pivots0, pivot0, bulk0 = after(0, fs0, cs0, inv_leaf, blocks0)
    pivot0_other = swap(pivot0, "sub", 1)
    bulk0_other = swap(bulk0, "sub", 1)

    def landing_from(src, row, out):
        packed = src[at_code:at_code + 16].astype(F32).astype(I32)
        high = jnp.concatenate([packed[row:row + 1], packed[row + 8:row + 9]], 1)[:, :rows]
        low = jnp.concatenate([packed[row + 2:row + 3], packed[row + 10:row + 11]], 1)[:, :rows]
        out[...] = landing_of(high * 256 + low, rows)

    def unpack1(mine, near_ref, inv_mid, heads1, land0):
        sub = lax.axis_index("sub")
        for q, src in enumerate((mine, near_ref)):
            at = ((sub & 1) ^ q) * 2 * mr
            inv_mid[pl.ds(pl.multiple_of(at, mr), mr), :] = src[at_mid:at_mid + mr, :block]
            inv_mid[pl.ds(pl.multiple_of(at + mr, mr), mr), :] = src[at_mid:at_mid + mr, block:]
            heads1[q] = src[at_mid + mr:at_mid + mr + up16(n[1])]
        landing_from(near_ref, 0, land0)

    def unpack2(mine, near_ref, wide2, wide3, inv_top, heads2, land1):
        sub = lax.axis_index("sub")
        for q, src in enumerate((mine, near_ref, wide2, wide3)):
            at = ((sub & 3) ^ q) * 2 * tr
            inv_top[pl.ds(pl.multiple_of(at, tr), tr), :] = src[at_top:at_top + tr, :block]
            inv_top[pl.ds(pl.multiple_of(at + tr, tr), tr), :] = src[at_top:at_top + tr, block:]
            heads2[q] = src[tr:tr + up16(n[2])]
        landing_from(wide2, 1, land1)

    inv_mid, heads1, land0 = call(
        unpack1, [VM] * 2, [(dinv_leaf.shape, BF), ((2, up16(n[1]), panel), BF), ((rows, half), BF)],
    )(near, later(near_1, pivot0))

    def early1(live_ref, code, front, top_ref, pick_out, cs, top_v, sems):
        made, = copies(sems, [(top_ref, top_v)])
        pick = row_picks(code_row(code), live_ref[0, 1], n[2])
        pick_out[...] = pick
        cs[...] = dot(pick, front[:, panel:], NN).astype(BF)
        made.wait()

    pick1, cs1, top = call(
        early1, [SM, VM, VM, AN], [((2 * n[2] + half, rows), BF)] + sent(2)[:1] + [(front_top.shape, BF)],
        scratch=[pltpu.SemaphoreType.DMA((1,))],
    )(live, later(code1, pivot0), mid, front_top)

    def raised(count, flip):
        def body(heads, *refs):
            others, out = refs[:-1], refs[-1]
            sub = lax.axis_index("sub")
            made = []
            for q in range(len(others)):
                total = others[q][:count].astype(F32) + others[q ^ flip][count:].astype(F32)
                made.append(heads[q][:count].astype(F32) + total)
            bit = 1
            while len(made) > 1:
                low = (sub & bit) == 0
                made = [
                    jnp.concatenate([jnp.where(low, a, b), jnp.where(low, b, a)], 0)
                    for a, b in zip(made[::2], made[1::2])
                ]
                bit *= 2
            out[...] = made[0].astype(BF)

        return body

    raw1, = call(raised(n[1], 1), [VM] * 3, [((2 * n[1], panel), BF)])(later(heads1, pick1), pivot0, pivot0_other)
    spread1 = spread(raw1)
    merged0 = own(0, code0, factor0, leaf, pivots0, mid)

    def before1(live_ref, pick, merged, got, land, inverse, fs, factor):
        assembled = (merged[...] + dot(land[...], got[...], NN)).astype(BF)
        factor[...] = factor_of(assembled, inverse[...], live_ref[0, 1])
        fs[...] = dot(pick[...], factor[...], NN).astype(BF)

    fs1, factor1 = call(
        before1, [SM] + [VM] * 5, sent(2)[:1] + [((rows, panel), BF)],
    )(live, pick1, merged0, bulk0_other, land0, inv_mid)
    blocks1 = collect(raw1, spread1, fs1)
    pivots1, pivot1, bulk1 = after(1, fs1, cs1, inv_mid, blocks1)
    others = [pivot1] + [swap(pivot1, "sub", m) for m in (1, 2, 3)]
    bulk1_other = swap(bulk1, "sub", 2)
    inv_top, heads2, land1 = call(
        unpack2, [VM] * 4,
        [(dinv_leaf.shape, BF), ((4, up16(n[2]), panel), BF), ((rows, half), BF)],
    )(near, near_1, wide_2, later(wide_3, pivot1))
    raw2, = call(raised(n[2], 2), [VM] * 5, [((4 * n[2], panel), BF)])(heads2, *others)
    spread2 = spread(raw2)
    merged1 = own(1, code1, factor1, mid, pivots1, top)
    blocks2 = collect(raw2, spread2, merged1)

    def last_pivots(inverse, *refs):
        pivots_from(refs[:-1], inverse, refs[-1], 4, inner)

    pivots2, = call(last_pivots, [VM] * (1 + len(blocks2)), [((cols, panel), BF)])(inv_top, *blocks2)

    steps = 2 if rows % 32 == 0 else 1
    part = rows // steps

    def level2(live_ref, front, merged, got, land, inverse, pivots, out, ov, sems):
        assembled = (merged[...] + dot(land[...], got[...], NN)).astype(BF)
        factor = factor_of(assembled, inverse[...], live_ref[0, 2])
        mask = lax.broadcasted_iota(I32, (rows, 1), 0) < live_ref[0, 2]
        writes = []
        for i in range(steps):
            at = slice(i * part, (i + 1) * part)
            product = dot(factor[at], pivots[...], NT)
            ov[at] = jnp.where(mask[at], front[at, panel:].astype(F32) - product, 0.0).astype(BF)
            writes += copies(sems.at[i:i + 1], [(ov.at[at], out.at[at])])
        for write in writes:
            write.wait()

    out, = call(
        level2, [SM] + [VM] * 6, [((rows, cols), BF)],
        scratch=[pltpu.VMEM((rows, cols), BF), pltpu.SemaphoreType.DMA((steps,))],
        out_specs=[AN],
    )(live, top, merged1, bulk1_other, land1, inv_top, pivots2)
    return out


def solution(mesh):
    row = P(("sub", "inner"), None)
    placed = (
        row, row, row, P("sub", None), P("sub", None), P("sub", None),
        P(None, ("sub", "inner")), P(("sub", "inner")), P(("sub", "inner")),
    )

    return jax.shard_map(per_device, mesh=mesh, in_specs=placed, out_specs=row, check_vma=False)
```

time: 74 us -> 77.4 us (1.046)
  blocking collectives: 28.7 us -> 0 us
  starting transfers between devices: 18.9 us -> 37.9 us
  waiting for transfers between devices: 8.29 us -> 22.4 us
  local copies, waits for them, and re-layouts: 6.75 us -> 0.01 us
  Pallas kernels: 10.4 us -> 16.6 us
    all_gather x3 -> x0, blocking collectives: 28.7 us -> none  [the longest x1 9.97 us: per_device(): lax.all_gather(front_leaf[:n[0], :panel], 'inner', axis=0, tiled=True)]
    ppermute x14 -> x30, starting transfers between devices: 18.9 us -> 37.9 us  [swap(): lax.ppermute(value, axis, [(i, i ^ mask) for i in range(lax.axis_size(axi...]
    ppermute x14 -> x30, waiting for transfers between devices: 8.29 us -> 22.4 us  [swap(): lax.ppermute(value, axis, [(i, i ^ mask) for i in range(lax.axis_size(axi...]
    pallas_call x6 -> x14, Pallas kernels: 10.4 us -> 16.6 us  [run(): made(*[pltpu.with_memory_space_constraint(a, pltpu.HBM) if spec is AN els...]
    unnamed x15 -> x2, local copies, waits for them, and re-layouts: 3.05 us -> 0.01 us
    slice x3 -> x0, local copies, waits for them, and re-layouts: 2.32 us -> none  [the longest x1 0.84 us: per_device(): front_leaf[:n[0], :panel]]
    reshape x2 -> x0, local copies, waits for them, and re-layouts: 1.38 us -> none  [the longest x1 0.69 us: per_device(): code0 = map_leaf.reshape(1, rows)]
  transfers between devices with their start and end apart: 14 -> 30, of which waited for: 3 -> 15; matrix products, arithmetic and copies ran while one was open for 6% -> 0% of each run, Pallas kernels for 10% -> 16%
where the time goes in v2:
time: 77.4 us; the launch traced here: 77.1 us
  starting transfers between devices  37.9 us (49%)
  waiting for transfers between devices  22.4 us (29%)
  Pallas kernels  16.6 us (21%)
    ppermute x30, starting transfers between devices, swap(): lax.ppermute(value, axis, [(i, i ^ mask) for i in range(lax.axis_size(axi...  37.9 us
    ppermute x30, waiting for transfers between devices, swap(): lax.ppermute(value, axis, [(i, i ^ mask) for i in range(lax.axis_size(axi...  22.4 us
    pallas_call x14, Pallas kernels, run(): made(*[pltpu.with_memory_space_constraint(a, pltpu.HBM) if spec is AN els...  16.6 us
  transfers between devices with their start and end apart: 30, of which 15 were waited for; matrix products, arithmetic and copies ran while one was open for 0% of the time, Pallas kernels for 16%

profile of v2, /device:TPU:0, one launch (start us, length us, event | category | flops | bytes accessed | tf_op | source)
XLA Modules:
  0.0 77.1 jit_solution(5970237202644305312)
XLA Ops:
  0.0 1.2 %shard_map.91 = (bf16[256,512]{1,0:T(8,128)(2,1)S(1)}, bf16[96,512]{1,0:T(8,128)(2,1)S(1)}, s32[5,128]{1,0:T(8,128)S(1)}, s32[5,128]{1,0:T(8,128)S(1)}, bf16[64,512]{1,0:T(8,128)(2,1)S(1)}) custom-call(s32[5,128]{1,0:T(8,128)} %bitcast.9, s32[5,128]{1,0:T(8,128)} %bitcast.10, bf16[256,256]{1,0:T(8,128)(2,1)} %mid.2, bf16[128,256]{1,0:T(8,128)(2,1)} %top.1, ...), custom_call_target="tpu_custom_call" | custom-call | tf_op jit(solution)/shard_map/pallas_call | solution.py:39
  1.2 4.0 %collective-permute-start.5 = (bf16[64,512]{1,0:T(8,128)(2,1)S(1)}, bf16[64,512]{1,0:T(8,128)(2,1)S(1)}, u32[]{:S(2)}, u32[]{:S(2)}) collective-permute-start(bf16[64,512]{1,0:T(8,128)(2,1)S(1)} %get-tuple-element.51.refs_0_), channel_id=1, source_target_pairs={{0,6},{1,7},{2,4},{3,5},{4,2},{5,3},{6,0},{7,1},{8,14},{9,15},{10,... | collective-permute-start | bytes 196616 | tf_op jit(solution)/shard_map/ppermute | solution.py:24
  5.8 3.0 %shard_map.92 = (bf16[384,512]{1,0:T(8,128)(2,1)S(1)}, bf16[384,512]{1,0:T(8,128)(2,1)S(1)}, bf16[640,512]{1,0:T(8,128)(2,1)S(1)}, bf16[512,256]{1,0:T(8,128)(2,...) custom-call(s32[1,3]{1,0:T(1,128)S(1)} %bitcast.3, s32[5,128]{1,0:T(8,128)S(1)} %get-tuple-element.47.code.code_ref, ...), custom_call_target="tpu_custom_call" | custom-call | tf_op jit(solution)/shard_map/pallas_call | solution.py:39
  10.4 1.6 %collective-permute-start.8 = (bf16[256,512]{1,0:T(8,128)(2,1)S(1)}, bf16[256,512]{1,0:T(8,128)(2,1)S(1)}, u32[]{:S(2)}, u32[]{:S(2)}) collective-permute-start(bf16[256,512]{1,0:T(8,128)(2,1)S(1)} %get-tuple-element.64.mine), channel_id=1, source_target_pairs={{0,8},{8,0},{16,24},{24,16},{1,9},{9,1},{17,25},{25,17},{2,10},{10... | collective-permute-start | bytes 786440 | tf_op jit(solution)/shard_map/ppermute | solution.py:24
  12.8 1.3 %collective-permute-start.7 = (bf16[320,512]{1,0:T(8,128)(2,1)S(1)}, bf16[320,512]{1,0:T(8,128)(2,1)S(1)}, u32[]{:S(2)}, u32[]{:S(2)}) collective-permute-start(bf16[320,512]{1,0:T(8,128)(2,1)S(1)} %get-tuple-element.63), channel_id=1, source_target_pairs={{0,8},{8,0},{16,24},{24,16},{1,9},{9,1},{17,25},{25,17},{2,10},{10... | collective-permute-start | bytes 983048 | tf_op jit(solution)/shard_map/ppermute | solution.py:24
  14.9 1.9 %shard_map.94 = (bf16[352,640]{1,0:T(8,128)(2,1)S(1)}, bf16[352,512]{1,0:T(8,128)(2,1)S(1)}, bf16[640,1024]{1,0:T(8,128)(2,1)S(1)}) custom-call(s32[1,3]{1,0:T(1,128)S(1)} %bitcast.4, s32[5,128]{1,0:T(8,128)S(1)} %get-tuple-element.56.code.code_ref, bf16[640,1024]{1,0:T(8,128)(2,1)S(1)} %get-tuple-element.57.front.parent_ref.front_ref, bf16[640,1024]{1,0:T(8,128)(2,1)} %top_ref.1), custom_call_target="tpu_custom_call" | custom-call | tf_op jit(solution)/shard_map/pallas_call | solution.py:39
  16.8 2.9 %collective-permute-done.8.near_ref = bf16[256,512]{1,0:T(8,128)(2,1)S(1)} collective-permute-done((bf16[256,512]{1,0:T(8,128)(2,1)S(1)}, bf16[256,512]{1,0:T(8,128)(2,1)S(1)}, u32[]{:S(2)}, u32[]{:S(2)}) %collective-permute-start.8) | collective-permute-done | bytes 262176 | tf_op jit(solution)/shard_map/ppermute | solution.py:24
  20.5 7.1 %collective-permute-done.9.refs_1_ = bf16[64,512]{1,0:T(8,128)(2,1)S(1)} collective-permute-done((bf16[64,512]{1,0:T(8,128)(2,1)S(1)}, bf16[64,512]{1,0:T(8,128)(2,1)S(1)}, u32[]{:S(2)}, u32[]{:S(2)}) %collective-permute-start.9) | collective-permute-done | bytes 65568 | tf_op jit(solution)/shard_map/ppermute | solution.py:24
  27.6 1.9 %collective-permute-start.15 = (bf16[64,512]{1,0:T(8,128)(2,1)S(1)}, bf16[64,512]{1,0:T(8,128)(2,1)S(1)}, u32[]{:S(2)}, u32[]{:S(2)}) collective-permute-start(bf16[64,512]{1,0:T(8,128)(2,1)S(1)} %shard_map.98.refs_0_), channel_id=1, source_target_pairs={{0,6},{1,7},{2,4},{3,5},{4,2},{5,3},{6,0},{7,1},{8,14},{9,15},{10,... | collective-permute-start | bytes 196616 | tf_op jit(solution)/shard_map/ppermute | solution.py:24
  30.1 1.1 %collective-permute-start.11 = (bf16[64,512]{1,0:T(8,128)(2,1)S(1)}, bf16[64,512]{1,0:T(8,128)(2,1)S(1)}, u32[]{:S(2)}, u32[]{:S(2)}) collective-permute-start(bf16[64,512]{1,0:T(8,128)(2,1)S(1)} %shard_map.98.refs_0_), channel_id=1, source_target_pairs={{0,2},{1,3},{2,0},{3,1},{4,6},{5,7},{6,4},{7,5},{8,10},{9,11},{10,... | collective-permute-start | bytes 196616 | tf_op jit(solution)/shard_map/ppermute | solution.py:24
  31.2 1.6 %shard_map.95.merged = f32[640,512]{1,0:T(8,128)S(1)} custom-call(s32[1,3]{1,0:T(1,128)S(1)} %bitcast.5, s32[5,128]{1,0:T(8,128)S(1)} %get-tuple-element.47.code.code_ref, bf16[640,512]{1,0:T(8,128)(2,1)S(1)} %get-tuple-element.60.factor_ref, bf16[640,1024]{1,0:T(8,128)(2,1)S(1)} %get-tuple-element.61.front_ref, ...), custom_call_target="tpu_custom_call" | custom-call | tf_op jit(solution)/shard_map/pallas_call | solution.py:39
  32.9 1.5 %shard_map.97 = (bf16[352,512]{1,0:T(8,128)(2,1)S(1)}, bf16[640,512]{1,0:T(8,128)(2,1)S(1)}) custom-call(s32[1,3]{1,0:T(1,128)S(1)} %bitcast.6, bf16[352,640]{1,0:T(8,128)(2,1)S(1)} %get-tuple-element.59.pick, f32[640,512]{1,0:T(8,128)S(1)} %shard_map.95.merged, bf16[320,512]{1,0:T(8,128)(2,1)S(1)} %collective-permute-done.7.got, ...), custom_call_target="tpu_custom_call" | custom-call | tf_op jit(solution)/shard_map/pallas_call | solution.py:39
  37.1 2.6 %collective-permute-start.17 = (bf16[320,512]{1,0:T(8,128)(2,1)S(1)}, bf16[320,512]{1,0:T(8,128)(2,1)S(1)}, u32[]{:S(2)}, u32[]{:S(2)}) collective-permute-start(bf16[320,512]{1,0:T(8,128)(2,1)S(1)} %get-tuple-element.77), channel_id=1, source_target_pairs={{0,16},{8,24},{16,0},{24,8},{1,17},{9,25},{17,1},{25,9},{2,18},{10... | collective-permute-start | bytes 983048 | tf_op jit(solution)/shard_map/ppermute | solution.py:24
  39.8 1.4 %collective-permute-start.19 = (bf16[96,512]{1,0:T(8,128)(2,1)S(1)}, bf16[96,512]{1,0:T(8,128)(2,1)S(1)}, u32[]{:S(2)}, u32[]{:S(2)}) collective-permute-start(bf16[96,512]{1,0:T(8,128)(2,1)S(1)} %get-tuple-element.78), channel_id=1, source_target_pairs={{0,24},{8,16},{16,8},{24,0},{1,25},{9,17},{17,9},{25,1},{2,26},{10... | collective-permute-start | bytes 294920 | tf_op jit(solution)/shard_map/ppermute | solution.py:24
  41.1 1.7 %collective-permute-start.18 = (bf16[96,512]{1,0:T(8,128)(2,1)S(1)}, bf16[96,512]{1,0:T(8,128)(2,1)S(1)}, u32[]{:S(2)}, u32[]{:S(2)}) collective-permute-start(bf16[96,512]{1,0:T(8,128)(2,1)S(1)} %get-tuple-element.78), channel_id=1, source_target_pairs={{0,16},{8,24},{16,0},{24,8},{1,17},{9,25},{17,1},{25,9},{2,18},{10... | collective-permute-start | bytes 294920 | tf_op jit(solution)/shard_map/ppermute | solution.py:24
  42.8 0.9 %collective-permute-start.22 = (bf16[32,512]{1,0:T(8,128)(2,1)S(1)}, bf16[32,512]{1,0:T(8,128)(2,1)S(1)}, u32[]{:S(2)}, u32[]{:S(2)}) collective-permute-start(bf16[32,512]{1,0:T(8,128)(2,1)S(1)} %get-tuple-element.79.refs_0_), channel_id=1, source_target_pairs={{0,24},{8,16},{16,8},{24,0},{1,25},{9,17},{17,9},{25,1},{2,26},{10... | collective-permute-start | bytes 98312 | tf_op jit(solution)/shard_map/ppermute | solution.py:24
  43.7 1.9 %collective-permute-start.21 = (bf16[32,512]{1,0:T(8,128)(2,1)S(1)}, bf16[32,512]{1,0:T(8,128)(2,1)S(1)}, u32[]{:S(2)}, u32[]{:S(2)}) collective-permute-start(bf16[32,512]{1,0:T(8,128)(2,1)S(1)} %get-tuple-element.79.refs_0_), channel_id=1, source_target_pairs={{0,16},{8,24},{16,0},{24,8},{1,17},{9,25},{17,1},{25,9},{2,18},{10... | collective-permute-start | bytes 98312 | tf_op jit(solution)/shard_map/ppermute | solution.py:24
  45.6 6.3 %collective-permute-done.19.wide3 = bf16[96,512]{1,0:T(8,128)(2,1)S(1)} collective-permute-done((bf16[96,512]{1,0:T(8,128)(2,1)S(1)}, bf16[96,512]{1,0:T(8,128)(2,1)S(1)}, u32[]{:S(2)}, u32[]{:S(2)}) %collective-permute-start.19) | collective-permute-done | bytes 98336 | tf_op jit(solution)/shard_map/ppermute | solution.py:24
  51.9 12.1 %collective-permute-start.20 = (bf16[32,512]{1,0:T(8,128)(2,1)S(1)}, bf16[32,512]{1,0:T(8,128)(2,1)S(1)}, u32[]{:S(2)}, u32[]{:S(2)}) collective-permute-start(bf16[32,512]{1,0:T(8,128)(2,1)S(1)} %get-tuple-element.79.refs_0_), channel_id=1, source_target_pairs={{0,8},{8,0},{16,24},{24,16},{1,9},{9,1},{17,25},{25,17},{2,10},{10... | collective-permute-start | bytes 98312 | tf_op jit(solution)/shard_map/ppermute | solution.py:24
  64.0 1.6 %collective-permute-done.18.wide2 = bf16[96,512]{1,0:T(8,128)(2,1)S(1)} collective-permute-done((bf16[96,512]{1,0:T(8,128)(2,1)S(1)}, bf16[96,512]{1,0:T(8,128)(2,1)S(1)}, u32[]{:S(2)}, u32[]{:S(2)}) %collective-permute-start.18) | collective-permute-done | bytes 98336 | tf_op jit(solution)/shard_map/ppermute | solution.py:24
  66.5 1.9 %collective-permute-start.28 = (bf16[64,512]{1,0:T(8,128)(2,1)S(1)}, bf16[64,512]{1,0:T(8,128)(2,1)S(1)}, u32[]{:S(2)}, u32[]{:S(2)}) collective-permute-start(bf16[64,512]{1,0:T(8,128)(2,1)S(1)} %shard_map.102.refs_0_), channel_id=1, source_target_pairs={{0,6},{1,7},{2,4},{3,5},{4,2},{5,3},{6,0},{7,1},{8,14},{9,15},{10,... | collective-permute-start | bytes 196616 | tf_op jit(solution)/shard_map/ppermute | solution.py:24
  69.0 1.1 %collective-permute-start.24 = (bf16[64,512]{1,0:T(8,128)(2,1)S(1)}, bf16[64,512]{1,0:T(8,128)(2,1)S(1)}, u32[]{:S(2)}, u32[]{:S(2)}) collective-permute-start(bf16[64,512]{1,0:T(8,128)(2,1)S(1)} %shard_map.102.refs_0_), channel_id=1, source_target_pairs={{0,2},{1,3},{2,0},{3,1},{4,6},{5,7},{6,4},{7,5},{8,10},{9,11},{10,... | collective-permute-start | bytes 196616 | tf_op jit(solution)/shard_map/ppermute | solution.py:24
  70.1 1.6 %shard_map.100.merged = f32[640,512]{1,0:T(8,128)S(1)} custom-call(s32[1,3]{1,0:T(1,128)S(1)} %bitcast.7, s32[5,128]{1,0:T(8,128)S(1)} %get-tuple-element.56.code.code_ref, bf16[640,512]{1,0:T(8,128)(2,1)S(1)} %get-tuple-element.68.factor_ref, bf16[640,1024]{1,0:T(8,128)(2,1)S(1)} %get-tuple-element.57.front.parent_ref.front_ref, ...), custom_call_target="tpu_custom_call" | custom-call | tf_op jit(solution)/shard_map/pallas_call | solution.py:39
  74.8 2.3 %shard_map.104 = bf16[640,512]{1,0:T(8,128)(2,1)} custom-call(s32[1,3]{1,0:T(1,128)S(1)} %bitcast.8, bf16[640,1024]{1,0:T(8,128)(2,1)S(1)} %get-tuple-element.58.parent_ref.front, f32[640,512]{1,0:T(8,128)S(1)} %shard_map.100.merged, bf16[320,512]{1,0:T(8,128)(2,1)S(1)} %collective-permute-done.17.got, bf16[640,320]{1,0:T(8,128)(2,1)S(1)} %get-tuple-element.81.land, ...), custom_call_target="tpu_custom_call" | custom-call | tf_op jit(solution)/shard_map/pallas_call | solution.py:39
  (52 shorter events, 12.5 us)
Async XLA Ops:
  1.2 7.6 %collective-permute-start.5 = (bf16[64,512]{1,0:T(8,128)(2,1)S(1)}, bf16[64,512]{1,0:T(8,128)(2,1)S(1)}, u32[]{:S(2)}, u32[]{:S(2)}) collective-permute-start(bf16[64,512]{1,0:T(8,128)(2,1)S(1)} %get-tuple-element.51.refs_0_), channel_id=1, source_target_pairs={{0,6},{1,7},{2,4},{3,5},{4,2},{5,3},{6,0},{7,1},{8,14},{9,15},{10,... | collective-permute-start | bytes 196616 | tf_op jit(solution)/shard_map/ppermute | solution.py:24
  5.2 4.3 %collective-permute-start.3 = (bf16[64,512]{1,0:T(8,128)(2,1)S(1)}, bf16[64,512]{1,0:T(8,128)(2,1)S(1)}, u32[]{:S(2)}, u32[]{:S(2)}) collective-permute-start(bf16[64,512]{1,0:T(8,128)(2,1)S(1)} %get-tuple-element.51.refs_0_), channel_id=1, source_target_pairs={{0,4},{1,5},{2,6},{3,7},{4,0},{5,1},{6,2},{7,3},{8,12},{9,13},{10,... | collective-permute-start | bytes 196616 | tf_op jit(solution)/shard_map/ppermute | solution.py:24
  5.7 4.3 %collective-permute-start.1 = (bf16[64,512]{1,0:T(8,128)(2,1)S(1)}, bf16[64,512]{1,0:T(8,128)(2,1)S(1)}, u32[]{:S(2)}, u32[]{:S(2)}) collective-permute-start(bf16[64,512]{1,0:T(8,128)(2,1)S(1)} %get-tuple-element.51.refs_0_), channel_id=1, source_target_pairs={{0,2},{1,3},{2,0},{3,1},{4,6},{5,7},{6,4},{7,5},{8,10},{9,11},{10,... | collective-permute-start | bytes 196616 | tf_op jit(solution)/shard_map/ppermute | solution.py:24
  5.8 6.2 %collective-permute-start = (bf16[64,512]{1,0:T(8,128)(2,1)S(1)}, bf16[64,512]{1,0:T(8,128)(2,1)S(1)}, u32[]{:S(2)}, u32[]{:S(2)}) collective-permute-start(bf16[64,512]{1,0:T(8,128)(2,1)S(1)} %get-tuple-element.51.refs_0_), channel_id=1, source_target_pairs={{0,1},{1,0},{2,3},{3,2},{4,5},{5,4},{6,7},{7,6},{8,9},{9,8},{10,11... | collective-permute-start | bytes 196616 | tf_op jit(solution)/shard_map/ppermute | solution.py:24
  9.9 2.1 %collective-permute-start.2 = (bf16[64,512]{1,0:T(8,128)(2,1)S(1)}, bf16[64,512]{1,0:T(8,128)(2,1)S(1)}, u32[]{:S(2)}, u32[]{:S(2)}) collective-permute-start(bf16[64,512]{1,0:T(8,128)(2,1)S(1)} %collective-permute-done.1.refs_2_), channel_id=1, source_target_pairs={{0,1},{1,0},{2,3},{3,2},{4,5},{5,4},{6,7},{7,6},{8,9},{9,8},{10,11... | collective-permute-start | bytes 196616 | tf_op jit(solution)/shard_map/ppermute | solution.py:24
  9.9 2.1 %collective-permute-start.4 = (bf16[64,512]{1,0:T(8,128)(2,1)S(1)}, bf16[64,512]{1,0:T(8,128)(2,1)S(1)}, u32[]{:S(2)}, u32[]{:S(2)}) collective-permute-start(bf16[64,512]{1,0:T(8,128)(2,1)S(1)} %collective-permute-done.3.refs_4_), channel_id=1, source_target_pairs={{0,1},{1,0},{2,3},{3,2},{4,5},{5,4},{6,7},{7,6},{8,9},{9,8},{10,11... | collective-permute-start | bytes 196616 | tf_op jit(solution)/shard_map/ppermute | solution.py:24
  10.4 1.6 %collective-permute-start.6 = (bf16[64,512]{1,0:T(8,128)(2,1)S(1)}, bf16[64,512]{1,0:T(8,128)(2,1)S(1)}, u32[]{:S(2)}, u32[]{:S(2)}) collective-permute-start(bf16[64,512]{1,0:T(8,128)(2,1)S(1)} %collective-permute-done.5.refs_6_), channel_id=1, source_target_pairs={{0,1},{1,0},{2,3},{3,2},{4,5},{5,4},{6,7},{7,6},{8,9},{9,8},{10,11... | collective-permute-start | bytes 196616 | tf_op jit(solution)/shard_map/ppermute | solution.py:24
  10.4 9.2 %collective-permute-start.8 = (bf16[256,512]{1,0:T(8,128)(2,1)S(1)}, bf16[256,512]{1,0:T(8,128)(2,1)S(1)}, u32[]{:S(2)}, u32[]{:S(2)}) collective-permute-start(bf16[256,512]{1,0:T(8,128)(2,1)S(1)} %get-tuple-element.64.mine), channel_id=1, source_target_pairs={{0,8},{8,0},{16,24},{24,16},{1,9},{9,1},{17,25},{25,17},{2,10},{10... | collective-permute-start | bytes 786440 | tf_op jit(solution)/shard_map/ppermute | solution.py:24
  12.8 20.1 %collective-permute-start.7 = (bf16[320,512]{1,0:T(8,128)(2,1)S(1)}, bf16[320,512]{1,0:T(8,128)(2,1)S(1)}, u32[]{:S(2)}, u32[]{:S(2)}) collective-permute-start(bf16[320,512]{1,0:T(8,128)(2,1)S(1)} %get-tuple-element.63), channel_id=1, source_target_pairs={{0,8},{8,0},{16,24},{24,16},{1,9},{9,1},{17,25},{25,17},{2,10},{10... | collective-permute-start | bytes 983048 | tf_op jit(solution)/shard_map/ppermute | solution.py:24
  14.1 13.5 %collective-permute-start.9 = (bf16[64,512]{1,0:T(8,128)(2,1)S(1)}, bf16[64,512]{1,0:T(8,128)(2,1)S(1)}, u32[]{:S(2)}, u32[]{:S(2)}) collective-permute-start(bf16[64,512]{1,0:T(8,128)(2,1)S(1)} %get-tuple-element.55.refs_0_), channel_id=1, source_target_pairs={{0,8},{8,0},{16,24},{24,16},{1,9},{9,1},{17,25},{25,17},{2,10},{10... | collective-permute-start | bytes 196616 | tf_op jit(solution)/shard_map/ppermute | solution.py:24
  27.6 6.8 %collective-permute-start.15 = (bf16[64,512]{1,0:T(8,128)(2,1)S(1)}, bf16[64,512]{1,0:T(8,128)(2,1)S(1)}, u32[]{:S(2)}, u32[]{:S(2)}) collective-permute-start(bf16[64,512]{1,0:T(8,128)(2,1)S(1)} %shard_map.98.refs_0_), channel_id=1, source_target_pairs={{0,6},{1,7},{2,4},{3,5},{4,2},{5,3},{6,0},{7,1},{8,14},{9,15},{10,... | collective-permute-start | bytes 196616 | tf_op jit(solution)/shard_map/ppermute | solution.py:24
  29.6 5.4 %collective-permute-start.13 = (bf16[64,512]{1,0:T(8,128)(2,1)S(1)}, bf16[64,512]{1,0:T(8,128)(2,1)S(1)}, u32[]{:S(2)}, u32[]{:S(2)}) collective-permute-start(bf16[64,512]{1,0:T(8,128)(2,1)S(1)} %shard_map.98.refs_0_), channel_id=1, source_target_pairs={{0,4},{1,5},{2,6},{3,7},{4,0},{5,1},{6,2},{7,3},{8,12},{9,13},{10,... | collective-permute-start | bytes 196616 | tf_op jit(solution)/shard_map/ppermute | solution.py:24
  30.1 5.0 %collective-permute-start.11 = (bf16[64,512]{1,0:T(8,128)(2,1)S(1)}, bf16[64,512]{1,0:T(8,128)(2,1)S(1)}, u32[]{:S(2)}, u32[]{:S(2)}) collective-permute-start(bf16[64,512]{1,0:T(8,128)(2,1)S(1)} %shard_map.98.refs_0_), channel_id=1, source_target_pairs={{0,2},{1,3},{2,0},{3,1},{4,6},{5,7},{6,4},{7,5},{8,10},{9,11},{10,... | collective-permute-start | bytes 196616 | tf_op jit(solution)/shard_map/ppermute | solution.py:24
  32.8 2.7 %collective-permute-start.10 = (bf16[64,512]{1,0:T(8,128)(2,1)S(1)}, bf16[64,512]{1,0:T(8,128)(2,1)S(1)}, u32[]{:S(2)}, u32[]{:S(2)}) collective-permute-start(bf16[64,512]{1,0:T(8,128)(2,1)S(1)} %shard_map.98.refs_0_), channel_id=1, source_target_pairs={{0,1},{1,0},{2,3},{3,2},{4,5},{5,4},{6,7},{7,6},{8,9},{9,8},{10,11... | collective-permute-start | bytes 196616 | tf_op jit(solution)/shard_map/ppermute | solution.py:24
  37.1 37.7 %collective-permute-start.17 = (bf16[320,512]{1,0:T(8,128)(2,1)S(1)}, bf16[320,512]{1,0:T(8,128)(2,1)S(1)}, u32[]{:S(2)}, u32[]{:S(2)}) collective-permute-start(bf16[320,512]{1,0:T(8,128)(2,1)S(1)} %get-tuple-element.77), channel_id=1, source_target_pairs={{0,16},{8,24},{16,0},{24,8},{1,17},{9,25},{17,1},{25,9},{2,18},{10... | collective-permute-start | bytes 983048 | tf_op jit(solution)/shard_map/ppermute | solution.py:24
  39.8 12.1 %collective-permute-start.19 = (bf16[96,512]{1,0:T(8,128)(2,1)S(1)}, bf16[96,512]{1,0:T(8,128)(2,1)S(1)}, u32[]{:S(2)}, u32[]{:S(2)}) collective-permute-start(bf16[96,512]{1,0:T(8,128)(2,1)S(1)} %get-tuple-element.78), channel_id=1, source_target_pairs={{0,24},{8,16},{16,8},{24,0},{1,25},{9,17},{17,9},{25,1},{2,26},{10... | collective-permute-start | bytes 294920 | tf_op jit(solution)/shard_map/ppermute | solution.py:24
  41.1 24.4 %collective-permute-start.18 = (bf16[96,512]{1,0:T(8,128)(2,1)S(1)}, bf16[96,512]{1,0:T(8,128)(2,1)S(1)}, u32[]{:S(2)}, u32[]{:S(2)}) collective-permute-start(bf16[96,512]{1,0:T(8,128)(2,1)S(1)} %get-tuple-element.78), channel_id=1, source_target_pairs={{0,16},{8,24},{16,0},{24,8},{1,17},{9,25},{17,1},{25,9},{2,18},{10... | collective-permute-start | bytes 294920 | tf_op jit(solution)/shard_map/ppermute | solution.py:24
  42.8 23.6 %collective-permute-start.22 = (bf16[32,512]{1,0:T(8,128)(2,1)S(1)}, bf16[32,512]{1,0:T(8,128)(2,1)S(1)}, u32[]{:S(2)}, u32[]{:S(2)}) collective-permute-start(bf16[32,512]{1,0:T(8,128)(2,1)S(1)} %get-tuple-element.79.refs_0_), channel_id=1, source_target_pairs={{0,24},{8,16},{16,8},{24,0},{1,25},{9,17},{17,9},{25,1},{2,26},{10... | collective-permute-start | bytes 98312 | tf_op jit(solution)/shard_map/ppermute | solution.py:24
  43.7 22.7 %collective-permute-start.21 = (bf16[32,512]{1,0:T(8,128)(2,1)S(1)}, bf16[32,512]{1,0:T(8,128)(2,1)S(1)}, u32[]{:S(2)}, u32[]{:S(2)}) collective-permute-start(bf16[32,512]{1,0:T(8,128)(2,1)S(1)} %get-tuple-element.79.refs_0_), channel_id=1, source_target_pairs={{0,16},{8,24},{16,0},{24,8},{1,17},{9,25},{17,1},{25,9},{2,18},{10... | collective-permute-start | bytes 98312 | tf_op jit(solution)/shard_map/ppermute | solution.py:24
  51.9 14.6 %collective-permute-start.20 = (bf16[32,512]{1,0:T(8,128)(2,1)S(1)}, bf16[32,512]{1,0:T(8,128)(2,1)S(1)}, u32[]{:S(2)}, u32[]{:S(2)}) collective-permute-start(bf16[32,512]{1,0:T(8,128)(2,1)S(1)} %get-tuple-element.79.refs_0_), channel_id=1, source_target_pairs={{0,8},{8,0},{16,24},{24,16},{1,9},{9,1},{17,25},{25,17},{2,10},{10... | collective-permute-start | bytes 98312 | tf_op jit(solution)/shard_map/ppermute | solution.py:24
  66.5 5.9 %collective-permute-start.28 = (bf16[64,512]{1,0:T(8,128)(2,1)S(1)}, bf16[64,512]{1,0:T(8,128)(2,1)S(1)}, u32[]{:S(2)}, u32[]{:S(2)}) collective-permute-start(bf16[64,512]{1,0:T(8,128)(2,1)S(1)} %shard_map.102.refs_0_), channel_id=1, source_target_pairs={{0,6},{1,7},{2,4},{3,5},{4,2},{5,3},{6,0},{7,1},{8,14},{9,15},{10,... | collective-permute-start | bytes 196616 | tf_op jit(solution)/shard_map/ppermute | solution.py:24
  68.4 4.5 %collective-permute-start.26 = (bf16[64,512]{1,0:T(8,128)(2,1)S(1)}, bf16[64,512]{1,0:T(8,128)(2,1)S(1)}, u32[]{:S(2)}, u32[]{:S(2)}) collective-permute-start(bf16[64,512]{1,0:T(8,128)(2,1)S(1)} %shard_map.102.refs_0_), channel_id=1, source_target_pairs={{0,4},{1,5},{2,6},{3,7},{4,0},{5,1},{6,2},{7,3},{8,12},{9,13},{10,... | collective-permute-start | bytes 196616 | tf_op jit(solution)/shard_map/ppermute | solution.py:24
  69.0 4.3 %collective-permute-start.24 = (bf16[64,512]{1,0:T(8,128)(2,1)S(1)}, bf16[64,512]{1,0:T(8,128)(2,1)S(1)}, u32[]{:S(2)}, u32[]{:S(2)}) collective-permute-start(bf16[64,512]{1,0:T(8,128)(2,1)S(1)} %shard_map.102.refs_0_), channel_id=1, source_target_pairs={{0,2},{1,3},{2,0},{3,1},{4,6},{5,7},{6,4},{7,5},{8,10},{9,11},{10,... | collective-permute-start | bytes 196616 | tf_op jit(solution)/shard_map/ppermute | solution.py:24
  71.7 1.7 %collective-permute-start.23 = (bf16[64,512]{1,0:T(8,128)(2,1)S(1)}, bf16[64,512]{1,0:T(8,128)(2,1)S(1)}, u32[]{:S(2)}, u32[]{:S(2)}) collective-permute-start(bf16[64,512]{1,0:T(8,128)(2,1)S(1)} %shard_map.102.refs_0_), channel_id=1, source_target_pairs={{0,1},{1,0},{2,3},{3,2},{4,5},{5,4},{6,7},{7,6},{8,9},{9,8},{10,11... | collective-permute-start | bytes 196616 | tf_op jit(solution)/shard_map/ppermute | solution.py:24
  (7 other events, 13.6 us)

commit v3 on v2

v3 whole, which is shorter than its diff:
```python
import jax
import jax.numpy as jnp
from jax import lax
from jax.experimental import pallas as pl
from jax.experimental.pallas import tpu as pltpu
from jax.sharding import PartitionSpec as P


BF = jnp.bfloat16
F32 = jnp.float32
I32 = jnp.int32
NT = (((1,), (1,)), ((), ()))
NN = (((1,), (0,)), ((), ()))
VM = pl.BlockSpec(memory_space=pltpu.VMEM)
SM = pl.BlockSpec(memory_space=pltpu.SMEM)
VP = pl.BlockSpec(memory_space=pltpu.VMEM)
AN = pl.BlockSpec(memory_space=pltpu.HBM)


def dot(a, b, dims):
    return lax.dot_general(a, b, dims, preferred_element_type=F32)


def swap(value, axis, mask):
    return lax.ppermute(value, axis, [(i, i ^ mask) for i in range(lax.axis_size(axis))])


def later(value, *others):
    return lax.optimization_barrier((value,) + others)[0]


def call(body, in_specs, outs, scratch=(), out_specs=None):
    made = pl.pallas_call(
        body, in_specs=in_specs, out_specs=out_specs or [VM] * len(outs),
        out_shape=[jax.ShapeDtypeStruct(s, d) for s, d in outs], scratch_shapes=scratch,
        compiler_params=pltpu.CompilerParams(vmem_limit_bytes=16 * 1024 * 1024),
    )

    def run(*args):
        return made(*[
            pltpu.with_memory_space_constraint(a, pltpu.HBM) if spec is AN
            else pltpu.with_memory_space_constraint(a, pltpu.VMEM) if spec is VP else a
            for a, spec in zip(args, in_specs)
        ])

    return run


def copies(sems, pairs):
    made = [pltpu.make_async_copy(a, b, sems.at[i]) for i, (a, b) in enumerate(pairs)]
    for c in made:
        c.start()
    return made


def one_hot(row, count):
    ids = lax.broadcasted_iota(I32, (count, row.shape[1]), 0)
    return jnp.where(ids == row, 1.0, 0.0).astype(BF)


def slots_of(code, rows):
    outward = code >= rows
    flags = jnp.broadcast_to(jnp.where(outward, 1.0, 0.0).astype(BF), (8, rows))
    a = lax.broadcasted_iota(I32, (rows, rows), 0)
    b = lax.broadcasted_iota(I32, (rows, rows), 1)
    upper = jnp.where(a < b, 1.0, 0.0).astype(BF)
    rank = dot(flags, upper, NN)[:1].astype(I32)
    return jnp.where(outward, rank, -1)


def landing_of(code, rows):
    pick = one_hot(slots_of(code, rows), rows // 2)
    target = one_hot(code - rows, rows)
    return dot(target, pick, NT).astype(BF)


def row_picks(code, live, n):
    rows = code.shape[1]
    alive = lax.broadcasted_iota(I32, (1, rows), 1) < live
    shown = jnp.where(alive, code, -1)
    slot = jnp.where(alive, slots_of(code, rows), -1)
    ids = lax.broadcasted_iota(I32, (2 * n, rows), 0)
    pivot = jnp.where(jnp.where(ids < n, ids, ids + (rows - n)) == shown, 1.0, 0.0).astype(BF)
    bulk = one_hot(slot, rows // 2)
    return jnp.concatenate([pivot, bulk], 0)


def own_pick(code, live):
    rows = code.shape[1]
    return one_hot(jnp.where(lax.broadcasted_iota(I32, (1, rows), 1) < live, code, -1), rows)


def scaled(panel, inverse):
    block = inverse.shape[1]
    parts = [
        dot(panel[:, b * block:(b + 1) * block], inverse[b * block:(b + 1) * block], NT)
        for b in range(inverse.shape[0] // block)
    ]
    return jnp.concatenate(parts, 1)


def factor_of(panel, inverse, live):
    mask = lax.broadcasted_iota(I32, (panel.shape[0], 1), 0) < live
    return jnp.where(mask, scaled(panel, inverse), 0.0).astype(BF)


def reordered(value, outer, middle):
    rows = value.shape[0]
    part = rows // (outer * middle)
    if middle == 1:
        return value
    if part % 16 == 0:
        return jnp.concatenate(
            [value[(o * middle + m) * part:(o * middle + m + 1) * part]
             for m in range(middle) for o in range(outer)], 0)
    target = lax.broadcasted_iota(I32, (rows, rows), 0)
    source = lax.broadcasted_iota(I32, (rows, rows), 1)
    k = target % part
    o = target // part % outer
    m = target // (part * outer)
    return dot(jnp.where((o * middle + m) * part + k == source, 1.0, 0.0).astype(BF), value, NN).astype(BF)


def spread(block):
    if lax.axis_size("inner") != 8 or block.shape[0] % 32:
        return {}
    return {m: swap(block, "inner", m) for m in GATHER_ORDER}


def collect(block, got):
    if not got:
        return [lax.all_gather(block, "inner", axis=0, tiled=True)]
    got = dict(got)
    got[0] = block
    for m in (0,) + GATHER_ORDER:
        got[m + 1] = swap(got[m], "inner", 1)
    return [got[m] for m in range(8)]


GATHER_ORDER = (6, 4, 2)


def pivots_from(blocks, inverse, pivots, middle, inner):
    if len(blocks) == 1:
        pivots[...] = reordered(scaled(blocks[0], inverse).astype(BF), inner, middle)
        return
    size = blocks[0].shape[0]
    part = size // middle
    made = scaled(jnp.concatenate(blocks, 0), inverse).astype(BF)
    for m in range(len(blocks)):
        at = (lax.axis_index("inner") ^ m) * part
        for q in range(middle):
            pivots[pl.ds(pl.multiple_of(q * part * inner + at, part), part), :] = (
                made[m * size + q * part:m * size + (q + 1) * part])


def up16(count):
    return (count + 15) // 16 * 16


def code_row(ref):
    return jnp.concatenate([ref[i:i + 1] for i in range(ref.shape[0])], 1)


def up16(count):
    return (count + 15) // 16 * 16


def per_device(front_leaf, front_mid, front_top, dinv_leaf, dinv_mid, dinv_top, live_rows, map_leaf, map_mid):
    rows = front_leaf.shape[0]
    panel, block = dinv_leaf.shape
    cols = front_leaf.shape[1] - panel
    inner = lax.axis_size("inner")
    half = rows // 2
    n = [cols // (inner << l) for l in range(3)]

    lanes = 128 if rows % 128 == 0 else rows
    code0 = map_leaf.reshape(rows // lanes, lanes)
    code1 = map_mid.reshape(rows // lanes, lanes)
    live = live_rows.reshape(1, 3)

    mr = dinv_mid.shape[0] // 2
    share = dinv_top.shape[0] // inner
    shared = inner == 8 and share % 16 == 0 and lanes == 128 and rows // lanes <= share and 2 * block == panel

    def pack(code0_ref, code1_ref, mid, fmid, ftop, leaf, near, c0v, c1v, head, top_head, sems):
        made = copies(sems, [
            (code0_ref, c0v), (code1_ref, c1v), (leaf.at[:n[0], :panel], head),
            (mid.at[:mr], near.at[:mr, :block]), (mid.at[mr:], near.at[:mr, block:]),
            (fmid.at[:n[1], :panel], near.at[mr + 16:mr + 16 + n[1]]), (ftop.at[:n[2], :panel], top_head),
        ])
        made[0].wait()
        code = code_row(c0v)
        parts = jnp.concatenate([code >> 8, code & 255, jnp.zeros((6, rows), I32)], 0).astype(F32).astype(BF)
        padded = jnp.concatenate([parts, jnp.zeros((8, 2 * panel - rows), BF)], 1)
        near[mr:mr + 16] = jnp.concatenate([padded[:, :panel], padded[:, panel:]], 0)
        for c in made[1:]:
            c.wait()

    near, code0, code1, block0, top_head = call(
        pack, [AN] * 6,
        [((mr + 16 + up16(n[1]), panel), BF), (code0.shape, I32), (code1.shape, I32), ((n[0], panel), BF),
         ((n[2], panel), BF)],
        scratch=[pltpu.SemaphoreType.DMA((7,))],
    )(code0, code1, dinv_mid, front_mid, front_top, front_leaf)
    got0 = spread(block0)
    near_1 = swap(near, "sub", 1)

    def sent(level):
        return [((2 * n[level] + half, cols), BF)] * 2

    def before0(live_ref, code, front, inverse, fs, cs, factor):
        pick = row_picks(code_row(code), live_ref[0, 0], n[1])
        factor[...] = factor_of(front[:, :panel], inverse[...], live_ref[0, 0])
        cs[...] = dot(pick, front[:, panel:], NN).astype(BF)
        fs[...] = dot(pick, factor[...], NN).astype(BF)

    fs0, cs0, factor0 = call(
        before0, [SM, VM, VP, VP], sent(1) + [((rows, panel), BF)],
    )(live, code0, front_leaf, dinv_leaf)
    blocks0 = collect(block0, got0)

    def chain(middle, count, headed, extra):
        def body(fs, cs, inverse, *refs):
            refs = list(refs)
            head = refs.pop(0) if headed else None
            code_ref, top = (refs.pop(0), refs.pop(0)) if extra else (None, None)
            blocks, (pivots, out, bulk) = refs[:-3], refs[-3:]
            pivots_from([ref[...] for ref in blocks], inverse[...], pivots, middle, inner)
            update = (cs[...].astype(F32) - dot(fs[...], pivots[...], NT)).astype(BF)
            out[:count] = (update[:count].astype(F32) + head[...].astype(F32)).astype(BF) if headed else update[:count]
            out[count:2 * count] = update[count:2 * count]
            if extra:
                tail = slice(2 * count, 2 * count + share)
                at = pl.multiple_of(lax.axis_index("inner") * share, share)
                out[tail, :block] = top[pl.ds(at, share), :]
                code = jnp.concatenate([code_ref[...], jnp.zeros((share - rows // lanes, lanes), I32)], 0)
                out[tail, block:block + lanes] = (code >> 8).astype(F32).astype(BF)
                out[tail, block + lanes:] = (code & 255).astype(F32).astype(BF)
            bulk[...] = update[2 * count:]

        return body

    def after(level, fs, cs, inverse, blocks, head=(), extra=()):
        count = n[level + 1]
        return call(
            chain(1 << level, count, bool(head), bool(extra)),
            [VM] * (3 + len(head) + len(extra) + len(blocks)),
            [((cols, panel), BF), ((2 * count + (share if extra else 0), cols), BF), ((half, cols), BF)],
        )(fs, cs, inverse, *head, *extra, *blocks)

    def own(level, code, factor, front, pivots, parent):
        def body(live_ref, code_ref, factor_ref, front_ref, pivots_ref, parent_ref, out):
            update = (front_ref[:, panel:].astype(F32) - dot(factor_ref[...], pivots_ref[...], NT)).astype(BF)
            pick = own_pick(code_row(code_ref), live_ref[0, level])
            out[...] = parent_ref[:, :cols].astype(F32) + dot(pick, update, NN)

        return call(body, [SM, VM, VM, VP, VM, VP], [((rows, cols), F32)])(
            live, code, factor, front, pivots, parent)[0]

    pivots0, pivot0, bulk0 = after(0, fs0, cs0, dinv_leaf, blocks0)
    pivot0_other = swap(pivot0, "sub", 1)
    bulk0_other = swap(bulk0, "sub", 1)

    def unpack1(mine, near_ref, inv_mid, heads1, land0):
        sub = lax.axis_index("sub")
        for q, src in enumerate((mine, near_ref)):
            at = ((sub & 1) ^ q) * 2 * mr
            inv_mid[pl.ds(pl.multiple_of(at, mr), mr), :] = src[:mr, :block]
            inv_mid[pl.ds(pl.multiple_of(at + mr, mr), mr), :] = src[:mr, block:]
            heads1[q] = src[mr + 16:]
        packed = near_ref[mr:mr + 16].astype(F32).astype(I32)
        high = jnp.concatenate([packed[0:1], packed[8:9]], 1)[:, :rows]
        low = jnp.concatenate([packed[1:2], packed[9:10]], 1)[:, :rows]
        land0[...] = landing_of(high * 256 + low, rows)

    inv_mid, heads1, land0 = call(
        unpack1, [VM] * 2,
        [(dinv_leaf.shape, BF), ((2, up16(n[1]), panel), BF), ((rows, half), BF)],
    )(near, later(near_1, pivot0))

    def early1(live_ref, code, front, pick_out, cs):
        pick = row_picks(code_row(code), live_ref[0, 1], n[2])
        pick_out[...] = pick
        cs[...] = dot(pick, front[:, panel:], NN).astype(BF)

    pick1, cs1 = call(
        early1, [SM, VM, VP], [((2 * n[2] + half, rows), BF)] + sent(2)[:1],
    )(live, later(code1, pivot0), front_mid)

    def raised(count, flip, headed, extra):
        def body(*refs):
            heads, others, out = refs[0] if headed else None, refs[headed:-1], refs[-1]
            sub = lax.axis_index("sub")

            def ordered(made):
                bit = 1
                while len(made) > 1:
                    low = (sub & bit) == 0
                    made = [
                        jnp.concatenate([jnp.where(low, a, b), jnp.where(low, b, a)], 0)
                        for a, b in zip(made[::2], made[1::2])
                    ]
                    bit *= 2
                return made[0]

            made = [
                others[q][:count].astype(F32) + others[q ^ flip][count:2 * count].astype(F32)
                for q in range(len(others))
            ]
            if headed:
                made = [heads[q][:count].astype(F32) + part for q, part in enumerate(made)]
            total = ordered(made)
            size = total.shape[0]
            out[:size] = total.astype(BF)
            if extra:
                tops = ordered([ref[2 * count:2 * count + share, :block].astype(F32) for ref in others]).astype(BF)
                for q in range(len(others)):
                    at = size + q // 2 * share
                    lane = q % 2 * block
                    out[at:at + share, lane:lane + block] = tops[q * share:(q + 1) * share]

        return body

    raw1, = call(raised(n[1], 1, 1, False), [VM] * 3, [((2 * n[1], panel), BF)])(
        later(heads1, pick1), pivot0, pivot0_other)
    spread1 = spread(raw1)
    merged0 = own(0, code0, factor0, front_leaf, pivots0, front_mid)

    def before1(live_ref, pick, merged, got, land, inverse, fs, factor):
        assembled = (merged[...] + dot(land[...], got[...], NN)).astype(BF)
        factor[...] = factor_of(assembled, inverse[...], live_ref[0, 1])
        fs[...] = dot(pick[...], factor[...], NN).astype(BF)

    fs1, factor1 = call(
        before1, [SM] + [VM] * 5, sent(2)[:1] + [((rows, panel), BF)],
    )(live, pick1, merged0, bulk0_other, land0, inv_mid)
    blocks1 = collect(raw1, spread1)
    pivots1, pivot1, bulk1 = after(
        1, fs1, cs1, inv_mid, blocks1, (top_head,), (code1, dinv_top) if shared else ())
    others = [pivot1] + [swap(pivot1, "sub", m) for m in (1, 2, 3)]
    bulk1_other = swap(bulk1, "sub", 2)
    raw2, = call(raised(n[2], 2, 0, shared), [VM] * 4, [((4 * n[2] + (2 * share if shared else 0), panel), BF)])(*others)
    spread2 = spread(raw2)
    merged1 = own(1, code1, factor1, front_mid, pivots1, front_top)
    blocks2 = collect(raw2, spread2)

    def landing1(src, land1):
        if not shared:
            land1[...] = landing_of(code_row(src), rows)
            return
        packed = src[2 * n[2]:, block:].astype(F32).astype(I32)
        code = packed[:rows // lanes, :lanes] * 256 + packed[:rows // lanes, lanes:]
        land1[...] = landing_of(jnp.concatenate([code[i:i + 1] for i in range(rows // lanes)], 1), rows)

    far1 = others[2] if shared else swap(code1, "sub", 2)
    land1, = call(landing1, [VM], [((rows, half), BF)])(later(far1, raw2))

    if shared:
        def last_pivots(*refs):
            blocks, pivots, inv_top = refs[:-2], refs[-2], refs[-1]
            size = 4 * n[2]
            for m, ref in enumerate(blocks):
                for q in range(4):
                    at = q * inner * share + (lax.axis_index("inner") ^ m) * share
                    row, lane = size + q // 2 * share, q % 2 * block
                    inv_top[pl.ds(pl.multiple_of(at, share), share), :] = ref[row:row + share, lane:lane + block]
            pivots_from([ref[:size] for ref in blocks], inv_top[...], pivots, 4, inner)

        pivots2, inv_top = call(
            last_pivots, [VM] * len(blocks2), [((cols, panel), BF), (dinv_leaf.shape, BF)])(*blocks2)
    else:
        def last_pivots(inverse, *refs):
            pivots_from([ref[...] for ref in refs[:-1]], inverse[...], refs[-1], 4, inner)

        sub = lax.axis_index("sub")
        inv_top = dinv_top
        for bit in (1, 2):
            other = swap(inv_top, "sub", bit)
            inv_top = jnp.where(
                sub & bit == 0, jnp.concatenate([inv_top, other], 0), jnp.concatenate([other, inv_top], 0))
        pivots2, = call(last_pivots, [VM] * (1 + len(blocks2)), [((cols, panel), BF)])(inv_top, *blocks2)

    steps = 2 if rows % 32 == 0 else 1
    part = rows // steps

    def level2(live_ref, front, merged, got, land, inverse, pivots, out, ov, sems):
        assembled = (merged[...] + dot(land[...], got[...], NN)).astype(BF)
        factor = factor_of(assembled, inverse[...], live_ref[0, 2])
        mask = lax.broadcasted_iota(I32, (rows, 1), 0) < live_ref[0, 2]
        writes = []
        for i in range(steps):
            at = slice(i * part, (i + 1) * part)
            product = dot(factor[at], pivots[...], NT)
            ov[at] = jnp.where(mask[at], front[at, panel:].astype(F32) - product, 0.0).astype(BF)
            writes += copies(sems.at[i:i + 1], [(ov.at[at], out.at[at])])
        for write in writes:
            write.wait()

    out, = call(
        level2, [SM, VP] + [VM] * 5, [((rows, cols), BF)],
        scratch=[pltpu.VMEM((rows, cols), BF), pltpu.SemaphoreType.DMA((steps,))],
        out_specs=[AN],
    )(live, front_top, merged1, bulk1_other, land1, inv_top, pivots2)
    return out


def solution(mesh):
    row = P(("sub", "inner"), None)
    placed = (
        row, row, row, P("sub", None), P("sub", None), P("sub", None),
        P(None, ("sub", "inner")), P(("sub", "inner")), P(("sub", "inner")),
    )

    return jax.shard_map(per_device, mesh=mesh, in_specs=placed, out_specs=row, check_vma=False)
```

time: 77.4 us -> 74.8 us (0.966)
  starting transfers between devices: 37.9 us -> 22.6 us
  waiting for transfers between devices: 22.4 us -> 37.1 us
  Pallas kernels: 16.6 us -> 14.6 us
    ppermute x30 -> x28, starting transfers between devices: 37.9 us -> 22.6 us  [swap(): lax.ppermute(value, axis, [(i, i ^ mask) for i in range(lax.axis_size(axi...]
    ppermute x30 -> x28, waiting for transfers between devices: 22.4 us -> 37.1 us  [swap(): lax.ppermute(value, axis, [(i, i ^ mask) for i in range(lax.axis_size(axi...]
    pallas_call x14, Pallas kernels: 16.6 us -> 14.6 us  [run(): made(*[pltpu.with_memory_space_constraint(a, pltpu.HBM) if spec is AN els...]
  transfers between devices with their start and end apart: 30 -> 28, of which waited for: 15 -> 11; matrix products, arithmetic and copies ran while one was open for 0% -> 0% of each run, Pallas kernels for 16% -> 13%
where the time goes in v3:
time: 74.8 us; the launch traced here: 74.7 us
  waiting for transfers between devices  37.1 us (50%)
  starting transfers between devices  22.6 us (30%)
  Pallas kernels  14.6 us (20%)
    ppermute x28, waiting for transfers between devices, swap(): lax.ppermute(value, axis, [(i, i ^ mask) for i in range(lax.axis_size(axi...  37.1 us
    ppermute x28, starting transfers between devices, swap(): lax.ppermute(value, axis, [(i, i ^ mask) for i in range(lax.axis_size(axi...  22.6 us
    pallas_call x14, Pallas kernels, run(): made(*[pltpu.with_memory_space_constraint(a, pltpu.HBM) if spec is AN els...  14.6 us
  transfers between devices with their start and end apart: 28, of which 11 were waited for; matrix products, arithmetic and copies ran while one was open for 0% of the time, Pallas kernels for 13%

profile of v3, /device:TPU:0, one launch (start us, length us, event | category | flops | bytes accessed | tf_op | source)
XLA Modules:
  0.0 74.7 jit_solution(18231475451210119406)
XLA Ops:
  1.1 3.0 %collective-permute-start.1 = (bf16[64,512]{1,0:T(8,128)(2,1)S(1)}, bf16[64,512]{1,0:T(8,128)(2,1)S(1)}, u32[]{:S(2)}, u32[]{:S(2)}) collective-permute-start(bf16[64,512]{1,0:T(8,128)(2,1)S(1)} %get-tuple-element.36.refs_0_), channel_id=1, source_target_pairs={{0,2},{1,3},{2,0},{3,1},{4,6},{5,7},{6,4},{7,5},{8,10},{9,11},{10,... | collective-permute-start | bytes 196616 | tf_op jit(solution)/shard_map/ppermute | solution.py:25
  4.2 1.5 %collective-permute-start.3 = (bf16[64,512]{1,0:T(8,128)(2,1)S(1)}, bf16[64,512]{1,0:T(8,128)(2,1)S(1)}, u32[]{:S(2)}, u32[]{:S(2)}) collective-permute-start(bf16[64,512]{1,0:T(8,128)(2,1)S(1)} %get-tuple-element.36.refs_0_), channel_id=1, source_target_pairs={{0,4},{1,5},{2,6},{3,7},{4,0},{5,1},{6,2},{7,3},{8,12},{9,13},{10,... | collective-permute-start | bytes 196616 | tf_op jit(solution)/shard_map/ppermute | solution.py:25
  6.5 1.9 %collective-permute-done.3.refs_4_ = bf16[64,512]{1,0:T(8,128)(2,1)S(1)} collective-permute-done((bf16[64,512]{1,0:T(8,128)(2,1)S(1)}, bf16[64,512]{1,0:T(8,128)(2,1)S(1)}, u32[]{:S(2)}, u32[]{:S(2)}) %collective-permute-start.3) | collective-permute-done | bytes 65568 | tf_op jit(solution)/shard_map/ppermute | solution.py:25
  8.4 2.4 %collective-permute-done.5.refs_6_ = bf16[64,512]{1,0:T(8,128)(2,1)S(1)} collective-permute-done((bf16[64,512]{1,0:T(8,128)(2,1)S(1)}, bf16[64,512]{1,0:T(8,128)(2,1)S(1)}, u32[]{:S(2)}, u32[]{:S(2)}) %collective-permute-start.5) | collective-permute-done | bytes 65568 | tf_op jit(solution)/shard_map/ppermute | solution.py:25
  10.9 1.6 %shard_map.92 = (bf16[384,512]{1,0:T(8,128)(2,1)S(1)}, bf16[384,512]{1,0:T(8,128)(2,1)S(1)}, bf16[640,512]{1,0:T(8,128)(2,1)S(1)}) custom-call(s32[1,3]{1,0:T(1,128)S(1)} %bitcast.3, s32[5,128]{1,0:T(8,128)S(1)} %get-tuple-element.33.code.code_ref, bf16[640,1024]{1,0:T(8,128)(2,1)S(1)} %copy-done.2, bf16[512,256]{1,0:T(8,128)(2,1)S(1)} %copy-done.3), custom_call_target="tpu_custom_call" | custom-call | tf_op jit(solution)/shard_map/pallas_call | solution.py:40
  13.3 1.6 %collective-permute-start.7 = (bf16[320,512]{1,0:T(8,128)(2,1)S(1)}, bf16[320,512]{1,0:T(8,128)(2,1)S(1)}, u32[]{:S(2)}, u32[]{:S(2)}) collective-permute-start(bf16[320,512]{1,0:T(8,128)(2,1)S(1)} %get-tuple-element.42), channel_id=1, source_target_pairs={{0,8},{8,0},{16,24},{24,16},{1,9},{9,1},{17,25},{25,17},{2,10},{10... | collective-permute-start | bytes 983048 | tf_op jit(solution)/shard_map/ppermute | solution.py:25
  15.4 1.6 %collective-permute-start.9 = (bf16[64,512]{1,0:T(8,128)(2,1)S(1)}, bf16[64,512]{1,0:T(8,128)(2,1)S(1)}, u32[]{:S(2)}, u32[]{:S(2)}) collective-permute-start(bf16[64,512]{1,0:T(8,128)(2,1)S(1)} %get-tuple-element.37.refs_1_), channel_id=1, source_target_pairs={{0,8},{8,0},{16,24},{24,16},{1,9},{9,1},{17,25},{25,17},{2,10},{10... | collective-permute-start | bytes 196616 | tf_op jit(solution)/shard_map/ppermute | solution.py:25
  17.0 1.2 %shard_map.94 = (bf16[352,640]{1,0:T(8,128)(2,1)S(1)}, bf16[352,512]{1,0:T(8,128)(2,1)S(1)}) custom-call(s32[1,3]{1,0:T(1,128)S(1)} %bitcast.4, s32[5,128]{1,0:T(8,128)S(1)} %get-tuple-element.38.code.refs_1_.code_ref, bf16[640,1024]{1,0:T(8,128)(2,1)S(1)} %copy-done), custom_call_target="tpu_custom_call" | custom-call | tf_op jit(solution)/shard_map/pallas_call | solution.py:40
  18.2 9.7 %collective-permute-done.8.near_ref = bf16[176,512]{1,0:T(8,128)(2,1)S(1)} collective-permute-done((bf16[176,512]{1,0:T(8,128)(2,1)S(1)}, bf16[176,512]{1,0:T(8,128)(2,1)S(1)}, u32[]{:S(2)}, u32[]{:S(2)}) %collective-permute-start.8) | collective-permute-done | bytes 180256 | tf_op jit(solution)/shard_map/ppermute | solution.py:25
  29.9 2.4 %collective-permute-start.15 = (bf16[64,512]{1,0:T(8,128)(2,1)S(1)}, bf16[64,512]{1,0:T(8,128)(2,1)S(1)}, u32[]{:S(2)}, u32[]{:S(2)}) collective-permute-start(bf16[64,512]{1,0:T(8,128)(2,1)S(1)} %shard_map.98.refs_3_), channel_id=1, source_target_pairs={{0,6},{1,7},{2,4},{3,5},{4,2},{5,3},{6,0},{7,1},{8,14},{9,15},{10,... | collective-permute-start | bytes 196616 | tf_op jit(solution)/shard_map/ppermute | solution.py:25
  32.3 1.4 %collective-permute-done.11.refs_5_ = bf16[64,512]{1,0:T(8,128)(2,1)S(1)} collective-permute-done((bf16[64,512]{1,0:T(8,128)(2,1)S(1)}, bf16[64,512]{1,0:T(8,128)(2,1)S(1)}, u32[]{:S(2)}, u32[]{:S(2)}) %collective-permute-start.11) | collective-permute-done | bytes 65568 | tf_op jit(solution)/shard_map/ppermute | solution.py:25
  35.1 1.6 %shard_map.95.merged = f32[640,512]{1,0:T(8,128)S(1)} custom-call(s32[1,3]{1,0:T(1,128)S(1)} %bitcast.5, s32[5,128]{1,0:T(8,128)S(1)} %get-tuple-element.33.code.code_ref, bf16[640,512]{1,0:T(8,128)(2,1)S(1)} %get-tuple-element.40.factor_ref, bf16[640,1024]{1,0:T(8,128)(2,1)S(1)} %copy-done.2, bf16[512,512]{1,0:T(8,128)(2,1)S(1)} %get-tuple-element.41.pivots_ref, ...), custom_call_target="tpu_custom_call" | custom-call | tf_op jit(solution)/shard_map/pallas_call | solution.py:40
  36.7 1.5 %shard_map.97 = (bf16[352,512]{1,0:T(8,128)(2,1)S(1)}, bf16[640,512]{1,0:T(8,128)(2,1)S(1)}) custom-call(s32[1,3]{1,0:T(1,128)S(1)} %bitcast.6, bf16[352,640]{1,0:T(8,128)(2,1)S(1)} %get-tuple-element.39.pick, f32[640,512]{1,0:T(8,128)S(1)} %shard_map.95.merged, bf16[320,512]{1,0:T(8,128)(2,1)S(1)} %collective-permute-done.7.got, ...), custom_call_target="tpu_custom_call" | custom-call | tf_op jit(solution)/shard_map/pallas_call | solution.py:40
  39.1 2.6 %collective-permute-start.17 = (bf16[320,512]{1,0:T(8,128)(2,1)S(1)}, bf16[320,512]{1,0:T(8,128)(2,1)S(1)}, u32[]{:S(2)}, u32[]{:S(2)}) collective-permute-start(bf16[320,512]{1,0:T(8,128)(2,1)S(1)} %get-tuple-element.54), channel_id=1, source_target_pairs={{0,16},{8,24},{16,0},{24,8},{1,17},{9,25},{17,1},{25,9},{2,18},{10... | collective-permute-start | bytes 983048 | tf_op jit(solution)/shard_map/ppermute | solution.py:25
  42.1 1.5 %collective-permute-start.19 = (bf16[48,512]{1,0:T(8,128)(2,1)S(1)}, bf16[48,512]{1,0:T(8,128)(2,1)S(1)}, u32[]{:S(2)}, u32[]{:S(2)}) collective-permute-start(bf16[48,512]{1,0:T(8,128)(2,1)S(1)} %get-tuple-element.55.refs_0_), channel_id=1, source_target_pairs={{0,8},{8,0},{16,24},{24,16},{1,9},{9,1},{17,25},{25,17},{2,10},{10... | collective-permute-start | bytes 147464 | tf_op jit(solution)/shard_map/ppermute | solution.py:25
  43.6 2.5 %collective-permute-start.20 = (bf16[48,512]{1,0:T(8,128)(2,1)S(1)}, bf16[48,512]{1,0:T(8,128)(2,1)S(1)}, u32[]{:S(2)}, u32[]{:S(2)}) collective-permute-start(bf16[48,512]{1,0:T(8,128)(2,1)S(1)} %get-tuple-element.55.refs_0_), channel_id=1, source_target_pairs={{0,24},{8,16},{16,8},{24,0},{1,25},{9,17},{17,9},{25,1},{2,26},{10... | collective-permute-start | bytes 147464 | tf_op jit(solution)/shard_map/ppermute | solution.py:25
  46.1 14.7 %collective-permute-done.18.refs_2_.src = bf16[48,512]{1,0:T(8,128)(2,1)S(1)} collective-permute-done((bf16[48,512]{1,0:T(8,128)(2,1)S(1)}, bf16[48,512]{1,0:T(8,128)(2,1)S(1)}, u32[]{:S(2)}, u32[]{:S(2)}) %collective-permute-start.18) | collective-permute-done | bytes 49184 | tf_op jit(solution)/shard_map/ppermute | solution.py:25
  60.9 1.5 %collective-permute-start.22 = (bf16[96,512]{1,0:T(8,128)(2,1)S(1)}, bf16[96,512]{1,0:T(8,128)(2,1)S(1)}, u32[]{:S(2)}, u32[]{:S(2)}) collective-permute-start(bf16[96,512]{1,0:T(8,128)(2,1)S(1)} %shard_map.101.refs_0_), channel_id=1, source_target_pairs={{0,2},{1,3},{2,0},{3,1},{4,6},{5,7},{6,4},{7,5},{8,10},{9,11},{10,... | collective-permute-start | bytes 294920 | tf_op jit(solution)/shard_map/ppermute | solution.py:25
  62.4 1.5 %collective-permute-start.24 = (bf16[96,512]{1,0:T(8,128)(2,1)S(1)}, bf16[96,512]{1,0:T(8,128)(2,1)S(1)}, u32[]{:S(2)}, u32[]{:S(2)}) collective-permute-start(bf16[96,512]{1,0:T(8,128)(2,1)S(1)} %shard_map.101.refs_0_), channel_id=1, source_target_pairs={{0,4},{1,5},{2,6},{3,7},{4,0},{5,1},{6,2},{7,3},{8,12},{9,13},{10,... | collective-permute-start | bytes 294920 | tf_op jit(solution)/shard_map/ppermute | solution.py:25
  64.4 1.6 %collective-permute-done.22.refs_2_ = bf16[96,512]{1,0:T(8,128)(2,1)S(1)} collective-permute-done((bf16[96,512]{1,0:T(8,128)(2,1)S(1)}, bf16[96,512]{1,0:T(8,128)(2,1)S(1)}, u32[]{:S(2)}, u32[]{:S(2)}) %collective-permute-start.22) | collective-permute-done | bytes 98336 | tf_op jit(solution)/shard_map/ppermute | solution.py:25
  66.1 2.0 %collective-permute-done.24.refs_4_ = bf16[96,512]{1,0:T(8,128)(2,1)S(1)} collective-permute-done((bf16[96,512]{1,0:T(8,128)(2,1)S(1)}, bf16[96,512]{1,0:T(8,128)(2,1)S(1)}, u32[]{:S(2)}, u32[]{:S(2)}) %collective-permute-start.24) | collective-permute-done | bytes 98336 | tf_op jit(solution)/shard_map/ppermute | solution.py:25
  68.0 1.4 %collective-permute-done.26.refs_6_ = bf16[96,512]{1,0:T(8,128)(2,1)S(1)} collective-permute-done((bf16[96,512]{1,0:T(8,128)(2,1)S(1)}, bf16[96,512]{1,0:T(8,128)(2,1)S(1)}, u32[]{:S(2)}, u32[]{:S(2)}) %collective-permute-start.26) | collective-permute-done | bytes 98336 | tf_op jit(solution)/shard_map/ppermute | solution.py:25
  69.4 1.6 %shard_map.100.merged = f32[640,512]{1,0:T(8,128)S(1)} custom-call(s32[1,3]{1,0:T(1,128)S(1)} %bitcast.7, s32[5,128]{1,0:T(8,128)S(1)} %get-tuple-element.38.code.refs_1_.code_ref, bf16[640,512]{1,0:T(8,128)(2,1)S(1)} %get-tuple-element.47.factor_ref, bf16[640,1024]{1,0:T(8,128)(2,1)S(1)} %copy-done, bf16[512,512]{1,0:T(8,128)(2,1)S(1)} %get-tuple-element.53.pivots_ref, ...), custom_call_target="tpu_custom_call" | custom-call | tf_op jit(solution)/shard_map/pallas_call | solution.py:40
  72.3 2.3 %shard_map.104 = bf16[640,512]{1,0:T(8,128)(2,1)} custom-call(s32[1,3]{1,0:T(1,128)S(1)} %bitcast.8, bf16[640,1024]{1,0:T(8,128)(2,1)S(1)} %copy-done.1, f32[640,512]{1,0:T(8,128)S(1)} %shard_map.100.merged, bf16[320,512]{1,0:T(8,128)(2,1)S(1)} %collective-permute-done.17.got, bf16[640,320]{1,0:T(8,128)(2,1)S(1)} %shard_map.102.land, ...), custom_call_target="tpu_custom_call" | custom-call | tf_op jit(solution)/shard_map/pallas_call | solution.py:40
  (58 shorter events, 9.6 us)
Async XLA Ops:
  1.1 5.4 %collective-permute-start.1 = (bf16[64,512]{1,0:T(8,128)(2,1)S(1)}, bf16[64,512]{1,0:T(8,128)(2,1)S(1)}, u32[]{:S(2)}, u32[]{:S(2)}) collective-permute-start(bf16[64,512]{1,0:T(8,128)(2,1)S(1)} %get-tuple-element.36.refs_0_), channel_id=1, source_target_pairs={{0,2},{1,3},{2,0},{3,1},{4,6},{5,7},{6,4},{7,5},{8,10},{9,11},{10,... | collective-permute-start | bytes 196616 | tf_op jit(solution)/shard_map/ppermute | solution.py:25
  4.2 4.3 %collective-permute-start.3 = (bf16[64,512]{1,0:T(8,128)(2,1)S(1)}, bf16[64,512]{1,0:T(8,128)(2,1)S(1)}, u32[]{:S(2)}, u32[]{:S(2)}) collective-permute-start(bf16[64,512]{1,0:T(8,128)(2,1)S(1)} %get-tuple-element.36.refs_0_), channel_id=1, source_target_pairs={{0,4},{1,5},{2,6},{3,7},{4,0},{5,1},{6,2},{7,3},{8,12},{9,13},{10,... | collective-permute-start | bytes 196616 | tf_op jit(solution)/shard_map/ppermute | solution.py:25
  5.7 5.2 %collective-permute-start.5 = (bf16[64,512]{1,0:T(8,128)(2,1)S(1)}, bf16[64,512]{1,0:T(8,128)(2,1)S(1)}, u32[]{:S(2)}, u32[]{:S(2)}) collective-permute-start(bf16[64,512]{1,0:T(8,128)(2,1)S(1)} %get-tuple-element.36.refs_0_), channel_id=1, source_target_pairs={{0,6},{1,7},{2,4},{3,5},{4,2},{5,3},{6,0},{7,1},{8,14},{9,15},{10,... | collective-permute-start | bytes 196616 | tf_op jit(solution)/shard_map/ppermute | solution.py:25
  5.7 6.8 %collective-permute-start = (bf16[64,512]{1,0:T(8,128)(2,1)S(1)}, bf16[64,512]{1,0:T(8,128)(2,1)S(1)}, u32[]{:S(2)}, u32[]{:S(2)}) collective-permute-start(bf16[64,512]{1,0:T(8,128)(2,1)S(1)} %get-tuple-element.36.refs_0_), channel_id=1, source_target_pairs={{0,1},{1,0},{2,3},{3,2},{4,5},{5,4},{6,7},{7,6},{8,9},{9,8},{10,11... | collective-permute-start | bytes 196616 | tf_op jit(solution)/shard_map/ppermute | solution.py:25
  6.5 6.0 %collective-permute-start.2 = (bf16[64,512]{1,0:T(8,128)(2,1)S(1)}, bf16[64,512]{1,0:T(8,128)(2,1)S(1)}, u32[]{:S(2)}, u32[]{:S(2)}) collective-permute-start(bf16[64,512]{1,0:T(8,128)(2,1)S(1)} %collective-permute-done.1.refs_2_), channel_id=1, source_target_pairs={{0,1},{1,0},{2,3},{3,2},{4,5},{5,4},{6,7},{7,6},{8,9},{9,8},{10,11... | collective-permute-start | bytes 196616 | tf_op jit(solution)/shard_map/ppermute | solution.py:25
  8.4 4.1 %collective-permute-start.4 = (bf16[64,512]{1,0:T(8,128)(2,1)S(1)}, bf16[64,512]{1,0:T(8,128)(2,1)S(1)}, u32[]{:S(2)}, u32[]{:S(2)}) collective-permute-start(bf16[64,512]{1,0:T(8,128)(2,1)S(1)} %collective-permute-done.3.refs_4_), channel_id=1, source_target_pairs={{0,1},{1,0},{2,3},{3,2},{4,5},{5,4},{6,7},{7,6},{8,9},{9,8},{10,11... | collective-permute-start | bytes 196616 | tf_op jit(solution)/shard_map/ppermute | solution.py:25
  13.3 23.4 %collective-permute-start.7 = (bf16[320,512]{1,0:T(8,128)(2,1)S(1)}, bf16[320,512]{1,0:T(8,128)(2,1)S(1)}, u32[]{:S(2)}, u32[]{:S(2)}) collective-permute-start(bf16[320,512]{1,0:T(8,128)(2,1)S(1)} %get-tuple-element.42), channel_id=1, source_target_pairs={{0,8},{8,0},{16,24},{24,16},{1,9},{9,1},{17,25},{25,17},{2,10},{10... | collective-permute-start | bytes 983048 | tf_op jit(solution)/shard_map/ppermute | solution.py:25
  14.9 12.9 %collective-permute-start.8 = (bf16[176,512]{1,0:T(8,128)(2,1)S(1)}, bf16[176,512]{1,0:T(8,128)(2,1)S(1)}, u32[]{:S(2)}, u32[]{:S(2)}) collective-permute-start(bf16[176,512]{1,0:T(8,128)(2,1)S(1)} %get-tuple-element.43.mine), channel_id=1, source_target_pairs={{0,8},{8,0},{16,24},{24,16},{1,9},{9,1},{17,25},{25,17},{2,10},{10... | collective-permute-start | bytes 540680 | tf_op jit(solution)/shard_map/ppermute | solution.py:25
  15.4 13.3 %collective-permute-start.9 = (bf16[64,512]{1,0:T(8,128)(2,1)S(1)}, bf16[64,512]{1,0:T(8,128)(2,1)S(1)}, u32[]{:S(2)}, u32[]{:S(2)}) collective-permute-start(bf16[64,512]{1,0:T(8,128)(2,1)S(1)} %get-tuple-element.37.refs_1_), channel_id=1, source_target_pairs={{0,8},{8,0},{16,24},{24,16},{1,9},{9,1},{17,25},{25,17},{2,10},{10... | collective-permute-start | bytes 196616 | tf_op jit(solution)/shard_map/ppermute | solution.py:25
  28.8 4.9 %collective-permute-start.11 = (bf16[64,512]{1,0:T(8,128)(2,1)S(1)}, bf16[64,512]{1,0:T(8,128)(2,1)S(1)}, u32[]{:S(2)}, u32[]{:S(2)}) collective-permute-start(bf16[64,512]{1,0:T(8,128)(2,1)S(1)} %shard_map.98.refs_3_), channel_id=1, source_target_pairs={{0,2},{1,3},{2,0},{3,1},{4,6},{5,7},{6,4},{7,5},{8,10},{9,11},{10,... | collective-permute-start | bytes 196616 | tf_op jit(solution)/shard_map/ppermute | solution.py:25
  29.4 4.6 %collective-permute-start.13 = (bf16[64,512]{1,0:T(8,128)(2,1)S(1)}, bf16[64,512]{1,0:T(8,128)(2,1)S(1)}, u32[]{:S(2)}, u32[]{:S(2)}) collective-permute-start(bf16[64,512]{1,0:T(8,128)(2,1)S(1)} %shard_map.98.refs_3_), channel_id=1, source_target_pairs={{0,4},{1,5},{2,6},{3,7},{4,0},{5,1},{6,2},{7,3},{8,12},{9,13},{10,... | collective-permute-start | bytes 196616 | tf_op jit(solution)/shard_map/ppermute | solution.py:25
  29.9 5.2 %collective-permute-start.15 = (bf16[64,512]{1,0:T(8,128)(2,1)S(1)}, bf16[64,512]{1,0:T(8,128)(2,1)S(1)}, u32[]{:S(2)}, u32[]{:S(2)}) collective-permute-start(bf16[64,512]{1,0:T(8,128)(2,1)S(1)} %shard_map.98.refs_3_), channel_id=1, source_target_pairs={{0,6},{1,7},{2,4},{3,5},{4,2},{5,3},{6,0},{7,1},{8,14},{9,15},{10,... | collective-permute-start | bytes 196616 | tf_op jit(solution)/shard_map/ppermute | solution.py:25
  32.3 6.0 %collective-permute-start.10 = (bf16[64,512]{1,0:T(8,128)(2,1)S(1)}, bf16[64,512]{1,0:T(8,128)(2,1)S(1)}, u32[]{:S(2)}, u32[]{:S(2)}) collective-permute-start(bf16[64,512]{1,0:T(8,128)(2,1)S(1)} %shard_map.98.refs_3_), channel_id=1, source_target_pairs={{0,1},{1,0},{2,3},{3,2},{4,5},{5,4},{6,7},{7,6},{8,9},{9,8},{10,11... | collective-permute-start | bytes 196616 | tf_op jit(solution)/shard_map/ppermute | solution.py:25
  33.7 4.6 %collective-permute-start.12 = (bf16[64,512]{1,0:T(8,128)(2,1)S(1)}, bf16[64,512]{1,0:T(8,128)(2,1)S(1)}, u32[]{:S(2)}, u32[]{:S(2)}) collective-permute-start(bf16[64,512]{1,0:T(8,128)(2,1)S(1)} %collective-permute-done.11.refs_5_), channel_id=1, source_target_pairs={{0,1},{1,0},{2,3},{3,2},{4,5},{5,4},{6,7},{7,6},{8,9},{9,8},{10,11... | collective-permute-start | bytes 196616 | tf_op jit(solution)/shard_map/ppermute | solution.py:25
  34.0 4.4 %collective-permute-start.14 = (bf16[64,512]{1,0:T(8,128)(2,1)S(1)}, bf16[64,512]{1,0:T(8,128)(2,1)S(1)}, u32[]{:S(2)}, u32[]{:S(2)}) collective-permute-start(bf16[64,512]{1,0:T(8,128)(2,1)S(1)} %collective-permute-done.13.refs_7_), channel_id=1, source_target_pairs={{0,1},{1,0},{2,3},{3,2},{4,5},{5,4},{6,7},{7,6},{8,9},{9,8},{10,11... | collective-permute-start | bytes 196616 | tf_op jit(solution)/shard_map/ppermute | solution.py:25
  39.1 33.2 %collective-permute-start.17 = (bf16[320,512]{1,0:T(8,128)(2,1)S(1)}, bf16[320,512]{1,0:T(8,128)(2,1)S(1)}, u32[]{:S(2)}, u32[]{:S(2)}) collective-permute-start(bf16[320,512]{1,0:T(8,128)(2,1)S(1)} %get-tuple-element.54), channel_id=1, source_target_pairs={{0,16},{8,24},{16,0},{24,8},{1,17},{9,25},{17,1},{25,9},{2,18},{10... | collective-permute-start | bytes 983048 | tf_op jit(solution)/shard_map/ppermute | solution.py:25
  41.7 19.1 %collective-permute-start.18 = (bf16[48,512]{1,0:T(8,128)(2,1)S(1)}, bf16[48,512]{1,0:T(8,128)(2,1)S(1)}, u32[]{:S(2)}, u32[]{:S(2)}) collective-permute-start(bf16[48,512]{1,0:T(8,128)(2,1)S(1)} %get-tuple-element.55.refs_0_), channel_id=1, source_target_pairs={{0,16},{8,24},{16,0},{24,8},{1,17},{9,25},{17,1},{25,9},{2,18},{10... | collective-permute-start | bytes 147464 | tf_op jit(solution)/shard_map/ppermute | solution.py:25
  42.1 18.7 %collective-permute-start.19 = (bf16[48,512]{1,0:T(8,128)(2,1)S(1)}, bf16[48,512]{1,0:T(8,128)(2,1)S(1)}, u32[]{:S(2)}, u32[]{:S(2)}) collective-permute-start(bf16[48,512]{1,0:T(8,128)(2,1)S(1)} %get-tuple-element.55.refs_0_), channel_id=1, source_target_pairs={{0,8},{8,0},{16,24},{24,16},{1,9},{9,1},{17,25},{25,17},{2,10},{10... | collective-permute-start | bytes 147464 | tf_op jit(solution)/shard_map/ppermute | solution.py:25
  43.6 17.2 %collective-permute-start.20 = (bf16[48,512]{1,0:T(8,128)(2,1)S(1)}, bf16[48,512]{1,0:T(8,128)(2,1)S(1)}, u32[]{:S(2)}, u32[]{:S(2)}) collective-permute-start(bf16[48,512]{1,0:T(8,128)(2,1)S(1)} %get-tuple-element.55.refs_0_), channel_id=1, source_target_pairs={{0,24},{8,16},{16,8},{24,0},{1,25},{9,17},{17,9},{25,1},{2,26},{10... | collective-permute-start | bytes 147464 | tf_op jit(solution)/shard_map/ppermute | solution.py:25
  60.9 5.2 %collective-permute-start.22 = (bf16[96,512]{1,0:T(8,128)(2,1)S(1)}, bf16[96,512]{1,0:T(8,128)(2,1)S(1)}, u32[]{:S(2)}, u32[]{:S(2)}) collective-permute-start(bf16[96,512]{1,0:T(8,128)(2,1)S(1)} %shard_map.101.refs_0_), channel_id=1, source_target_pairs={{0,2},{1,3},{2,0},{3,1},{4,6},{5,7},{6,4},{7,5},{8,10},{9,11},{10,... | collective-permute-start | bytes 294920 | tf_op jit(solution)/shard_map/ppermute | solution.py:25
  62.4 5.7 %collective-permute-start.24 = (bf16[96,512]{1,0:T(8,128)(2,1)S(1)}, bf16[96,512]{1,0:T(8,128)(2,1)S(1)}, u32[]{:S(2)}, u32[]{:S(2)}) collective-permute-start(bf16[96,512]{1,0:T(8,128)(2,1)S(1)} %shard_map.101.refs_0_), channel_id=1, source_target_pairs={{0,4},{1,5},{2,6},{3,7},{4,0},{5,1},{6,2},{7,3},{8,12},{9,13},{10,... | collective-permute-start | bytes 294920 | tf_op jit(solution)/shard_map/ppermute | solution.py:25
  63.9 5.5 %collective-permute-start.26 = (bf16[96,512]{1,0:T(8,128)(2,1)S(1)}, bf16[96,512]{1,0:T(8,128)(2,1)S(1)}, u32[]{:S(2)}, u32[]{:S(2)}) collective-permute-start(bf16[96,512]{1,0:T(8,128)(2,1)S(1)} %shard_map.101.refs_0_), channel_id=1, source_target_pairs={{0,6},{1,7},{2,4},{3,5},{4,2},{5,3},{6,0},{7,1},{8,14},{9,15},{10,... | collective-permute-start | bytes 294920 | tf_op jit(solution)/shard_map/ppermute | solution.py:25
  64.4 7.5 %collective-permute-start.21 = (bf16[96,512]{1,0:T(8,128)(2,1)S(1)}, bf16[96,512]{1,0:T(8,128)(2,1)S(1)}, u32[]{:S(2)}, u32[]{:S(2)}) collective-permute-start(bf16[96,512]{1,0:T(8,128)(2,1)S(1)} %shard_map.101.refs_0_), channel_id=1, source_target_pairs={{0,1},{1,0},{2,3},{3,2},{4,5},{5,4},{6,7},{7,6},{8,9},{9,8},{10,11... | collective-permute-start | bytes 294920 | tf_op jit(solution)/shard_map/ppermute | solution.py:25
  66.1 5.8 %collective-permute-start.23 = (bf16[96,512]{1,0:T(8,128)(2,1)S(1)}, bf16[96,512]{1,0:T(8,128)(2,1)S(1)}, u32[]{:S(2)}, u32[]{:S(2)}) collective-permute-start(bf16[96,512]{1,0:T(8,128)(2,1)S(1)} %collective-permute-done.22.refs_2_), channel_id=1, source_target_pairs={{0,1},{1,0},{2,3},{3,2},{4,5},{5,4},{6,7},{7,6},{8,9},{9,8},{10,11... | collective-permute-start | bytes 294920 | tf_op jit(solution)/shard_map/ppermute | solution.py:25
  (10 other events, 82.7 us)

commit v4 on v3

--- a/solution.py
+++ b/solution.py
@@ -12,7 +12,6 @@
 NT = (((1,), (1,)), ((), ()))
 NN = (((1,), (0,)), ((), ()))
 VM = pl.BlockSpec(memory_space=pltpu.VMEM)
-SM = pl.BlockSpec(memory_space=pltpu.SMEM)
 VP = pl.BlockSpec(memory_space=pltpu.VMEM)
 AN = pl.BlockSpec(memory_space=pltpu.HBM)
 
@@ -210,13 +209,13 @@
         return [((2 * n[level] + half, cols), BF)] * 2
 
     def before0(live_ref, code, front, inverse, fs, cs, factor):
-        pick = row_picks(code_row(code), live_ref[0, 0], n[1])
-        factor[...] = factor_of(front[:, :panel], inverse[...], live_ref[0, 0])
+        pick = row_picks(code_row(code), live_ref[0:1, 0:0 + 1], n[1])
+        factor[...] = factor_of(front[:, :panel], inverse[...], live_ref[0:1, 0:0 + 1])
         cs[...] = dot(pick, front[:, panel:], NN).astype(BF)
         fs[...] = dot(pick, factor[...], NN).astype(BF)
 
     fs0, cs0, factor0 = call(
-        before0, [SM, VM, VP, VP], sent(1) + [((rows, panel), BF)],
+        before0, [VM, VM, VP, VP], sent(1) + [((rows, panel), BF)],
     )(live, code0, front_leaf, dinv_leaf)
     blocks0 = collect(block0, got0)
 
@@ -252,10 +251,10 @@
     def own(level, code, factor, front, pivots, parent):
         def body(live_ref, code_ref, factor_ref, front_ref, pivots_ref, parent_ref, out):
             update = (front_ref[:, panel:].astype(F32) - dot(factor_ref[...], pivots_ref[...], NT)).astype(BF)
-            pick = own_pick(code_row(code_ref), live_ref[0, level])
+            pick = own_pick(code_row(code_ref), live_ref[0:1, level:level + 1])
             out[...] = parent_ref[:, :cols].astype(F32) + dot(pick, update, NN)
 
-        return call(body, [SM, VM, VM, VP, VM, VP], [((rows, cols), F32)])(
+        return call(body, [VM, VM, VM, VP, VM, VP], [((rows, cols), F32)])(
             live, code, factor, front, pivots, parent)[0]
 
     pivots0, pivot0, bulk0 = after(0, fs0, cs0, dinv_leaf, blocks0)
@@ -280,12 +279,12 @@
     )(near, later(near_1, pivot0))
 
     def early1(live_ref, code, front, pick_out, cs):
-        pick = row_picks(code_row(code), live_ref[0, 1], n[2])
+        pick = row_picks(code_row(code), live_ref[0:1, 1:1 + 1], n[2])
         pick_out[...] = pick
         cs[...] = dot(pick, front[:, panel:], NN).astype(BF)
 
     pick1, cs1 = call(
-        early1, [SM, VM, VP], [((2 * n[2] + half, rows), BF)] + sent(2)[:1],
+        early1, [VM, VM, VP], [((2 * n[2] + half, rows), BF)] + sent(2)[:1],
     )(live, later(code1, pivot0), front_mid)
 
     def raised(count, flip, headed, extra):
@@ -329,11 +328,11 @@
 
     def before1(live_ref, pick, merged, got, land, inverse, fs, factor):
         assembled = (merged[...] + dot(land[...], got[...], NN)).astype(BF)
-        factor[...] = factor_of(assembled, inverse[...], live_ref[0, 1])
+        factor[...] = factor_of(assembled, inverse[...], live_ref[0:1, 1:1 + 1])
         fs[...] = dot(pick[...], factor[...], NN).astype(BF)
 
     fs1, factor1 = call(
-        before1, [SM] + [VM] * 5, sent(2)[:1] + [((rows, panel), BF)],
+        before1, [VM] * 6, sent(2)[:1] + [((rows, panel), BF)],
     )(live, pick1, merged0, bulk0_other, land0, inv_mid)
     blocks1 = collect(raw1, spread1)
     pivots1, pivot1, bulk1 = after(
@@ -386,8 +385,8 @@
 
     def level2(live_ref, front, merged, got, land, inverse, pivots, out, ov, sems):
         assembled = (merged[...] + dot(land[...], got[...], NN)).astype(BF)
-        factor = factor_of(assembled, inverse[...], live_ref[0, 2])
-        mask = lax.broadcasted_iota(I32, (rows, 1), 0) < live_ref[0, 2]
+        factor = factor_of(assembled, inverse[...], live_ref[0:1, 2:2 + 1])
+        mask = lax.broadcasted_iota(I32, (rows, 1), 0) < live_ref[0:1, 2:2 + 1]
         writes = []
         for i in range(steps):
             at = slice(i * part, (i + 1) * part)
@@ -398,7 +397,7 @@
             write.wait()
 
     out, = call(
-        level2, [SM, VP] + [VM] * 5, [((rows, cols), BF)],
+        level2, [VM, VP] + [VM] * 5, [((rows, cols), BF)],
         scratch=[pltpu.VMEM((rows, cols), BF), pltpu.SemaphoreType.DMA((steps,))],
         out_specs=[AN],
     )(live, front_top, merged1, bulk1_other, land1, inv_top, pivots2)

time: 74.8 us -> 72.1 us (0.964)
  Pallas kernels: 14.6 us -> 11.3 us
    pallas_call x14, Pallas kernels: 14.6 us -> 11.3 us  [run(): made(*[pltpu.with_memory_space_constraint(a, pltpu.HBM) if spec is AN els...]
  transfers between devices with their start and end apart: 28 -> 28, of which waited for: 11 -> 11; matrix products, arithmetic and copies ran while one was open for 0% -> 0% of each run, Pallas kernels for 13% -> 10%
where the time goes in v4:
time: 72.1 us; the launch traced here: 72 us
  waiting for transfers between devices  37.4 us (52%)
  starting transfers between devices  22.9 us (32%)
  Pallas kernels  11.3 us (16%)
    ppermute x28, waiting for transfers between devices, swap(): lax.ppermute(value, axis, [(i, i ^ mask) for i in range(lax.axis_size(axi...  37.4 us
    ppermute x28, starting transfers between devices, swap(): lax.ppermute(value, axis, [(i, i ^ mask) for i in range(lax.axis_size(axi...  22.9 us
    pallas_call x14, Pallas kernels, run(): made(*[pltpu.with_memory_space_constraint(a, pltpu.HBM) if spec is AN els...  11.3 us
  transfers between devices with their start and end apart: 28, of which 11 were waited for; matrix products, arithmetic and copies ran while one was open for 0% of the time, Pallas kernels for 10%

profile of v4, /device:TPU:0, one launch (start us, length us, event | category | flops | bytes accessed | tf_op | source)
XLA Modules:
  0.0 72.0 jit_solution(8270243798154792382)
XLA Ops:
  0.0 1.1 %shard_map.91 = (bf16[176,512]{1,0:T(8,128)(2,1)S(1)}, s32[5,128]{1,0:T(8,128)S(1)}, s32[5,128]{1,0:T(8,128)S(1)}, bf16[64,512]{1,0:T(8,128)(2,1)S(1)}, bf16[16,512]{1,0:T(8,128)(2,1)S(1)}) custom-call(s32[5,128]{1,0:T(8,128)} %bitcast.9, s32[5,128]{1,0:T(8,128)} %bitcast.10, bf16[256,256]{1,0:T(8,128)(2,1)} %mid.1, bf16[640,1024]{1,0:T(8,128)(2,1)} %front_ref.3, ...), custom_call_target="tpu_custom_call" | custom-call | tf_op jit(solution)/shard_map/pallas_call | solution.py:39
  1.1 3.0 %collective-permute-start.1 = (bf16[64,512]{1,0:T(8,128)(2,1)S(1)}, bf16[64,512]{1,0:T(8,128)(2,1)S(1)}, u32[]{:S(2)}, u32[]{:S(2)}) collective-permute-start(bf16[64,512]{1,0:T(8,128)(2,1)S(1)} %get-tuple-element.36.refs_0_), channel_id=1, source_target_pairs={{0,2},{1,3},{2,0},{3,1},{4,6},{5,7},{6,4},{7,5},{8,10},{9,11},{10,... | collective-permute-start | bytes 196616 | tf_op jit(solution)/shard_map/ppermute | solution.py:24
  4.2 1.5 %collective-permute-start.3 = (bf16[64,512]{1,0:T(8,128)(2,1)S(1)}, bf16[64,512]{1,0:T(8,128)(2,1)S(1)}, u32[]{:S(2)}, u32[]{:S(2)}) collective-permute-start(bf16[64,512]{1,0:T(8,128)(2,1)S(1)} %get-tuple-element.36.refs_0_), channel_id=1, source_target_pairs={{0,4},{1,5},{2,6},{3,7},{4,0},{5,1},{6,2},{7,3},{8,12},{9,13},{10,... | collective-permute-start | bytes 196616 | tf_op jit(solution)/shard_map/ppermute | solution.py:24
  6.5 1.9 %collective-permute-done.3.refs_4_ = bf16[64,512]{1,0:T(8,128)(2,1)S(1)} collective-permute-done((bf16[64,512]{1,0:T(8,128)(2,1)S(1)}, bf16[64,512]{1,0:T(8,128)(2,1)S(1)}, u32[]{:S(2)}, u32[]{:S(2)}) %collective-permute-start.3) | collective-permute-done | bytes 65568 | tf_op jit(solution)/shard_map/ppermute | solution.py:24
  8.4 2.4 %collective-permute-done.5.refs_6_ = bf16[64,512]{1,0:T(8,128)(2,1)S(1)} collective-permute-done((bf16[64,512]{1,0:T(8,128)(2,1)S(1)}, bf16[64,512]{1,0:T(8,128)(2,1)S(1)}, u32[]{:S(2)}, u32[]{:S(2)}) %collective-permute-start.5) | collective-permute-done | bytes 65568 | tf_op jit(solution)/shard_map/ppermute | solution.py:24
  10.9 1.1 %shard_map.92 = (bf16[384,512]{1,0:T(8,128)(2,1)S(1)}, bf16[384,512]{1,0:T(8,128)(2,1)S(1)}, bf16[640,512]{1,0:T(8,128)(2,1)S(1)}) custom-call(s32[1,3]{1,0:T(1,128)S(1)} %bitcast.3, s32[5,128]{1,0:T(8,128)S(1)} %get-tuple-element.33.code.code_ref, bf16[640,1024]{1,0:T(8,128)(2,1)S(1)} %copy-done.2, bf16[512,256]{1,0:T(8,128)(2,1)S(1)} %copy-done.3), custom_call_target="tpu_custom_call" | custom-call | tf_op jit(solution)/shard_map/pallas_call | solution.py:39
  12.8 1.6 %collective-permute-start.7 = (bf16[320,512]{1,0:T(8,128)(2,1)S(1)}, bf16[320,512]{1,0:T(8,128)(2,1)S(1)}, u32[]{:S(2)}, u32[]{:S(2)}) collective-permute-start(bf16[320,512]{1,0:T(8,128)(2,1)S(1)} %get-tuple-element.42), channel_id=1, source_target_pairs={{0,8},{8,0},{16,24},{24,16},{1,9},{9,1},{17,25},{25,17},{2,10},{10... | collective-permute-start | bytes 983048 | tf_op jit(solution)/shard_map/ppermute | solution.py:24
  14.9 1.6 %collective-permute-start.9 = (bf16[64,512]{1,0:T(8,128)(2,1)S(1)}, bf16[64,512]{1,0:T(8,128)(2,1)S(1)}, u32[]{:S(2)}, u32[]{:S(2)}) collective-permute-start(bf16[64,512]{1,0:T(8,128)(2,1)S(1)} %get-tuple-element.37.refs_1_), channel_id=1, source_target_pairs={{0,8},{8,0},{16,24},{24,16},{1,9},{9,1},{17,25},{25,17},{2,10},{10... | collective-permute-start | bytes 196616 | tf_op jit(solution)/shard_map/ppermute | solution.py:24
  17.2 10.2 %collective-permute-done.8.near_ref = bf16[176,512]{1,0:T(8,128)(2,1)S(1)} collective-permute-done((bf16[176,512]{1,0:T(8,128)(2,1)S(1)}, bf16[176,512]{1,0:T(8,128)(2,1)S(1)}, u32[]{:S(2)}, u32[]{:S(2)}) %collective-permute-start.8) | collective-permute-done | bytes 180256 | tf_op jit(solution)/shard_map/ppermute | solution.py:24
  29.4 2.4 %collective-permute-start.15 = (bf16[64,512]{1,0:T(8,128)(2,1)S(1)}, bf16[64,512]{1,0:T(8,128)(2,1)S(1)}, u32[]{:S(2)}, u32[]{:S(2)}) collective-permute-start(bf16[64,512]{1,0:T(8,128)(2,1)S(1)} %shard_map.98.refs_3_), channel_id=1, source_target_pairs={{0,6},{1,7},{2,4},{3,5},{4,2},{5,3},{6,0},{7,1},{8,14},{9,15},{10,... | collective-permute-start | bytes 196616 | tf_op jit(solution)/shard_map/ppermute | solution.py:24
  31.8 1.4 %collective-permute-done.11.refs_5_ = bf16[64,512]{1,0:T(8,128)(2,1)S(1)} collective-permute-done((bf16[64,512]{1,0:T(8,128)(2,1)S(1)}, bf16[64,512]{1,0:T(8,128)(2,1)S(1)}, u32[]{:S(2)}, u32[]{:S(2)}) %collective-permute-start.11) | collective-permute-done | bytes 65568 | tf_op jit(solution)/shard_map/ppermute | solution.py:24
  34.6 1.1 %shard_map.95.merged = f32[640,512]{1,0:T(8,128)S(1)} custom-call(s32[1,3]{1,0:T(1,128)S(1)} %bitcast.5, s32[5,128]{1,0:T(8,128)S(1)} %get-tuple-element.33.code.code_ref, bf16[640,512]{1,0:T(8,128)(2,1)S(1)} %get-tuple-element.40.factor_ref, bf16[640,1024]{1,0:T(8,128)(2,1)S(1)} %copy-done.2, bf16[512,512]{1,0:T(8,128)(2,1)S(1)} %get-tuple-element.41.pivots_ref, ...), custom_call_target="tpu_custom_call" | custom-call | tf_op jit(solution)/shard_map/pallas_call | solution.py:39
  35.7 1.0 %shard_map.97 = (bf16[352,512]{1,0:T(8,128)(2,1)S(1)}, bf16[640,512]{1,0:T(8,128)(2,1)S(1)}) custom-call(s32[1,3]{1,0:T(1,128)S(1)} %bitcast.6, bf16[352,640]{1,0:T(8,128)(2,1)S(1)} %get-tuple-element.39.pick, f32[640,512]{1,0:T(8,128)S(1)} %shard_map.95.merged, bf16[320,512]{1,0:T(8,128)(2,1)S(1)} %collective-permute-done.7.got, ...), custom_call_target="tpu_custom_call" | custom-call | tf_op jit(solution)/shard_map/pallas_call | solution.py:39
  37.5 2.6 %collective-permute-start.17 = (bf16[320,512]{1,0:T(8,128)(2,1)S(1)}, bf16[320,512]{1,0:T(8,128)(2,1)S(1)}, u32[]{:S(2)}, u32[]{:S(2)}) collective-permute-start(bf16[320,512]{1,0:T(8,128)(2,1)S(1)} %get-tuple-element.54), channel_id=1, source_target_pairs={{0,16},{8,24},{16,0},{24,8},{1,17},{9,25},{17,1},{25,9},{2,18},{10... | collective-permute-start | bytes 983048 | tf_op jit(solution)/shard_map/ppermute | solution.py:24
  40.5 1.6 %collective-permute-start.19 = (bf16[48,512]{1,0:T(8,128)(2,1)S(1)}, bf16[48,512]{1,0:T(8,128)(2,1)S(1)}, u32[]{:S(2)}, u32[]{:S(2)}) collective-permute-start(bf16[48,512]{1,0:T(8,128)(2,1)S(1)} %get-tuple-element.55.refs_0_), channel_id=1, source_target_pairs={{0,8},{8,0},{16,24},{24,16},{1,9},{9,1},{17,25},{25,17},{2,10},{10... | collective-permute-start | bytes 147464 | tf_op jit(solution)/shard_map/ppermute | solution.py:24
  42.0 2.5 %collective-permute-start.20 = (bf16[48,512]{1,0:T(8,128)(2,1)S(1)}, bf16[48,512]{1,0:T(8,128)(2,1)S(1)}, u32[]{:S(2)}, u32[]{:S(2)}) collective-permute-start(bf16[48,512]{1,0:T(8,128)(2,1)S(1)} %get-tuple-element.55.refs_0_), channel_id=1, source_target_pairs={{0,24},{8,16},{16,8},{24,0},{1,25},{9,17},{17,9},{25,1},{2,26},{10... | collective-permute-start | bytes 147464 | tf_op jit(solution)/shard_map/ppermute | solution.py:24
  44.5 14.7 %collective-permute-done.18.refs_2_.src = bf16[48,512]{1,0:T(8,128)(2,1)S(1)} collective-permute-done((bf16[48,512]{1,0:T(8,128)(2,1)S(1)}, bf16[48,512]{1,0:T(8,128)(2,1)S(1)}, u32[]{:S(2)}, u32[]{:S(2)}) %collective-permute-start.18) | collective-permute-done | bytes 49184 | tf_op jit(solution)/shard_map/ppermute | solution.py:24
  59.2 1.6 %collective-permute-start.22 = (bf16[96,512]{1,0:T(8,128)(2,1)S(1)}, bf16[96,512]{1,0:T(8,128)(2,1)S(1)}, u32[]{:S(2)}, u32[]{:S(2)}) collective-permute-start(bf16[96,512]{1,0:T(8,128)(2,1)S(1)} %shard_map.101.refs_0_), channel_id=1, source_target_pairs={{0,2},{1,3},{2,0},{3,1},{4,6},{5,7},{6,4},{7,5},{8,10},{9,11},{10,... | collective-permute-start | bytes 294920 | tf_op jit(solution)/shard_map/ppermute | solution.py:24
  60.8 1.5 %collective-permute-start.24 = (bf16[96,512]{1,0:T(8,128)(2,1)S(1)}, bf16[96,512]{1,0:T(8,128)(2,1)S(1)}, u32[]{:S(2)}, u32[]{:S(2)}) collective-permute-start(bf16[96,512]{1,0:T(8,128)(2,1)S(1)} %shard_map.101.refs_0_), channel_id=1, source_target_pairs={{0,4},{1,5},{2,6},{3,7},{4,0},{5,1},{6,2},{7,3},{8,12},{9,13},{10,... | collective-permute-start | bytes 294920 | tf_op jit(solution)/shard_map/ppermute | solution.py:24
  62.8 1.6 %collective-permute-done.22.refs_2_ = bf16[96,512]{1,0:T(8,128)(2,1)S(1)} collective-permute-done((bf16[96,512]{1,0:T(8,128)(2,1)S(1)}, bf16[96,512]{1,0:T(8,128)(2,1)S(1)}, u32[]{:S(2)}, u32[]{:S(2)}) %collective-permute-start.22) | collective-permute-done | bytes 98336 | tf_op jit(solution)/shard_map/ppermute | solution.py:24
  64.4 2.1 %collective-permute-done.24.refs_4_ = bf16[96,512]{1,0:T(8,128)(2,1)S(1)} collective-permute-done((bf16[96,512]{1,0:T(8,128)(2,1)S(1)}, bf16[96,512]{1,0:T(8,128)(2,1)S(1)}, u32[]{:S(2)}, u32[]{:S(2)}) %collective-permute-start.24) | collective-permute-done | bytes 98336 | tf_op jit(solution)/shard_map/ppermute | solution.py:24
  66.5 1.4 %collective-permute-done.26.refs_6_ = bf16[96,512]{1,0:T(8,128)(2,1)S(1)} collective-permute-done((bf16[96,512]{1,0:T(8,128)(2,1)S(1)}, bf16[96,512]{1,0:T(8,128)(2,1)S(1)}, u32[]{:S(2)}, u32[]{:S(2)}) %collective-permute-start.26) | collective-permute-done | bytes 98336 | tf_op jit(solution)/shard_map/ppermute | solution.py:24
  67.8 1.1 %shard_map.100.merged = f32[640,512]{1,0:T(8,128)S(1)} custom-call(s32[1,3]{1,0:T(1,128)S(1)} %bitcast.7, s32[5,128]{1,0:T(8,128)S(1)} %get-tuple-element.38.code.refs_1_.code_ref, bf16[640,512]{1,0:T(8,128)(2,1)S(1)} %get-tuple-element.47.factor_ref, bf16[640,1024]{1,0:T(8,128)(2,1)S(1)} %copy-done, bf16[512,512]{1,0:T(8,128)(2,1)S(1)} %get-tuple-element.53.pivots_ref, ...), custom_call_target="tpu_custom_call" | custom-call | tf_op jit(solution)/shard_map/pallas_call | solution.py:39
  70.2 1.8 %shard_map.104 = bf16[640,512]{1,0:T(8,128)(2,1)} custom-call(s32[1,3]{1,0:T(1,128)S(1)} %bitcast.8, bf16[640,1024]{1,0:T(8,128)(2,1)S(1)} %copy-done.1, f32[640,512]{1,0:T(8,128)S(1)} %shard_map.100.merged, bf16[320,512]{1,0:T(8,128)(2,1)S(1)} %collective-permute-done.17.got, bf16[640,320]{1,0:T(8,128)(2,1)S(1)} %shard_map.102.land, ...), custom_call_target="tpu_custom_call" | custom-call | tf_op jit(solution)/shard_map/pallas_call | solution.py:39
  (58 shorter events, 9.0 us)
Async XLA Ops:
  1.1 5.4 %collective-permute-start.1 = (bf16[64,512]{1,0:T(8,128)(2,1)S(1)}, bf16[64,512]{1,0:T(8,128)(2,1)S(1)}, u32[]{:S(2)}, u32[]{:S(2)}) collective-permute-start(bf16[64,512]{1,0:T(8,128)(2,1)S(1)} %get-tuple-element.36.refs_0_), channel_id=1, source_target_pairs={{0,2},{1,3},{2,0},{3,1},{4,6},{5,7},{6,4},{7,5},{8,10},{9,11},{10,... | collective-permute-start | bytes 196616 | tf_op jit(solution)/shard_map/ppermute | solution.py:24
  4.2 4.3 %collective-permute-start.3 = (bf16[64,512]{1,0:T(8,128)(2,1)S(1)}, bf16[64,512]{1,0:T(8,128)(2,1)S(1)}, u32[]{:S(2)}, u32[]{:S(2)}) collective-permute-start(bf16[64,512]{1,0:T(8,128)(2,1)S(1)} %get-tuple-element.36.refs_0_), channel_id=1, source_target_pairs={{0,4},{1,5},{2,6},{3,7},{4,0},{5,1},{6,2},{7,3},{8,12},{9,13},{10,... | collective-permute-start | bytes 196616 | tf_op jit(solution)/shard_map/ppermute | solution.py:24
  5.7 5.2 %collective-permute-start.5 = (bf16[64,512]{1,0:T(8,128)(2,1)S(1)}, bf16[64,512]{1,0:T(8,128)(2,1)S(1)}, u32[]{:S(2)}, u32[]{:S(2)}) collective-permute-start(bf16[64,512]{1,0:T(8,128)(2,1)S(1)} %get-tuple-element.36.refs_0_), channel_id=1, source_target_pairs={{0,6},{1,7},{2,4},{3,5},{4,2},{5,3},{6,0},{7,1},{8,14},{9,15},{10,... | collective-permute-start | bytes 196616 | tf_op jit(solution)/shard_map/ppermute | solution.py:24
  5.7 6.3 %collective-permute-start = (bf16[64,512]{1,0:T(8,128)(2,1)S(1)}, bf16[64,512]{1,0:T(8,128)(2,1)S(1)}, u32[]{:S(2)}, u32[]{:S(2)}) collective-permute-start(bf16[64,512]{1,0:T(8,128)(2,1)S(1)} %get-tuple-element.36.refs_0_), channel_id=1, source_target_pairs={{0,1},{1,0},{2,3},{3,2},{4,5},{5,4},{6,7},{7,6},{8,9},{9,8},{10,11... | collective-permute-start | bytes 196616 | tf_op jit(solution)/shard_map/ppermute | solution.py:24
  6.5 5.5 %collective-permute-start.2 = (bf16[64,512]{1,0:T(8,128)(2,1)S(1)}, bf16[64,512]{1,0:T(8,128)(2,1)S(1)}, u32[]{:S(2)}, u32[]{:S(2)}) collective-permute-start(bf16[64,512]{1,0:T(8,128)(2,1)S(1)} %collective-permute-done.1.refs_2_), channel_id=1, source_target_pairs={{0,1},{1,0},{2,3},{3,2},{4,5},{5,4},{6,7},{7,6},{8,9},{9,8},{10,11... | collective-permute-start | bytes 196616 | tf_op jit(solution)/shard_map/ppermute | solution.py:24
  8.4 3.6 %collective-permute-start.4 = (bf16[64,512]{1,0:T(8,128)(2,1)S(1)}, bf16[64,512]{1,0:T(8,128)(2,1)S(1)}, u32[]{:S(2)}, u32[]{:S(2)}) collective-permute-start(bf16[64,512]{1,0:T(8,128)(2,1)S(1)} %collective-permute-done.3.refs_4_), channel_id=1, source_target_pairs={{0,1},{1,0},{2,3},{3,2},{4,5},{5,4},{6,7},{7,6},{8,9},{9,8},{10,11... | collective-permute-start | bytes 196616 | tf_op jit(solution)/shard_map/ppermute | solution.py:24
  12.8 22.8 %collective-permute-start.7 = (bf16[320,512]{1,0:T(8,128)(2,1)S(1)}, bf16[320,512]{1,0:T(8,128)(2,1)S(1)}, u32[]{:S(2)}, u32[]{:S(2)}) collective-permute-start(bf16[320,512]{1,0:T(8,128)(2,1)S(1)} %get-tuple-element.42), channel_id=1, source_target_pairs={{0,8},{8,0},{16,24},{24,16},{1,9},{9,1},{17,25},{25,17},{2,10},{10... | collective-permute-start | bytes 983048 | tf_op jit(solution)/shard_map/ppermute | solution.py:24
  14.5 12.9 %collective-permute-start.8 = (bf16[176,512]{1,0:T(8,128)(2,1)S(1)}, bf16[176,512]{1,0:T(8,128)(2,1)S(1)}, u32[]{:S(2)}, u32[]{:S(2)}) collective-permute-start(bf16[176,512]{1,0:T(8,128)(2,1)S(1)} %get-tuple-element.43.mine), channel_id=1, source_target_pairs={{0,8},{8,0},{16,24},{24,16},{1,9},{9,1},{17,25},{25,17},{2,10},{10... | collective-permute-start | bytes 540680 | tf_op jit(solution)/shard_map/ppermute | solution.py:24
  14.9 13.3 %collective-permute-start.9 = (bf16[64,512]{1,0:T(8,128)(2,1)S(1)}, bf16[64,512]{1,0:T(8,128)(2,1)S(1)}, u32[]{:S(2)}, u32[]{:S(2)}) collective-permute-start(bf16[64,512]{1,0:T(8,128)(2,1)S(1)} %get-tuple-element.37.refs_1_), channel_id=1, source_target_pairs={{0,8},{8,0},{16,24},{24,16},{1,9},{9,1},{17,25},{25,17},{2,10},{10... | collective-permute-start | bytes 196616 | tf_op jit(solution)/shard_map/ppermute | solution.py:24
  28.3 5.0 %collective-permute-start.11 = (bf16[64,512]{1,0:T(8,128)(2,1)S(1)}, bf16[64,512]{1,0:T(8,128)(2,1)S(1)}, u32[]{:S(2)}, u32[]{:S(2)}) collective-permute-start(bf16[64,512]{1,0:T(8,128)(2,1)S(1)} %shard_map.98.refs_3_), channel_id=1, source_target_pairs={{0,2},{1,3},{2,0},{3,1},{4,6},{5,7},{6,4},{7,5},{8,10},{9,11},{10,... | collective-permute-start | bytes 196616 | tf_op jit(solution)/shard_map/ppermute | solution.py:24
  28.9 4.4 %collective-permute-start.13 = (bf16[64,512]{1,0:T(8,128)(2,1)S(1)}, bf16[64,512]{1,0:T(8,128)(2,1)S(1)}, u32[]{:S(2)}, u32[]{:S(2)}) collective-permute-start(bf16[64,512]{1,0:T(8,128)(2,1)S(1)} %shard_map.98.refs_3_), channel_id=1, source_target_pairs={{0,4},{1,5},{2,6},{3,7},{4,0},{5,1},{6,2},{7,3},{8,12},{9,13},{10,... | collective-permute-start | bytes 196616 | tf_op jit(solution)/shard_map/ppermute | solution.py:24
  29.4 5.2 %collective-permute-start.15 = (bf16[64,512]{1,0:T(8,128)(2,1)S(1)}, bf16[64,512]{1,0:T(8,128)(2,1)S(1)}, u32[]{:S(2)}, u32[]{:S(2)}) collective-permute-start(bf16[64,512]{1,0:T(8,128)(2,1)S(1)} %shard_map.98.refs_3_), channel_id=1, source_target_pairs={{0,6},{1,7},{2,4},{3,5},{4,2},{5,3},{6,0},{7,1},{8,14},{9,15},{10,... | collective-permute-start | bytes 196616 | tf_op jit(solution)/shard_map/ppermute | solution.py:24
  31.8 4.8 %collective-permute-start.10 = (bf16[64,512]{1,0:T(8,128)(2,1)S(1)}, bf16[64,512]{1,0:T(8,128)(2,1)S(1)}, u32[]{:S(2)}, u32[]{:S(2)}) collective-permute-start(bf16[64,512]{1,0:T(8,128)(2,1)S(1)} %shard_map.98.refs_3_), channel_id=1, source_target_pairs={{0,1},{1,0},{2,3},{3,2},{4,5},{5,4},{6,7},{7,6},{8,9},{9,8},{10,11... | collective-permute-start | bytes 196616 | tf_op jit(solution)/shard_map/ppermute | solution.py:24
  33.3 3.4 %collective-permute-start.12 = (bf16[64,512]{1,0:T(8,128)(2,1)S(1)}, bf16[64,512]{1,0:T(8,128)(2,1)S(1)}, u32[]{:S(2)}, u32[]{:S(2)}) collective-permute-start(bf16[64,512]{1,0:T(8,128)(2,1)S(1)} %collective-permute-done.11.refs_5_), channel_id=1, source_target_pairs={{0,1},{1,0},{2,3},{3,2},{4,5},{5,4},{6,7},{7,6},{8,9},{9,8},{10,11... | collective-permute-start | bytes 196616 | tf_op jit(solution)/shard_map/ppermute | solution.py:24
  33.3 3.4 %collective-permute-start.14 = (bf16[64,512]{1,0:T(8,128)(2,1)S(1)}, bf16[64,512]{1,0:T(8,128)(2,1)S(1)}, u32[]{:S(2)}, u32[]{:S(2)}) collective-permute-start(bf16[64,512]{1,0:T(8,128)(2,1)S(1)} %collective-permute-done.13.refs_7_), channel_id=1, source_target_pairs={{0,1},{1,0},{2,3},{3,2},{4,5},{5,4},{6,7},{7,6},{8,9},{9,8},{10,11... | collective-permute-start | bytes 196616 | tf_op jit(solution)/shard_map/ppermute | solution.py:24
  37.5 32.7 %collective-permute-start.17 = (bf16[320,512]{1,0:T(8,128)(2,1)S(1)}, bf16[320,512]{1,0:T(8,128)(2,1)S(1)}, u32[]{:S(2)}, u32[]{:S(2)}) collective-permute-start(bf16[320,512]{1,0:T(8,128)(2,1)S(1)} %get-tuple-element.54), channel_id=1, source_target_pairs={{0,16},{8,24},{16,0},{24,8},{1,17},{9,25},{17,1},{25,9},{2,18},{10... | collective-permute-start | bytes 983048 | tf_op jit(solution)/shard_map/ppermute | solution.py:24
  40.1 19.1 %collective-permute-start.18 = (bf16[48,512]{1,0:T(8,128)(2,1)S(1)}, bf16[48,512]{1,0:T(8,128)(2,1)S(1)}, u32[]{:S(2)}, u32[]{:S(2)}) collective-permute-start(bf16[48,512]{1,0:T(8,128)(2,1)S(1)} %get-tuple-element.55.refs_0_), channel_id=1, source_target_pairs={{0,16},{8,24},{16,0},{24,8},{1,17},{9,25},{17,1},{25,9},{2,18},{10... | collective-permute-start | bytes 147464 | tf_op jit(solution)/shard_map/ppermute | solution.py:24
  40.5 18.7 %collective-permute-start.19 = (bf16[48,512]{1,0:T(8,128)(2,1)S(1)}, bf16[48,512]{1,0:T(8,128)(2,1)S(1)}, u32[]{:S(2)}, u32[]{:S(2)}) collective-permute-start(bf16[48,512]{1,0:T(8,128)(2,1)S(1)} %get-tuple-element.55.refs_0_), channel_id=1, source_target_pairs={{0,8},{8,0},{16,24},{24,16},{1,9},{9,1},{17,25},{25,17},{2,10},{10... | collective-permute-start | bytes 147464 | tf_op jit(solution)/shard_map/ppermute | solution.py:24
  42.0 17.2 %collective-permute-start.20 = (bf16[48,512]{1,0:T(8,128)(2,1)S(1)}, bf16[48,512]{1,0:T(8,128)(2,1)S(1)}, u32[]{:S(2)}, u32[]{:S(2)}) collective-permute-start(bf16[48,512]{1,0:T(8,128)(2,1)S(1)} %get-tuple-element.55.refs_0_), channel_id=1, source_target_pairs={{0,24},{8,16},{16,8},{24,0},{1,25},{9,17},{17,9},{25,1},{2,26},{10... | collective-permute-start | bytes 147464 | tf_op jit(solution)/shard_map/ppermute | solution.py:24
  59.2 5.1 %collective-permute-start.22 = (bf16[96,512]{1,0:T(8,128)(2,1)S(1)}, bf16[96,512]{1,0:T(8,128)(2,1)S(1)}, u32[]{:S(2)}, u32[]{:S(2)}) collective-permute-start(bf16[96,512]{1,0:T(8,128)(2,1)S(1)} %shard_map.101.refs_0_), channel_id=1, source_target_pairs={{0,2},{1,3},{2,0},{3,1},{4,6},{5,7},{6,4},{7,5},{8,10},{9,11},{10,... | collective-permute-start | bytes 294920 | tf_op jit(solution)/shard_map/ppermute | solution.py:24
  60.8 5.7 %collective-permute-start.24 = (bf16[96,512]{1,0:T(8,128)(2,1)S(1)}, bf16[96,512]{1,0:T(8,128)(2,1)S(1)}, u32[]{:S(2)}, u32[]{:S(2)}) collective-permute-start(bf16[96,512]{1,0:T(8,128)(2,1)S(1)} %shard_map.101.refs_0_), channel_id=1, source_target_pairs={{0,4},{1,5},{2,6},{3,7},{4,0},{5,1},{6,2},{7,3},{8,12},{9,13},{10,... | collective-permute-start | bytes 294920 | tf_op jit(solution)/shard_map/ppermute | solution.py:24
  62.3 5.5 %collective-permute-start.26 = (bf16[96,512]{1,0:T(8,128)(2,1)S(1)}, bf16[96,512]{1,0:T(8,128)(2,1)S(1)}, u32[]{:S(2)}, u32[]{:S(2)}) collective-permute-start(bf16[96,512]{1,0:T(8,128)(2,1)S(1)} %shard_map.101.refs_0_), channel_id=1, source_target_pairs={{0,6},{1,7},{2,4},{3,5},{4,2},{5,3},{6,0},{7,1},{8,14},{9,15},{10,... | collective-permute-start | bytes 294920 | tf_op jit(solution)/shard_map/ppermute | solution.py:24
  62.8 7.0 %collective-permute-start.21 = (bf16[96,512]{1,0:T(8,128)(2,1)S(1)}, bf16[96,512]{1,0:T(8,128)(2,1)S(1)}, u32[]{:S(2)}, u32[]{:S(2)}) collective-permute-start(bf16[96,512]{1,0:T(8,128)(2,1)S(1)} %shard_map.101.refs_0_), channel_id=1, source_target_pairs={{0,1},{1,0},{2,3},{3,2},{4,5},{5,4},{6,7},{7,6},{8,9},{9,8},{10,11... | collective-permute-start | bytes 294920 | tf_op jit(solution)/shard_map/ppermute | solution.py:24
  64.4 5.4 %collective-permute-start.23 = (bf16[96,512]{1,0:T(8,128)(2,1)S(1)}, bf16[96,512]{1,0:T(8,128)(2,1)S(1)}, u32[]{:S(2)}, u32[]{:S(2)}) collective-permute-start(bf16[96,512]{1,0:T(8,128)(2,1)S(1)} %collective-permute-done.22.refs_2_), channel_id=1, source_target_pairs={{0,1},{1,0},{2,3},{3,2},{4,5},{5,4},{6,7},{7,6},{8,9},{9,8},{10,11... | collective-permute-start | bytes 294920 | tf_op jit(solution)/shard_map/ppermute | solution.py:24
  (10 other events, 79.1 us)

commit v5 on v4

--- a/solution.py
+++ b/solution.py
@@ -219,12 +219,13 @@
     )(live, code0, front_leaf, dinv_leaf)
     blocks0 = collect(block0, got0)
 
-    def chain(middle, count, headed, extra):
+    def chain(middle, count, headed, extra, parts):
         def body(fs, cs, inverse, *refs):
             refs = list(refs)
             head = refs.pop(0) if headed else None
             code_ref, top = (refs.pop(0), refs.pop(0)) if extra else (None, None)
-            blocks, (pivots, out, bulk) = refs[:-3], refs[-3:]
+            bulks = refs[-parts:]
+            blocks, (pivots, out) = refs[:-2 - parts], refs[-2 - parts:-parts]
             pivots_from([ref[...] for ref in blocks], inverse[...], pivots, middle, inner)
             update = (cs[...].astype(F32) - dot(fs[...], pivots[...], NT)).astype(BF)
             out[:count] = (update[:count].astype(F32) + head[...].astype(F32)).astype(BF) if headed else update[:count]
@@ -236,16 +237,17 @@
                 code = jnp.concatenate([code_ref[...], jnp.zeros((share - rows // lanes, lanes), I32)], 0)
                 out[tail, block:block + lanes] = (code >> 8).astype(F32).astype(BF)
                 out[tail, block + lanes:] = (code & 255).astype(F32).astype(BF)
-            bulk[...] = update[2 * count:]
+            for i, bulk in enumerate(bulks):
+                bulk[...] = update[2 * count:, i * (cols // parts):(i + 1) * (cols // parts)]
 
         return body
 
-    def after(level, fs, cs, inverse, blocks, head=(), extra=()):
+    def after(level, fs, cs, inverse, blocks, parts, head=(), extra=()):
         count = n[level + 1]
         return call(
-            chain(1 << level, count, bool(head), bool(extra)),
+            chain(1 << level, count, bool(head), bool(extra), parts),
             [VM] * (3 + len(head) + len(extra) + len(blocks)),
-            [((cols, panel), BF), ((2 * count + (share if extra else 0), cols), BF), ((half, cols), BF)],
+            [((cols, panel), BF), ((2 * count + (share if extra else 0), cols), BF)] + [((half, cols // parts), BF)] * parts,
         )(fs, cs, inverse, *head, *extra, *blocks)
 
     def own(level, code, factor, front, pivots, parent):
@@ -257,7 +259,7 @@
         return call(body, [VM, VM, VM, VP, VM, VP], [((rows, cols), F32)])(
             live, code, factor, front, pivots, parent)[0]
 
-    pivots0, pivot0, bulk0 = after(0, fs0, cs0, dinv_leaf, blocks0)
+    pivots0, pivot0, bulk0 = after(0, fs0, cs0, dinv_leaf, blocks0, 1)
     pivot0_other = swap(pivot0, "sub", 1)
     bulk0_other = swap(bulk0, "sub", 1)
 
@@ -335,10 +337,10 @@
         before1, [VM] * 6, sent(2)[:1] + [((rows, panel), BF)],
     )(live, pick1, merged0, bulk0_other, land0, inv_mid)
     blocks1 = collect(raw1, spread1)
-    pivots1, pivot1, bulk1 = after(
-        1, fs1, cs1, inv_mid, blocks1, (top_head,), (code1, dinv_top) if shared else ())
+    pivots1, pivot1, *bulk1 = after(
+        1, fs1, cs1, inv_mid, blocks1, panel // block, (top_head,), (code1, dinv_top) if shared else ())
     others = [pivot1] + [swap(pivot1, "sub", m) for m in (1, 2, 3)]
-    bulk1_other = swap(bulk1, "sub", 2)
+    bulk1_other = [swap(part, "sub", 2) for part in bulk1]
     raw2, = call(raised(n[2], 2, 0, shared), [VM] * 4, [((4 * n[2] + (2 * share if shared else 0), panel), BF)])(*others)
     spread2 = spread(raw2)
     merged1 = own(1, code1, factor1, front_mid, pivots1, front_top)
@@ -380,28 +382,41 @@
                 sub & bit == 0, jnp.concatenate([inv_top, other], 0), jnp.concatenate([other, inv_top], 0))
         pivots2, = call(last_pivots, [VM] * (1 + len(blocks2)), [((cols, panel), BF)])(inv_top, *blocks2)
 
+    def level2_part(i, first, last):
+        lane = slice(i * block, (i + 1) * block)
+
+        def body(live_ref, merged, got, land, inverse, pivots, so_far, out, *scratch):
+            assembled = (merged[:, lane] + dot(land[...], got[...], NN)).astype(BF)
+            factor = factor_of(assembled, inverse[lane], live_ref[0:1, 2:3])
+            if not last:
+                out[...] = (so_far[:, panel:].astype(F32) if first else so_far[...]) - dot(factor, pivots[:, lane], NT)
+                return
+            ov, sems = scratch
+            mask = lax.broadcasted_iota(I32, (rows, 1), 0) < live_ref[0:1, 2:3]
+            writes = []
+            for k in range(steps):
+                at = slice(k * part, (k + 1) * part)
+                start = so_far[at, panel:].astype(F32) if first else so_far[at]
+                ov[at] = jnp.where(mask[at], start - dot(factor[at], pivots[:, lane], NT), 0.0).astype(BF)
+                writes += copies(sems.at[k:k + 1], [(ov.at[at], out.at[at])])
+            for write in writes:
+                write.wait()
+
+        return body
+
     steps = 2 if rows % 32 == 0 else 1
     part = rows // steps
-
-    def level2(live_ref, front, merged, got, land, inverse, pivots, out, ov, sems):
-        assembled = (merged[...] + dot(land[...], got[...], NN)).astype(BF)
-        factor = factor_of(assembled, inverse[...], live_ref[0:1, 2:2 + 1])
-        mask = lax.broadcasted_iota(I32, (rows, 1), 0) < live_ref[0:1, 2:2 + 1]
-        writes = []
-        for i in range(steps):
-            at = slice(i * part, (i + 1) * part)
-            product = dot(factor[at], pivots[...], NT)
-            ov[at] = jnp.where(mask[at], front[at, panel:].astype(F32) - product, 0.0).astype(BF)
-            writes += copies(sems.at[i:i + 1], [(ov.at[at], out.at[at])])
-        for write in writes:
-            write.wait()
-
-    out, = call(
-        level2, [VM, VP] + [VM] * 5, [((rows, cols), BF)],
-        scratch=[pltpu.VMEM((rows, cols), BF), pltpu.SemaphoreType.DMA((steps,))],
-        out_specs=[AN],
-    )(live, front_top, merged1, bulk1_other, land1, inv_top, pivots2)
-    return out
+    count = panel // block
+    result = front_top
+    for i in range(count):
+        last = i == count - 1
+        result, = call(
+            level2_part(i, i == 0, last), [VM] * 6 + [VP if i == 0 else VM],
+            [((rows, cols), BF if last else F32)],
+            scratch=[pltpu.VMEM((rows, cols), BF), pltpu.SemaphoreType.DMA((steps,))] if last else (),
+            out_specs=[AN] if last else None,
+        )(live, merged1, bulk1_other[i], land1, inv_top, pivots2, result)
+    return result
 
 
 def solution(mesh):

time: 72.1 us -> 69.6 us (0.965)
  waiting for transfers between devices: 37.4 us -> 34.2 us
    ppermute x28 -> x29, waiting for transfers between devices: 37.4 us -> 34.2 us  [swap(): lax.ppermute(value, axis, [(i, i ^ mask) for i in range(lax.axis_size(axi...]
    pallas_call x14 -> x15, Pallas kernels: 11.3 us -> 12 us  [run(): made(*[pltpu.with_memory_space_constraint(a, pltpu.HBM) if spec is AN els...]
    ppermute x28 -> x29, starting transfers between devices: 22.9 us -> 23 us  [swap(): lax.ppermute(value, axis, [(i, i ^ mask) for i in range(lax.axis_size(axi...]
  transfers between devices with their start and end apart: 28 -> 29, of which waited for: 11 -> 13; matrix products, arithmetic and copies ran while one was open for 0% -> 0% of each run, Pallas kernels for 10% -> 11%
where the time goes in v5:
time: 69.6 us; the launch traced here: 69.4 us
  waiting for transfers between devices  34.2 us (49%)
  starting transfers between devices  23 us (33%)
  Pallas kernels  12 us (17%)
    ppermute x29, waiting for transfers between devices, swap(): lax.ppermute(value, axis, [(i, i ^ mask) for i in range(lax.axis_size(axi...  34.2 us
    ppermute x29, starting transfers between devices, swap(): lax.ppermute(value, axis, [(i, i ^ mask) for i in range(lax.axis_size(axi...  23 us
    pallas_call x15, Pallas kernels, run(): made(*[pltpu.with_memory_space_constraint(a, pltpu.HBM) if spec is AN els...  12 us
  transfers between devices with their start and end apart: 29, of which 13 were waited for; matrix products, arithmetic and copies ran while one was open for 0% of the time, Pallas kernels for 11%

profile of v5, /device:TPU:0, one launch (start us, length us, event | category | flops | bytes accessed | tf_op | source)
XLA Modules:
  0.0 69.4 jit_solution(11436701325041436381)
XLA Ops:
  0.0 1.1 %shard_map.91 = (bf16[176,512]{1,0:T(8,128)(2,1)S(1)}, s32[5,128]{1,0:T(8,128)S(1)}, s32[5,128]{1,0:T(8,128)S(1)}, bf16[64,512]{1,0:T(8,128)(2,1)S(1)}, bf16[16,512]{1,0:T(8,128)(2,1)S(1)}) custom-call(s32[5,128]{1,0:T(8,128)} %bitcast.10, s32[5,128]{1,0:T(8,128)} %bitcast.11, bf16[256,256]{1,0:T(8,128)(2,1)} %mid.1, bf16[640,1024]{1,0:T(8,128)(2,1)} %front_ref.3, ...), custom_call_target="tpu_custom_call" | custom-call | tf_op jit(solution)/shard_map/pallas_call | solution.py:39
  1.1 4.0 %collective-permute-start.5 = (bf16[64,512]{1,0:T(8,128)(2,1)S(1)}, bf16[64,512]{1,0:T(8,128)(2,1)S(1)}, u32[]{:S(2)}, u32[]{:S(2)}) collective-permute-start(bf16[64,512]{1,0:T(8,128)(2,1)S(1)} %get-tuple-element.37.refs_0_), channel_id=1, source_target_pairs={{0,6},{1,7},{2,4},{3,5},{4,2},{5,3},{6,0},{7,1},{8,14},{9,15},{10,... | collective-permute-start | bytes 196616 | tf_op jit(solution)/shard_map/ppermute | solution.py:24
  5.8 1.6 %collective-permute-done.5.refs_6_ = bf16[64,512]{1,0:T(8,128)(2,1)S(1)} collective-permute-done((bf16[64,512]{1,0:T(8,128)(2,1)S(1)}, bf16[64,512]{1,0:T(8,128)(2,1)S(1)}, u32[]{:S(2)}, u32[]{:S(2)}) %collective-permute-start.5) | collective-permute-done | bytes 65568 | tf_op jit(solution)/shard_map/ppermute | solution.py:24
  7.4 2.0 %collective-permute-done.3.refs_4_ = bf16[64,512]{1,0:T(8,128)(2,1)S(1)} collective-permute-done((bf16[64,512]{1,0:T(8,128)(2,1)S(1)}, bf16[64,512]{1,0:T(8,128)(2,1)S(1)}, u32[]{:S(2)}, u32[]{:S(2)}) %collective-permute-start.3) | collective-permute-done | bytes 65568 | tf_op jit(solution)/shard_map/ppermute | solution.py:24
  9.9 1.1 %shard_map.92 = (bf16[384,512]{1,0:T(8,128)(2,1)S(1)}, bf16[384,512]{1,0:T(8,128)(2,1)S(1)}, bf16[640,512]{1,0:T(8,128)(2,1)S(1)}) custom-call(s32[1,3]{1,0:T(1,128)S(1)} %bitcast.3, s32[5,128]{1,0:T(8,128)S(1)} %get-tuple-element.34.code.code_ref, bf16[640,1024]{1,0:T(8,128)(2,1)S(1)} %copy-done.1, bf16[512,256]{1,0:T(8,128)(2,1)S(1)} %copy-done.3), custom_call_target="tpu_custom_call" | custom-call | tf_op jit(solution)/shard_map/pallas_call | solution.py:39
  11.9 1.6 %collective-permute-start.7 = (bf16[320,512]{1,0:T(8,128)(2,1)S(1)}, bf16[320,512]{1,0:T(8,128)(2,1)S(1)}, u32[]{:S(2)}, u32[]{:S(2)}) collective-permute-start(bf16[320,512]{1,0:T(8,128)(2,1)S(1)} %get-tuple-element.43), channel_id=1, source_target_pairs={{0,8},{8,0},{16,24},{24,16},{1,9},{9,1},{17,25},{25,17},{2,10},{10... | collective-permute-start | bytes 983048 | tf_op jit(solution)/shard_map/ppermute | solution.py:24
  14.0 1.6 %collective-permute-start.9 = (bf16[64,512]{1,0:T(8,128)(2,1)S(1)}, bf16[64,512]{1,0:T(8,128)(2,1)S(1)}, u32[]{:S(2)}, u32[]{:S(2)}) collective-permute-start(bf16[64,512]{1,0:T(8,128)(2,1)S(1)} %get-tuple-element.38.refs_1_), channel_id=1, source_target_pairs={{0,8},{8,0},{16,24},{24,16},{1,9},{9,1},{17,25},{25,17},{2,10},{10... | collective-permute-start | bytes 196616 | tf_op jit(solution)/shard_map/ppermute | solution.py:24
  16.2 10.2 %collective-permute-done.8.near_ref = bf16[176,512]{1,0:T(8,128)(2,1)S(1)} collective-permute-done((bf16[176,512]{1,0:T(8,128)(2,1)S(1)}, bf16[176,512]{1,0:T(8,128)(2,1)S(1)}, u32[]{:S(2)}, u32[]{:S(2)}) %collective-permute-start.8) | collective-permute-done | bytes 180256 | tf_op jit(solution)/shard_map/ppermute | solution.py:24
  27.3 1.6 %collective-permute-start.15 = (bf16[64,512]{1,0:T(8,128)(2,1)S(1)}, bf16[64,512]{1,0:T(8,128)(2,1)S(1)}, u32[]{:S(2)}, u32[]{:S(2)}) collective-permute-start(bf16[64,512]{1,0:T(8,128)(2,1)S(1)} %shard_map.98.refs_3_), channel_id=1, source_target_pairs={{0,6},{1,7},{2,4},{3,5},{4,2},{5,3},{6,0},{7,1},{8,14},{9,15},{10,... | collective-permute-start | bytes 196616 | tf_op jit(solution)/shard_map/ppermute | solution.py:24
  29.5 1.4 %collective-permute-start.11 = (bf16[64,512]{1,0:T(8,128)(2,1)S(1)}, bf16[64,512]{1,0:T(8,128)(2,1)S(1)}, u32[]{:S(2)}, u32[]{:S(2)}) collective-permute-start(bf16[64,512]{1,0:T(8,128)(2,1)S(1)} %shard_map.98.refs_3_), channel_id=1, source_target_pairs={{0,2},{1,3},{2,0},{3,1},{4,6},{5,7},{6,4},{7,5},{8,10},{9,11},{10,... | collective-permute-start | bytes 196616 | tf_op jit(solution)/shard_map/ppermute | solution.py:24
  30.9 2.4 %collective-permute-done.15.refs_9_ = bf16[64,512]{1,0:T(8,128)(2,1)S(1)} collective-permute-done((bf16[64,512]{1,0:T(8,128)(2,1)S(1)}, bf16[64,512]{1,0:T(8,128)(2,1)S(1)}, u32[]{:S(2)}, u32[]{:S(2)}) %collective-permute-start.15) | collective-permute-done | bytes 65568 | tf_op jit(solution)/shard_map/ppermute | solution.py:24
  34.1 1.1 %shard_map.95.merged = f32[640,512]{1,0:T(8,128)S(1)} custom-call(s32[1,3]{1,0:T(1,128)S(1)} %bitcast.5, s32[5,128]{1,0:T(8,128)S(1)} %get-tuple-element.34.code.code_ref, bf16[640,512]{1,0:T(8,128)(2,1)S(1)} %get-tuple-element.41.factor_ref, bf16[640,1024]{1,0:T(8,128)(2,1)S(1)} %copy-done.1, bf16[512,512]{1,0:T(8,128)(2,1)S(1)} %get-tuple-element.42.pivots_ref, ...), custom_call_target="tpu_custom_call" | custom-call | tf_op jit(solution)/shard_map/pallas_call | solution.py:39
  35.2 1.0 %shard_map.97 = (bf16[352,512]{1,0:T(8,128)(2,1)S(1)}, bf16[640,512]{1,0:T(8,128)(2,1)S(1)}) custom-call(s32[1,3]{1,0:T(1,128)S(1)} %bitcast.6, bf16[352,640]{1,0:T(8,128)(2,1)S(1)} %get-tuple-element.40.pick, f32[640,512]{1,0:T(8,128)S(1)} %shard_map.95.merged, bf16[320,512]{1,0:T(8,128)(2,1)S(1)} %collective-permute-done.7.got, ...), custom_call_target="tpu_custom_call" | custom-call | tf_op jit(solution)/shard_map/pallas_call | solution.py:39
  37.0 3.7 %collective-permute-start.20 = (bf16[48,512]{1,0:T(8,128)(2,1)S(1)}, bf16[48,512]{1,0:T(8,128)(2,1)S(1)}, u32[]{:S(2)}, u32[]{:S(2)}) collective-permute-start(bf16[48,512]{1,0:T(8,128)(2,1)S(1)} %get-tuple-element.56.refs_0_), channel_id=1, source_target_pairs={{0,24},{8,16},{16,8},{24,0},{1,25},{9,17},{17,9},{25,1},{2,26},{10... | collective-permute-start | bytes 147464 | tf_op jit(solution)/shard_map/ppermute | solution.py:24
  41.4 1.9 %collective-permute-done.20.refs_3_ = bf16[48,512]{1,0:T(8,128)(2,1)S(1)} collective-permute-done((bf16[48,512]{1,0:T(8,128)(2,1)S(1)}, bf16[48,512]{1,0:T(8,128)(2,1)S(1)}, u32[]{:S(2)}, u32[]{:S(2)}) %collective-permute-start.20) | collective-permute-done | bytes 49184 | tf_op jit(solution)/shard_map/ppermute | solution.py:24
  43.3 2.1 %collective-permute-done.19.refs_1_ = bf16[48,512]{1,0:T(8,128)(2,1)S(1)} collective-permute-done((bf16[48,512]{1,0:T(8,128)(2,1)S(1)}, bf16[48,512]{1,0:T(8,128)(2,1)S(1)}, u32[]{:S(2)}, u32[]{:S(2)}) %collective-permute-start.19) | collective-permute-done | bytes 49184 | tf_op jit(solution)/shard_map/ppermute | solution.py:24
  46.2 1.7 %collective-permute-start.26 = (bf16[96,512]{1,0:T(8,128)(2,1)S(1)}, bf16[96,512]{1,0:T(8,128)(2,1)S(1)}, u32[]{:S(2)}, u32[]{:S(2)}) collective-permute-start(bf16[96,512]{1,0:T(8,128)(2,1)S(1)} %shard_map.101.refs_0_), channel_id=1, source_target_pairs={{0,6},{1,7},{2,4},{3,5},{4,2},{5,3},{6,0},{7,1},{8,14},{9,15},{10,... | collective-permute-start | bytes 294920 | tf_op jit(solution)/shard_map/ppermute | solution.py:24
  48.4 1.3 %collective-permute-start.22 = (bf16[96,512]{1,0:T(8,128)(2,1)S(1)}, bf16[96,512]{1,0:T(8,128)(2,1)S(1)}, u32[]{:S(2)}, u32[]{:S(2)}) collective-permute-start(bf16[96,512]{1,0:T(8,128)(2,1)S(1)} %shard_map.101.refs_0_), channel_id=1, source_target_pairs={{0,2},{1,3},{2,0},{3,1},{4,6},{5,7},{6,4},{7,5},{8,10},{9,11},{10,... | collective-permute-start | bytes 294920 | tf_op jit(solution)/shard_map/ppermute | solution.py:24
  49.7 1.4 %collective-permute-start.28 = (bf16[320,256]{1,0:T(8,128)(2,1)S(1)}, bf16[320,256]{1,0:T(8,128)(2,1)S(1)}, u32[]{:S(2)}, u32[]{:S(2)}) collective-permute-start(bf16[320,256]{1,0:T(8,128)(2,1)S(1)} %get-tuple-element.60), channel_id=1, source_target_pairs={{0,16},{8,24},{16,0},{24,8},{1,17},{9,25},{17,1},{25,9},{2,18},{10... | collective-permute-start | bytes 491528 | tf_op jit(solution)/shard_map/ppermute | solution.py:24
  51.1 1.5 %collective-permute-done.26.refs_6_ = bf16[96,512]{1,0:T(8,128)(2,1)S(1)} collective-permute-done((bf16[96,512]{1,0:T(8,128)(2,1)S(1)}, bf16[96,512]{1,0:T(8,128)(2,1)S(1)}, u32[]{:S(2)}, u32[]{:S(2)}) %collective-permute-start.26) | collective-permute-done | bytes 98336 | tf_op jit(solution)/shard_map/ppermute | solution.py:24
  53.9 1.1 %shard_map.100.merged = f32[640,512]{1,0:T(8,128)S(1)} custom-call(s32[1,3]{1,0:T(1,128)S(1)} %bitcast.7, s32[5,128]{1,0:T(8,128)S(1)} %get-tuple-element.39.code.refs_1_.code_ref, bf16[640,512]{1,0:T(8,128)(2,1)S(1)} %get-tuple-element.48.factor_ref, bf16[640,1024]{1,0:T(8,128)(2,1)S(1)} %copy-done, bf16[512,512]{1,0:T(8,128)(2,1)S(1)} %get-tuple-element.54.pivots_ref, ...), custom_call_target="tpu_custom_call" | custom-call | tf_op jit(solution)/shard_map/pallas_call | solution.py:39
  56.2 8.5 %collective-permute-done.28.got = bf16[320,256]{1,0:T(8,128)(2,1)S(1)} collective-permute-done((bf16[320,256]{1,0:T(8,128)(2,1)S(1)}, bf16[320,256]{1,0:T(8,128)(2,1)S(1)}, u32[]{:S(2)}, u32[]{:S(2)}) %collective-permute-start.28) | collective-permute-done | bytes 163872 | tf_op jit(solution)/shard_map/ppermute | solution.py:24
  65.5 2.3 %collective-permute-done.17.got = bf16[320,256]{1,0:T(8,128)(2,1)S(1)} collective-permute-done((bf16[320,256]{1,0:T(8,128)(2,1)S(1)}, bf16[320,256]{1,0:T(8,128)(2,1)S(1)}, u32[]{:S(2)}, u32[]{:S(2)}) %collective-permute-start.17) | collective-permute-done | bytes 163872 | tf_op jit(solution)/shard_map/ppermute | solution.py:24
  67.8 1.6 %shard_map.105 = bf16[640,512]{1,0:T(8,128)(2,1)} custom-call(s32[1,3]{1,0:T(1,128)S(1)} %bitcast.9, f32[640,512]{1,0:T(8,128)S(1)} %shard_map.100.merged, bf16[320,256]{1,0:T(8,128)(2,1)S(1)} %collective-permute-done.17.got, bf16[640,320]{1,0:T(8,128)(2,1)S(1)} %shard_map.102.land, bf16[512,256]{1,0:T(8,128)(2,1)S(1)} %get-tuple-element.58.inverse, ...), custom_call_target="tpu_custom_call" | custom-call | tf_op jit(solution)/shard_map/pallas_call | solution.py:39
  (61 shorter events, 11.5 us)
Async XLA Ops:
  1.1 6.2 %collective-permute-start.5 = (bf16[64,512]{1,0:T(8,128)(2,1)S(1)}, bf16[64,512]{1,0:T(8,128)(2,1)S(1)}, u32[]{:S(2)}, u32[]{:S(2)}) collective-permute-start(bf16[64,512]{1,0:T(8,128)(2,1)S(1)} %get-tuple-element.37.refs_0_), channel_id=1, source_target_pairs={{0,6},{1,7},{2,4},{3,5},{4,2},{5,3},{6,0},{7,1},{8,14},{9,15},{10,... | collective-permute-start | bytes 196616 | tf_op jit(solution)/shard_map/ppermute | solution.py:24
  5.1 4.3 %collective-permute-start.3 = (bf16[64,512]{1,0:T(8,128)(2,1)S(1)}, bf16[64,512]{1,0:T(8,128)(2,1)S(1)}, u32[]{:S(2)}, u32[]{:S(2)}) collective-permute-start(bf16[64,512]{1,0:T(8,128)(2,1)S(1)} %get-tuple-element.37.refs_0_), channel_id=1, source_target_pairs={{0,4},{1,5},{2,6},{3,7},{4,0},{5,1},{6,2},{7,3},{8,12},{9,13},{10,... | collective-permute-start | bytes 196616 | tf_op jit(solution)/shard_map/ppermute | solution.py:24
  5.6 4.3 %collective-permute-start.1 = (bf16[64,512]{1,0:T(8,128)(2,1)S(1)}, bf16[64,512]{1,0:T(8,128)(2,1)S(1)}, u32[]{:S(2)}, u32[]{:S(2)}) collective-permute-start(bf16[64,512]{1,0:T(8,128)(2,1)S(1)} %get-tuple-element.37.refs_0_), channel_id=1, source_target_pairs={{0,2},{1,3},{2,0},{3,1},{4,6},{5,7},{6,4},{7,5},{8,10},{9,11},{10,... | collective-permute-start | bytes 196616 | tf_op jit(solution)/shard_map/ppermute | solution.py:24
  5.8 5.3 %collective-permute-start = (bf16[64,512]{1,0:T(8,128)(2,1)S(1)}, bf16[64,512]{1,0:T(8,128)(2,1)S(1)}, u32[]{:S(2)}, u32[]{:S(2)}) collective-permute-start(bf16[64,512]{1,0:T(8,128)(2,1)S(1)} %get-tuple-element.37.refs_0_), channel_id=1, source_target_pairs={{0,1},{1,0},{2,3},{3,2},{4,5},{5,4},{6,7},{7,6},{8,9},{9,8},{10,11... | collective-permute-start | bytes 196616 | tf_op jit(solution)/shard_map/ppermute | solution.py:24
  7.4 3.7 %collective-permute-start.6 = (bf16[64,512]{1,0:T(8,128)(2,1)S(1)}, bf16[64,512]{1,0:T(8,128)(2,1)S(1)}, u32[]{:S(2)}, u32[]{:S(2)}) collective-permute-start(bf16[64,512]{1,0:T(8,128)(2,1)S(1)} %collective-permute-done.5.refs_6_), channel_id=1, source_target_pairs={{0,1},{1,0},{2,3},{3,2},{4,5},{5,4},{6,7},{7,6},{8,9},{9,8},{10,11... | collective-permute-start | bytes 196616 | tf_op jit(solution)/shard_map/ppermute | solution.py:24
  11.9 23.3 %collective-permute-start.7 = (bf16[320,512]{1,0:T(8,128)(2,1)S(1)}, bf16[320,512]{1,0:T(8,128)(2,1)S(1)}, u32[]{:S(2)}, u32[]{:S(2)}) collective-permute-start(bf16[320,512]{1,0:T(8,128)(2,1)S(1)} %get-tuple-element.43), channel_id=1, source_target_pairs={{0,8},{8,0},{16,24},{24,16},{1,9},{9,1},{17,25},{25,17},{2,10},{10... | collective-permute-start | bytes 983048 | tf_op jit(solution)/shard_map/ppermute | solution.py:24
  13.5 12.9 %collective-permute-start.8 = (bf16[176,512]{1,0:T(8,128)(2,1)S(1)}, bf16[176,512]{1,0:T(8,128)(2,1)S(1)}, u32[]{:S(2)}, u32[]{:S(2)}) collective-permute-start(bf16[176,512]{1,0:T(8,128)(2,1)S(1)} %get-tuple-element.44.mine), channel_id=1, source_target_pairs={{0,8},{8,0},{16,24},{24,16},{1,9},{9,1},{17,25},{25,17},{2,10},{10... | collective-permute-start | bytes 540680 | tf_op jit(solution)/shard_map/ppermute | solution.py:24
  14.0 13.3 %collective-permute-start.9 = (bf16[64,512]{1,0:T(8,128)(2,1)S(1)}, bf16[64,512]{1,0:T(8,128)(2,1)S(1)}, u32[]{:S(2)}, u32[]{:S(2)}) collective-permute-start(bf16[64,512]{1,0:T(8,128)(2,1)S(1)} %get-tuple-element.38.refs_1_), channel_id=1, source_target_pairs={{0,8},{8,0},{16,24},{24,16},{1,9},{9,1},{17,25},{25,17},{2,10},{10... | collective-permute-start | bytes 196616 | tf_op jit(solution)/shard_map/ppermute | solution.py:24
  27.3 5.9 %collective-permute-start.15 = (bf16[64,512]{1,0:T(8,128)(2,1)S(1)}, bf16[64,512]{1,0:T(8,128)(2,1)S(1)}, u32[]{:S(2)}, u32[]{:S(2)}) collective-permute-start(bf16[64,512]{1,0:T(8,128)(2,1)S(1)} %shard_map.98.refs_3_), channel_id=1, source_target_pairs={{0,6},{1,7},{2,4},{3,5},{4,2},{5,3},{6,0},{7,1},{8,14},{9,15},{10,... | collective-permute-start | bytes 196616 | tf_op jit(solution)/shard_map/ppermute | solution.py:24
  28.9 4.7 %collective-permute-start.13 = (bf16[64,512]{1,0:T(8,128)(2,1)S(1)}, bf16[64,512]{1,0:T(8,128)(2,1)S(1)}, u32[]{:S(2)}, u32[]{:S(2)}) collective-permute-start(bf16[64,512]{1,0:T(8,128)(2,1)S(1)} %shard_map.98.refs_3_), channel_id=1, source_target_pairs={{0,4},{1,5},{2,6},{3,7},{4,0},{5,1},{6,2},{7,3},{8,12},{9,13},{10,... | collective-permute-start | bytes 196616 | tf_op jit(solution)/shard_map/ppermute | solution.py:24
  29.5 4.3 %collective-permute-start.11 = (bf16[64,512]{1,0:T(8,128)(2,1)S(1)}, bf16[64,512]{1,0:T(8,128)(2,1)S(1)}, u32[]{:S(2)}, u32[]{:S(2)}) collective-permute-start(bf16[64,512]{1,0:T(8,128)(2,1)S(1)} %shard_map.98.refs_3_), channel_id=1, source_target_pairs={{0,2},{1,3},{2,0},{3,1},{4,6},{5,7},{6,4},{7,5},{8,10},{9,11},{10,... | collective-permute-start | bytes 196616 | tf_op jit(solution)/shard_map/ppermute | solution.py:24
  30.9 5.3 %collective-permute-start.10 = (bf16[64,512]{1,0:T(8,128)(2,1)S(1)}, bf16[64,512]{1,0:T(8,128)(2,1)S(1)}, u32[]{:S(2)}, u32[]{:S(2)}) collective-permute-start(bf16[64,512]{1,0:T(8,128)(2,1)S(1)} %shard_map.98.refs_3_), channel_id=1, source_target_pairs={{0,1},{1,0},{2,3},{3,2},{4,5},{5,4},{6,7},{7,6},{8,9},{9,8},{10,11... | collective-permute-start | bytes 196616 | tf_op jit(solution)/shard_map/ppermute | solution.py:24
  33.2 2.9 %collective-permute-start.16 = (bf16[64,512]{1,0:T(8,128)(2,1)S(1)}, bf16[64,512]{1,0:T(8,128)(2,1)S(1)}, u32[]{:S(2)}, u32[]{:S(2)}) collective-permute-start(bf16[64,512]{1,0:T(8,128)(2,1)S(1)} %collective-permute-done.15.refs_9_), channel_id=1, source_target_pairs={{0,1},{1,0},{2,3},{3,2},{4,5},{5,4},{6,7},{7,6},{8,9},{9,8},{10,11... | collective-permute-start | bytes 196616 | tf_op jit(solution)/shard_map/ppermute | solution.py:24
  33.5 2.7 %collective-permute-start.14 = (bf16[64,512]{1,0:T(8,128)(2,1)S(1)}, bf16[64,512]{1,0:T(8,128)(2,1)S(1)}, u32[]{:S(2)}, u32[]{:S(2)}) collective-permute-start(bf16[64,512]{1,0:T(8,128)(2,1)S(1)} %collective-permute-done.13.refs_7_), channel_id=1, source_target_pairs={{0,1},{1,0},{2,3},{3,2},{4,5},{5,4},{6,7},{7,6},{8,9},{9,8},{10,11... | collective-permute-start | bytes 196616 | tf_op jit(solution)/shard_map/ppermute | solution.py:24
  37.0 6.4 %collective-permute-start.20 = (bf16[48,512]{1,0:T(8,128)(2,1)S(1)}, bf16[48,512]{1,0:T(8,128)(2,1)S(1)}, u32[]{:S(2)}, u32[]{:S(2)}) collective-permute-start(bf16[48,512]{1,0:T(8,128)(2,1)S(1)} %get-tuple-element.56.refs_0_), channel_id=1, source_target_pairs={{0,24},{8,16},{16,8},{24,0},{1,25},{9,17},{17,9},{25,1},{2,26},{10... | collective-permute-start | bytes 147464 | tf_op jit(solution)/shard_map/ppermute | solution.py:24
  40.6 4.8 %collective-permute-start.19 = (bf16[48,512]{1,0:T(8,128)(2,1)S(1)}, bf16[48,512]{1,0:T(8,128)(2,1)S(1)}, u32[]{:S(2)}, u32[]{:S(2)}) collective-permute-start(bf16[48,512]{1,0:T(8,128)(2,1)S(1)} %get-tuple-element.56.refs_0_), channel_id=1, source_target_pairs={{0,8},{8,0},{16,24},{24,16},{1,9},{9,1},{17,25},{25,17},{2,10},{10... | collective-permute-start | bytes 147464 | tf_op jit(solution)/shard_map/ppermute | solution.py:24
  40.6 5.5 %collective-permute-start.18 = (bf16[48,512]{1,0:T(8,128)(2,1)S(1)}, bf16[48,512]{1,0:T(8,128)(2,1)S(1)}, u32[]{:S(2)}, u32[]{:S(2)}) collective-permute-start(bf16[48,512]{1,0:T(8,128)(2,1)S(1)} %get-tuple-element.56.refs_0_), channel_id=1, source_target_pairs={{0,16},{8,24},{16,0},{24,8},{1,17},{9,25},{17,1},{25,9},{2,18},{10... | collective-permute-start | bytes 147464 | tf_op jit(solution)/shard_map/ppermute | solution.py:24
  46.2 6.5 %collective-permute-start.26 = (bf16[96,512]{1,0:T(8,128)(2,1)S(1)}, bf16[96,512]{1,0:T(8,128)(2,1)S(1)}, u32[]{:S(2)}, u32[]{:S(2)}) collective-permute-start(bf16[96,512]{1,0:T(8,128)(2,1)S(1)} %shard_map.101.refs_0_), channel_id=1, source_target_pairs={{0,6},{1,7},{2,4},{3,5},{4,2},{5,3},{6,0},{7,1},{8,14},{9,15},{10,... | collective-permute-start | bytes 294920 | tf_op jit(solution)/shard_map/ppermute | solution.py:24
  47.9 5.4 %collective-permute-start.24 = (bf16[96,512]{1,0:T(8,128)(2,1)S(1)}, bf16[96,512]{1,0:T(8,128)(2,1)S(1)}, u32[]{:S(2)}, u32[]{:S(2)}) collective-permute-start(bf16[96,512]{1,0:T(8,128)(2,1)S(1)} %shard_map.101.refs_0_), channel_id=1, source_target_pairs={{0,4},{1,5},{2,6},{3,7},{4,0},{5,1},{6,2},{7,3},{8,12},{9,13},{10,... | collective-permute-start | bytes 294920 | tf_op jit(solution)/shard_map/ppermute | solution.py:24
  48.4 4.9 %collective-permute-start.22 = (bf16[96,512]{1,0:T(8,128)(2,1)S(1)}, bf16[96,512]{1,0:T(8,128)(2,1)S(1)}, u32[]{:S(2)}, u32[]{:S(2)}) collective-permute-start(bf16[96,512]{1,0:T(8,128)(2,1)S(1)} %shard_map.101.refs_0_), channel_id=1, source_target_pairs={{0,2},{1,3},{2,0},{3,1},{4,6},{5,7},{6,4},{7,5},{8,10},{9,11},{10,... | collective-permute-start | bytes 294920 | tf_op jit(solution)/shard_map/ppermute | solution.py:24
  49.7 4.1 %collective-permute-start.21 = (bf16[96,512]{1,0:T(8,128)(2,1)S(1)}, bf16[96,512]{1,0:T(8,128)(2,1)S(1)}, u32[]{:S(2)}, u32[]{:S(2)}) collective-permute-start(bf16[96,512]{1,0:T(8,128)(2,1)S(1)} %shard_map.101.refs_0_), channel_id=1, source_target_pairs={{0,1},{1,0},{2,3},{3,2},{4,5},{5,4},{6,7},{7,6},{8,9},{9,8},{10,11... | collective-permute-start | bytes 294920 | tf_op jit(solution)/shard_map/ppermute | solution.py:24
  49.7 15.0 %collective-permute-start.28 = (bf16[320,256]{1,0:T(8,128)(2,1)S(1)}, bf16[320,256]{1,0:T(8,128)(2,1)S(1)}, u32[]{:S(2)}, u32[]{:S(2)}) collective-permute-start(bf16[320,256]{1,0:T(8,128)(2,1)S(1)} %get-tuple-element.60), channel_id=1, source_target_pairs={{0,16},{8,24},{16,0},{24,8},{1,17},{9,25},{17,1},{25,9},{2,18},{10... | collective-permute-start | bytes 491528 | tf_op jit(solution)/shard_map/ppermute | solution.py:24
  52.7 15.1 %collective-permute-start.17 = (bf16[320,256]{1,0:T(8,128)(2,1)S(1)}, bf16[320,256]{1,0:T(8,128)(2,1)S(1)}, u32[]{:S(2)}, u32[]{:S(2)}) collective-permute-start(bf16[320,256]{1,0:T(8,128)(2,1)S(1)} %get-tuple-element.55), channel_id=1, source_target_pairs={{0,16},{8,24},{16,0},{24,8},{1,17},{9,25},{17,1},{25,9},{2,18},{10... | collective-permute-start | bytes 491528 | tf_op jit(solution)/shard_map/ppermute | solution.py:24
  53.3 2.5 %collective-permute-start.25 = (bf16[96,512]{1,0:T(8,128)(2,1)S(1)}, bf16[96,512]{1,0:T(8,128)(2,1)S(1)}, u32[]{:S(2)}, u32[]{:S(2)}) collective-permute-start(bf16[96,512]{1,0:T(8,128)(2,1)S(1)} %collective-permute-done.24.refs_4_), channel_id=1, source_target_pairs={{0,1},{1,0},{2,3},{3,2},{4,5},{5,4},{6,7},{7,6},{8,9},{9,8},{10,11... | collective-permute-start | bytes 294920 | tf_op jit(solution)/shard_map/ppermute | solution.py:24
  (11 other events, 64.0 us)

commit v6 on v5

--- a/solution.py
+++ b/solution.py
@@ -224,10 +224,11 @@
             refs = list(refs)
             head = refs.pop(0) if headed else None
             code_ref, top = (refs.pop(0), refs.pop(0)) if extra else (None, None)
-            bulks = refs[-parts:]
-            blocks, (pivots, out) = refs[:-2 - parts], refs[-2 - parts:-parts]
+            at = len(refs) - parts
+            blocks, (pivots, out), bulks = refs[:at - 2], refs[at - 2:at], refs[at:]
             pivots_from([ref[...] for ref in blocks], inverse[...], pivots, middle, inner)
-            update = (cs[...].astype(F32) - dot(fs[...], pivots[...], NT)).astype(BF)
+            used = slice(None) if parts else slice(0, 2 * count)
+            update = (cs[used].astype(F32) - dot(fs[used], pivots[...], NT)).astype(BF)
             out[:count] = (update[:count].astype(F32) + head[...].astype(F32)).astype(BF) if headed else update[:count]
             out[count:2 * count] = update[count:2 * count]
             if extra:
@@ -247,7 +248,7 @@
         return call(
             chain(1 << level, count, bool(head), bool(extra), parts),
             [VM] * (3 + len(head) + len(extra) + len(blocks)),
-            [((cols, panel), BF), ((2 * count + (share if extra else 0), cols), BF)] + [((half, cols // parts), BF)] * parts,
+            [((cols, panel), BF), ((2 * count + (share if extra else 0), cols), BF)] + [((half, cols // max(parts, 1)), BF)] * parts,
         )(fs, cs, inverse, *head, *extra, *blocks)
 
     def own(level, code, factor, front, pivots, parent):
@@ -259,7 +260,11 @@
         return call(body, [VM, VM, VM, VP, VM, VP], [((rows, cols), F32)])(
             live, code, factor, front, pivots, parent)[0]
 
-    pivots0, pivot0, bulk0 = after(0, fs0, cs0, dinv_leaf, blocks0, 1)
+    def rest(fs, cs, pivots, out):
+        out[...] = (cs[2 * n[1]:].astype(F32) - dot(fs[2 * n[1]:], pivots[...], NT)).astype(BF)
+
+    pivots0, pivot0 = after(0, fs0, cs0, dinv_leaf, blocks0, 0)
+    bulk0, = call(rest, [VM] * 3, [((half, cols), BF)])(fs0, cs0, pivots0)
     pivot0_other = swap(pivot0, "sub", 1)
     bulk0_other = swap(bulk0, "sub", 1)
 

time: 69.6 us -> 69.8 us (level)
    pallas_call x15 -> x16, Pallas kernels: 12 us -> 12.2 us  [run(): made(*[pltpu.with_memory_space_constraint(a, pltpu.HBM) if spec is AN els...]
where the time goes in v6:
time: 69.8 us; the launch traced here: 69.7 us
  waiting for transfers between devices  34.2 us (49%)
  starting transfers between devices  22.9 us (33%)
  Pallas kernels  12.2 us (17%)
    ppermute x29, waiting for transfers between devices, swap(): lax.ppermute(value, axis, [(i, i ^ mask) for i in range(lax.axis_size(axi...  34.2 us
    ppermute x29, starting transfers between devices, swap(): lax.ppermute(value, axis, [(i, i ^ mask) for i in range(lax.axis_size(axi...  22.9 us
    pallas_call x16, Pallas kernels, run(): made(*[pltpu.with_memory_space_constraint(a, pltpu.HBM) if spec is AN els...  12.2 us
  transfers between devices with their start and end apart: 29, of which 13 were waited for; matrix products, arithmetic and copies ran while one was open for 0% of the time, Pallas kernels for 11%

profile of v6, /device:TPU:0, one launch (start us, length us, event | category | flops | bytes accessed | tf_op | source)
XLA Modules:
  0.0 69.7 jit_solution(8021160537215325462)
XLA Ops:
  0.0 1.1 %shard_map.91 = (bf16[176,512]{1,0:T(8,128)(2,1)S(1)}, s32[5,128]{1,0:T(8,128)S(1)}, s32[5,128]{1,0:T(8,128)S(1)}, bf16[64,512]{1,0:T(8,128)(2,1)S(1)}, bf16[16,512]{1,0:T(8,128)(2,1)S(1)}) custom-call(s32[5,128]{1,0:T(8,128)} %bitcast.10, s32[5,128]{1,0:T(8,128)} %bitcast.11, bf16[256,256]{1,0:T(8,128)(2,1)} %mid.1, bf16[640,1024]{1,0:T(8,128)(2,1)} %front_ref.3, ...), custom_call_target="tpu_custom_call" | custom-call | tf_op jit(solution)/shard_map/pallas_call | solution.py:39
  1.1 4.0 %collective-permute-start.5 = (bf16[64,512]{1,0:T(8,128)(2,1)S(1)}, bf16[64,512]{1,0:T(8,128)(2,1)S(1)}, u32[]{:S(2)}, u32[]{:S(2)}) collective-permute-start(bf16[64,512]{1,0:T(8,128)(2,1)S(1)} %get-tuple-element.36.refs_0_), channel_id=1, source_target_pairs={{0,6},{1,7},{2,4},{3,5},{4,2},{5,3},{6,0},{7,1},{8,14},{9,15},{10,... | collective-permute-start | bytes 196616 | tf_op jit(solution)/shard_map/ppermute | solution.py:24
  5.8 1.6 %collective-permute-done.5.refs_6_ = bf16[64,512]{1,0:T(8,128)(2,1)S(1)} collective-permute-done((bf16[64,512]{1,0:T(8,128)(2,1)S(1)}, bf16[64,512]{1,0:T(8,128)(2,1)S(1)}, u32[]{:S(2)}, u32[]{:S(2)}) %collective-permute-start.5) | collective-permute-done | bytes 65568 | tf_op jit(solution)/shard_map/ppermute | solution.py:24
  7.4 2.0 %collective-permute-done.3.refs_4_ = bf16[64,512]{1,0:T(8,128)(2,1)S(1)} collective-permute-done((bf16[64,512]{1,0:T(8,128)(2,1)S(1)}, bf16[64,512]{1,0:T(8,128)(2,1)S(1)}, u32[]{:S(2)}, u32[]{:S(2)}) %collective-permute-start.3) | collective-permute-done | bytes 65568 | tf_op jit(solution)/shard_map/ppermute | solution.py:24
  9.9 1.1 %shard_map.92 = (bf16[384,512]{1,0:T(8,128)(2,1)S(1)}, bf16[384,512]{1,0:T(8,128)(2,1)S(1)}, bf16[640,512]{1,0:T(8,128)(2,1)S(1)}) custom-call(s32[1,3]{1,0:T(1,128)S(1)} %bitcast.3, s32[5,128]{1,0:T(8,128)S(1)} %get-tuple-element.33.code.code_ref, bf16[640,1024]{1,0:T(8,128)(2,1)S(1)} %copy-done.1, bf16[512,256]{1,0:T(8,128)(2,1)S(1)} %copy-done.3), custom_call_target="tpu_custom_call" | custom-call | tf_op jit(solution)/shard_map/pallas_call | solution.py:39
  12.1 1.6 %collective-permute-start.7 = (bf16[320,512]{1,0:T(8,128)(2,1)S(1)}, bf16[320,512]{1,0:T(8,128)(2,1)S(1)}, u32[]{:S(2)}, u32[]{:S(2)}) collective-permute-start(bf16[320,512]{1,0:T(8,128)(2,1)S(1)} %shard_map.96), channel_id=1, source_target_pairs={{0,8},{8,0},{16,24},{24,16},{1,9},{9,1},{17,25},{25,17},{2,10},{10... | collective-permute-start | bytes 983048 | tf_op jit(solution)/shard_map/ppermute | solution.py:24
  14.2 1.6 %collective-permute-start.9 = (bf16[64,512]{1,0:T(8,128)(2,1)S(1)}, bf16[64,512]{1,0:T(8,128)(2,1)S(1)}, u32[]{:S(2)}, u32[]{:S(2)}) collective-permute-start(bf16[64,512]{1,0:T(8,128)(2,1)S(1)} %get-tuple-element.37.refs_1_), channel_id=1, source_target_pairs={{0,8},{8,0},{16,24},{24,16},{1,9},{9,1},{17,25},{25,17},{2,10},{10... | collective-permute-start | bytes 196616 | tf_op jit(solution)/shard_map/ppermute | solution.py:24
  16.5 10.2 %collective-permute-done.8.near_ref = bf16[176,512]{1,0:T(8,128)(2,1)S(1)} collective-permute-done((bf16[176,512]{1,0:T(8,128)(2,1)S(1)}, bf16[176,512]{1,0:T(8,128)(2,1)S(1)}, u32[]{:S(2)}, u32[]{:S(2)}) %collective-permute-start.8) | collective-permute-done | bytes 180256 | tf_op jit(solution)/shard_map/ppermute | solution.py:24
  27.6 1.6 %collective-permute-start.15 = (bf16[64,512]{1,0:T(8,128)(2,1)S(1)}, bf16[64,512]{1,0:T(8,128)(2,1)S(1)}, u32[]{:S(2)}, u32[]{:S(2)}) collective-permute-start(bf16[64,512]{1,0:T(8,128)(2,1)S(1)} %shard_map.99.refs_3_), channel_id=1, source_target_pairs={{0,6},{1,7},{2,4},{3,5},{4,2},{5,3},{6,0},{7,1},{8,14},{9,15},{10,... | collective-permute-start | bytes 196616 | tf_op jit(solution)/shard_map/ppermute | solution.py:24
  29.8 1.4 %collective-permute-start.11 = (bf16[64,512]{1,0:T(8,128)(2,1)S(1)}, bf16[64,512]{1,0:T(8,128)(2,1)S(1)}, u32[]{:S(2)}, u32[]{:S(2)}) collective-permute-start(bf16[64,512]{1,0:T(8,128)(2,1)S(1)} %shard_map.99.refs_3_), channel_id=1, source_target_pairs={{0,2},{1,3},{2,0},{3,1},{4,6},{5,7},{6,4},{7,5},{8,10},{9,11},{10,... | collective-permute-start | bytes 196616 | tf_op jit(solution)/shard_map/ppermute | solution.py:24
  31.1 2.3 %collective-permute-done.15.refs_9_ = bf16[64,512]{1,0:T(8,128)(2,1)S(1)} collective-permute-done((bf16[64,512]{1,0:T(8,128)(2,1)S(1)}, bf16[64,512]{1,0:T(8,128)(2,1)S(1)}, u32[]{:S(2)}, u32[]{:S(2)}) %collective-permute-start.15) | collective-permute-done | bytes 65568 | tf_op jit(solution)/shard_map/ppermute | solution.py:24
  34.3 1.1 %shard_map.95.merged = f32[640,512]{1,0:T(8,128)S(1)} custom-call(s32[1,3]{1,0:T(1,128)S(1)} %bitcast.5, s32[5,128]{1,0:T(8,128)S(1)} %get-tuple-element.33.code.code_ref, bf16[640,512]{1,0:T(8,128)(2,1)S(1)} %get-tuple-element.40.factor_ref, bf16[640,1024]{1,0:T(8,128)(2,1)S(1)} %copy-done.1, bf16[512,512]{1,0:T(8,128)(2,1)S(1)} %get-tuple-element.41.pivots_ref.pivots, ...), custom_call_target="tpu_custom_call" | custom-call | tf_op jit(solution)/shard_map/pallas_call | solution.py:39
  35.4 1.0 %shard_map.98 = (bf16[352,512]{1,0:T(8,128)(2,1)S(1)}, bf16[640,512]{1,0:T(8,128)(2,1)S(1)}) custom-call(s32[1,3]{1,0:T(1,128)S(1)} %bitcast.6, bf16[352,640]{1,0:T(8,128)(2,1)S(1)} %get-tuple-element.39.pick, f32[640,512]{1,0:T(8,128)S(1)} %shard_map.95.merged, bf16[320,512]{1,0:T(8,128)(2,1)S(1)} %collective-permute-done.7.got, ...), custom_call_target="tpu_custom_call" | custom-call | tf_op jit(solution)/shard_map/pallas_call | solution.py:39
  37.2 3.6 %collective-permute-start.20 = (bf16[48,512]{1,0:T(8,128)(2,1)S(1)}, bf16[48,512]{1,0:T(8,128)(2,1)S(1)}, u32[]{:S(2)}, u32[]{:S(2)}) collective-permute-start(bf16[48,512]{1,0:T(8,128)(2,1)S(1)} %get-tuple-element.54.refs_0_), channel_id=1, source_target_pairs={{0,24},{8,16},{16,8},{24,0},{1,25},{9,17},{17,9},{25,1},{2,26},{10... | collective-permute-start | bytes 147464 | tf_op jit(solution)/shard_map/ppermute | solution.py:24
  41.7 1.9 %collective-permute-done.20.refs_3_ = bf16[48,512]{1,0:T(8,128)(2,1)S(1)} collective-permute-done((bf16[48,512]{1,0:T(8,128)(2,1)S(1)}, bf16[48,512]{1,0:T(8,128)(2,1)S(1)}, u32[]{:S(2)}, u32[]{:S(2)}) %collective-permute-start.20) | collective-permute-done | bytes 49184 | tf_op jit(solution)/shard_map/ppermute | solution.py:24
  43.5 2.1 %collective-permute-done.19.refs_1_ = bf16[48,512]{1,0:T(8,128)(2,1)S(1)} collective-permute-done((bf16[48,512]{1,0:T(8,128)(2,1)S(1)}, bf16[48,512]{1,0:T(8,128)(2,1)S(1)}, u32[]{:S(2)}, u32[]{:S(2)}) %collective-permute-start.19) | collective-permute-done | bytes 49184 | tf_op jit(solution)/shard_map/ppermute | solution.py:24
  46.4 1.8 %collective-permute-start.26 = (bf16[96,512]{1,0:T(8,128)(2,1)S(1)}, bf16[96,512]{1,0:T(8,128)(2,1)S(1)}, u32[]{:S(2)}, u32[]{:S(2)}) collective-permute-start(bf16[96,512]{1,0:T(8,128)(2,1)S(1)} %shard_map.102.refs_0_), channel_id=1, source_target_pairs={{0,6},{1,7},{2,4},{3,5},{4,2},{5,3},{6,0},{7,1},{8,14},{9,15},{10,... | collective-permute-start | bytes 294920 | tf_op jit(solution)/shard_map/ppermute | solution.py:24
  48.7 1.3 %collective-permute-start.22 = (bf16[96,512]{1,0:T(8,128)(2,1)S(1)}, bf16[96,512]{1,0:T(8,128)(2,1)S(1)}, u32[]{:S(2)}, u32[]{:S(2)}) collective-permute-start(bf16[96,512]{1,0:T(8,128)(2,1)S(1)} %shard_map.102.refs_0_), channel_id=1, source_target_pairs={{0,2},{1,3},{2,0},{3,1},{4,6},{5,7},{6,4},{7,5},{8,10},{9,11},{10,... | collective-permute-start | bytes 294920 | tf_op jit(solution)/shard_map/ppermute | solution.py:24
  50.0 1.4 %collective-permute-start.28 = (bf16[320,256]{1,0:T(8,128)(2,1)S(1)}, bf16[320,256]{1,0:T(8,128)(2,1)S(1)}, u32[]{:S(2)}, u32[]{:S(2)}) collective-permute-start(bf16[320,256]{1,0:T(8,128)(2,1)S(1)} %get-tuple-element.58), channel_id=1, source_target_pairs={{0,16},{8,24},{16,0},{24,8},{1,17},{9,25},{17,1},{25,9},{2,18},{10... | collective-permute-start | bytes 491528 | tf_op jit(solution)/shard_map/ppermute | solution.py:24
  51.4 1.5 %collective-permute-done.26.refs_6_ = bf16[96,512]{1,0:T(8,128)(2,1)S(1)} collective-permute-done((bf16[96,512]{1,0:T(8,128)(2,1)S(1)}, bf16[96,512]{1,0:T(8,128)(2,1)S(1)}, u32[]{:S(2)}, u32[]{:S(2)}) %collective-permute-start.26) | collective-permute-done | bytes 98336 | tf_op jit(solution)/shard_map/ppermute | solution.py:24
  54.1 1.1 %shard_map.101.merged = f32[640,512]{1,0:T(8,128)S(1)} custom-call(s32[1,3]{1,0:T(1,128)S(1)} %bitcast.7, s32[5,128]{1,0:T(8,128)S(1)} %get-tuple-element.38.code.refs_1_.code_ref, bf16[640,512]{1,0:T(8,128)(2,1)S(1)} %get-tuple-element.46.factor_ref, bf16[640,1024]{1,0:T(8,128)(2,1)S(1)} %copy-done, bf16[512,512]{1,0:T(8,128)(2,1)S(1)} %get-tuple-element.52.pivots_ref, ...), custom_call_target="tpu_custom_call" | custom-call | tf_op jit(solution)/shard_map/pallas_call | solution.py:39
  56.4 8.5 %collective-permute-done.28.got = bf16[320,256]{1,0:T(8,128)(2,1)S(1)} collective-permute-done((bf16[320,256]{1,0:T(8,128)(2,1)S(1)}, bf16[320,256]{1,0:T(8,128)(2,1)S(1)}, u32[]{:S(2)}, u32[]{:S(2)}) %collective-permute-start.28) | collective-permute-done | bytes 163872 | tf_op jit(solution)/shard_map/ppermute | solution.py:24
  65.8 2.3 %collective-permute-done.17.got = bf16[320,256]{1,0:T(8,128)(2,1)S(1)} collective-permute-done((bf16[320,256]{1,0:T(8,128)(2,1)S(1)}, bf16[320,256]{1,0:T(8,128)(2,1)S(1)}, u32[]{:S(2)}, u32[]{:S(2)}) %collective-permute-start.17) | collective-permute-done | bytes 163872 | tf_op jit(solution)/shard_map/ppermute | solution.py:24
  68.0 1.6 %shard_map.106 = bf16[640,512]{1,0:T(8,128)(2,1)} custom-call(s32[1,3]{1,0:T(1,128)S(1)} %bitcast.9, f32[640,512]{1,0:T(8,128)S(1)} %shard_map.101.merged, bf16[320,256]{1,0:T(8,128)(2,1)S(1)} %collective-permute-done.17.got, bf16[640,320]{1,0:T(8,128)(2,1)S(1)} %shard_map.103.land, bf16[512,256]{1,0:T(8,128)(2,1)S(1)} %get-tuple-element.56.inverse, ...), custom_call_target="tpu_custom_call" | custom-call | tf_op jit(solution)/shard_map/pallas_call | solution.py:39
  (62 shorter events, 11.7 us)
Async XLA Ops:
  1.1 6.2 %collective-permute-start.5 = (bf16[64,512]{1,0:T(8,128)(2,1)S(1)}, bf16[64,512]{1,0:T(8,128)(2,1)S(1)}, u32[]{:S(2)}, u32[]{:S(2)}) collective-permute-start(bf16[64,512]{1,0:T(8,128)(2,1)S(1)} %get-tuple-element.36.refs_0_), channel_id=1, source_target_pairs={{0,6},{1,7},{2,4},{3,5},{4,2},{5,3},{6,0},{7,1},{8,14},{9,15},{10,... | collective-permute-start | bytes 196616 | tf_op jit(solution)/shard_map/ppermute | solution.py:24
  5.1 4.3 %collective-permute-start.3 = (bf16[64,512]{1,0:T(8,128)(2,1)S(1)}, bf16[64,512]{1,0:T(8,128)(2,1)S(1)}, u32[]{:S(2)}, u32[]{:S(2)}) collective-permute-start(bf16[64,512]{1,0:T(8,128)(2,1)S(1)} %get-tuple-element.36.refs_0_), channel_id=1, source_target_pairs={{0,4},{1,5},{2,6},{3,7},{4,0},{5,1},{6,2},{7,3},{8,12},{9,13},{10,... | collective-permute-start | bytes 196616 | tf_op jit(solution)/shard_map/ppermute | solution.py:24
  5.6 4.3 %collective-permute-start.1 = (bf16[64,512]{1,0:T(8,128)(2,1)S(1)}, bf16[64,512]{1,0:T(8,128)(2,1)S(1)}, u32[]{:S(2)}, u32[]{:S(2)}) collective-permute-start(bf16[64,512]{1,0:T(8,128)(2,1)S(1)} %get-tuple-element.36.refs_0_), channel_id=1, source_target_pairs={{0,2},{1,3},{2,0},{3,1},{4,6},{5,7},{6,4},{7,5},{8,10},{9,11},{10,... | collective-permute-start | bytes 196616 | tf_op jit(solution)/shard_map/ppermute | solution.py:24
  5.8 5.2 %collective-permute-start = (bf16[64,512]{1,0:T(8,128)(2,1)S(1)}, bf16[64,512]{1,0:T(8,128)(2,1)S(1)}, u32[]{:S(2)}, u32[]{:S(2)}) collective-permute-start(bf16[64,512]{1,0:T(8,128)(2,1)S(1)} %get-tuple-element.36.refs_0_), channel_id=1, source_target_pairs={{0,1},{1,0},{2,3},{3,2},{4,5},{5,4},{6,7},{7,6},{8,9},{9,8},{10,11... | collective-permute-start | bytes 196616 | tf_op jit(solution)/shard_map/ppermute | solution.py:24
  7.4 3.6 %collective-permute-start.6 = (bf16[64,512]{1,0:T(8,128)(2,1)S(1)}, bf16[64,512]{1,0:T(8,128)(2,1)S(1)}, u32[]{:S(2)}, u32[]{:S(2)}) collective-permute-start(bf16[64,512]{1,0:T(8,128)(2,1)S(1)} %collective-permute-done.5.refs_6_), channel_id=1, source_target_pairs={{0,1},{1,0},{2,3},{3,2},{4,5},{5,4},{6,7},{7,6},{8,9},{9,8},{10,11... | collective-permute-start | bytes 196616 | tf_op jit(solution)/shard_map/ppermute | solution.py:24
  12.1 23.3 %collective-permute-start.7 = (bf16[320,512]{1,0:T(8,128)(2,1)S(1)}, bf16[320,512]{1,0:T(8,128)(2,1)S(1)}, u32[]{:S(2)}, u32[]{:S(2)}) collective-permute-start(bf16[320,512]{1,0:T(8,128)(2,1)S(1)} %shard_map.96), channel_id=1, source_target_pairs={{0,8},{8,0},{16,24},{24,16},{1,9},{9,1},{17,25},{25,17},{2,10},{10... | collective-permute-start | bytes 983048 | tf_op jit(solution)/shard_map/ppermute | solution.py:24
  13.8 12.9 %collective-permute-start.8 = (bf16[176,512]{1,0:T(8,128)(2,1)S(1)}, bf16[176,512]{1,0:T(8,128)(2,1)S(1)}, u32[]{:S(2)}, u32[]{:S(2)}) collective-permute-start(bf16[176,512]{1,0:T(8,128)(2,1)S(1)} %get-tuple-element.42.mine), channel_id=1, source_target_pairs={{0,8},{8,0},{16,24},{24,16},{1,9},{9,1},{17,25},{25,17},{2,10},{10... | collective-permute-start | bytes 540680 | tf_op jit(solution)/shard_map/ppermute | solution.py:24
  14.2 13.3 %collective-permute-start.9 = (bf16[64,512]{1,0:T(8,128)(2,1)S(1)}, bf16[64,512]{1,0:T(8,128)(2,1)S(1)}, u32[]{:S(2)}, u32[]{:S(2)}) collective-permute-start(bf16[64,512]{1,0:T(8,128)(2,1)S(1)} %get-tuple-element.37.refs_1_), channel_id=1, source_target_pairs={{0,8},{8,0},{16,24},{24,16},{1,9},{9,1},{17,25},{25,17},{2,10},{10... | collective-permute-start | bytes 196616 | tf_op jit(solution)/shard_map/ppermute | solution.py:24
  27.6 5.9 %collective-permute-start.15 = (bf16[64,512]{1,0:T(8,128)(2,1)S(1)}, bf16[64,512]{1,0:T(8,128)(2,1)S(1)}, u32[]{:S(2)}, u32[]{:S(2)}) collective-permute-start(bf16[64,512]{1,0:T(8,128)(2,1)S(1)} %shard_map.99.refs_3_), channel_id=1, source_target_pairs={{0,6},{1,7},{2,4},{3,5},{4,2},{5,3},{6,0},{7,1},{8,14},{9,15},{10,... | collective-permute-start | bytes 196616 | tf_op jit(solution)/shard_map/ppermute | solution.py:24
  29.1 4.7 %collective-permute-start.13 = (bf16[64,512]{1,0:T(8,128)(2,1)S(1)}, bf16[64,512]{1,0:T(8,128)(2,1)S(1)}, u32[]{:S(2)}, u32[]{:S(2)}) collective-permute-start(bf16[64,512]{1,0:T(8,128)(2,1)S(1)} %shard_map.99.refs_3_), channel_id=1, source_target_pairs={{0,4},{1,5},{2,6},{3,7},{4,0},{5,1},{6,2},{7,3},{8,12},{9,13},{10,... | collective-permute-start | bytes 196616 | tf_op jit(solution)/shard_map/ppermute | solution.py:24
  29.8 4.3 %collective-permute-start.11 = (bf16[64,512]{1,0:T(8,128)(2,1)S(1)}, bf16[64,512]{1,0:T(8,128)(2,1)S(1)}, u32[]{:S(2)}, u32[]{:S(2)}) collective-permute-start(bf16[64,512]{1,0:T(8,128)(2,1)S(1)} %shard_map.99.refs_3_), channel_id=1, source_target_pairs={{0,2},{1,3},{2,0},{3,1},{4,6},{5,7},{6,4},{7,5},{8,10},{9,11},{10,... | collective-permute-start | bytes 196616 | tf_op jit(solution)/shard_map/ppermute | solution.py:24
  31.1 5.3 %collective-permute-start.10 = (bf16[64,512]{1,0:T(8,128)(2,1)S(1)}, bf16[64,512]{1,0:T(8,128)(2,1)S(1)}, u32[]{:S(2)}, u32[]{:S(2)}) collective-permute-start(bf16[64,512]{1,0:T(8,128)(2,1)S(1)} %shard_map.99.refs_3_), channel_id=1, source_target_pairs={{0,1},{1,0},{2,3},{3,2},{4,5},{5,4},{6,7},{7,6},{8,9},{9,8},{10,11... | collective-permute-start | bytes 196616 | tf_op jit(solution)/shard_map/ppermute | solution.py:24
  33.5 2.9 %collective-permute-start.16 = (bf16[64,512]{1,0:T(8,128)(2,1)S(1)}, bf16[64,512]{1,0:T(8,128)(2,1)S(1)}, u32[]{:S(2)}, u32[]{:S(2)}) collective-permute-start(bf16[64,512]{1,0:T(8,128)(2,1)S(1)} %collective-permute-done.15.refs_9_), channel_id=1, source_target_pairs={{0,1},{1,0},{2,3},{3,2},{4,5},{5,4},{6,7},{7,6},{8,9},{9,8},{10,11... | collective-permute-start | bytes 196616 | tf_op jit(solution)/shard_map/ppermute | solution.py:24
  33.8 2.6 %collective-permute-start.14 = (bf16[64,512]{1,0:T(8,128)(2,1)S(1)}, bf16[64,512]{1,0:T(8,128)(2,1)S(1)}, u32[]{:S(2)}, u32[]{:S(2)}) collective-permute-start(bf16[64,512]{1,0:T(8,128)(2,1)S(1)} %collective-permute-done.13.refs_7_), channel_id=1, source_target_pairs={{0,1},{1,0},{2,3},{3,2},{4,5},{5,4},{6,7},{7,6},{8,9},{9,8},{10,11... | collective-permute-start | bytes 196616 | tf_op jit(solution)/shard_map/ppermute | solution.py:24
  37.2 6.3 %collective-permute-start.20 = (bf16[48,512]{1,0:T(8,128)(2,1)S(1)}, bf16[48,512]{1,0:T(8,128)(2,1)S(1)}, u32[]{:S(2)}, u32[]{:S(2)}) collective-permute-start(bf16[48,512]{1,0:T(8,128)(2,1)S(1)} %get-tuple-element.54.refs_0_), channel_id=1, source_target_pairs={{0,24},{8,16},{16,8},{24,0},{1,25},{9,17},{17,9},{25,1},{2,26},{10... | collective-permute-start | bytes 147464 | tf_op jit(solution)/shard_map/ppermute | solution.py:24
  40.9 4.8 %collective-permute-start.19 = (bf16[48,512]{1,0:T(8,128)(2,1)S(1)}, bf16[48,512]{1,0:T(8,128)(2,1)S(1)}, u32[]{:S(2)}, u32[]{:S(2)}) collective-permute-start(bf16[48,512]{1,0:T(8,128)(2,1)S(1)} %get-tuple-element.54.refs_0_), channel_id=1, source_target_pairs={{0,8},{8,0},{16,24},{24,16},{1,9},{9,1},{17,25},{25,17},{2,10},{10... | collective-permute-start | bytes 147464 | tf_op jit(solution)/shard_map/ppermute | solution.py:24
  40.9 5.5 %collective-permute-start.18 = (bf16[48,512]{1,0:T(8,128)(2,1)S(1)}, bf16[48,512]{1,0:T(8,128)(2,1)S(1)}, u32[]{:S(2)}, u32[]{:S(2)}) collective-permute-start(bf16[48,512]{1,0:T(8,128)(2,1)S(1)} %get-tuple-element.54.refs_0_), channel_id=1, source_target_pairs={{0,16},{8,24},{16,0},{24,8},{1,17},{9,25},{17,1},{25,9},{2,18},{10... | collective-permute-start | bytes 147464 | tf_op jit(solution)/shard_map/ppermute | solution.py:24
  46.4 6.5 %collective-permute-start.26 = (bf16[96,512]{1,0:T(8,128)(2,1)S(1)}, bf16[96,512]{1,0:T(8,128)(2,1)S(1)}, u32[]{:S(2)}, u32[]{:S(2)}) collective-permute-start(bf16[96,512]{1,0:T(8,128)(2,1)S(1)} %shard_map.102.refs_0_), channel_id=1, source_target_pairs={{0,6},{1,7},{2,4},{3,5},{4,2},{5,3},{6,0},{7,1},{8,14},{9,15},{10,... | collective-permute-start | bytes 294920 | tf_op jit(solution)/shard_map/ppermute | solution.py:24
  48.2 5.3 %collective-permute-start.24 = (bf16[96,512]{1,0:T(8,128)(2,1)S(1)}, bf16[96,512]{1,0:T(8,128)(2,1)S(1)}, u32[]{:S(2)}, u32[]{:S(2)}) collective-permute-start(bf16[96,512]{1,0:T(8,128)(2,1)S(1)} %shard_map.102.refs_0_), channel_id=1, source_target_pairs={{0,4},{1,5},{2,6},{3,7},{4,0},{5,1},{6,2},{7,3},{8,12},{9,13},{10,... | collective-permute-start | bytes 294920 | tf_op jit(solution)/shard_map/ppermute | solution.py:24
  48.7 4.8 %collective-permute-start.22 = (bf16[96,512]{1,0:T(8,128)(2,1)S(1)}, bf16[96,512]{1,0:T(8,128)(2,1)S(1)}, u32[]{:S(2)}, u32[]{:S(2)}) collective-permute-start(bf16[96,512]{1,0:T(8,128)(2,1)S(1)} %shard_map.102.refs_0_), channel_id=1, source_target_pairs={{0,2},{1,3},{2,0},{3,1},{4,6},{5,7},{6,4},{7,5},{8,10},{9,11},{10,... | collective-permute-start | bytes 294920 | tf_op jit(solution)/shard_map/ppermute | solution.py:24
  50.0 4.1 %collective-permute-start.21 = (bf16[96,512]{1,0:T(8,128)(2,1)S(1)}, bf16[96,512]{1,0:T(8,128)(2,1)S(1)}, u32[]{:S(2)}, u32[]{:S(2)}) collective-permute-start(bf16[96,512]{1,0:T(8,128)(2,1)S(1)} %shard_map.102.refs_0_), channel_id=1, source_target_pairs={{0,1},{1,0},{2,3},{3,2},{4,5},{5,4},{6,7},{7,6},{8,9},{9,8},{10,11... | collective-permute-start | bytes 294920 | tf_op jit(solution)/shard_map/ppermute | solution.py:24
  50.0 15.0 %collective-permute-start.28 = (bf16[320,256]{1,0:T(8,128)(2,1)S(1)}, bf16[320,256]{1,0:T(8,128)(2,1)S(1)}, u32[]{:S(2)}, u32[]{:S(2)}) collective-permute-start(bf16[320,256]{1,0:T(8,128)(2,1)S(1)} %get-tuple-element.58), channel_id=1, source_target_pairs={{0,16},{8,24},{16,0},{24,8},{1,17},{9,25},{17,1},{25,9},{2,18},{10... | collective-permute-start | bytes 491528 | tf_op jit(solution)/shard_map/ppermute | solution.py:24
  52.9 15.1 %collective-permute-start.17 = (bf16[320,256]{1,0:T(8,128)(2,1)S(1)}, bf16[320,256]{1,0:T(8,128)(2,1)S(1)}, u32[]{:S(2)}, u32[]{:S(2)}) collective-permute-start(bf16[320,256]{1,0:T(8,128)(2,1)S(1)} %get-tuple-element.53), channel_id=1, source_target_pairs={{0,16},{8,24},{16,0},{24,8},{1,17},{9,25},{17,1},{25,9},{2,18},{10... | collective-permute-start | bytes 491528 | tf_op jit(solution)/shard_map/ppermute | solution.py:24
  53.5 2.5 %collective-permute-start.25 = (bf16[96,512]{1,0:T(8,128)(2,1)S(1)}, bf16[96,512]{1,0:T(8,128)(2,1)S(1)}, u32[]{:S(2)}, u32[]{:S(2)}) collective-permute-start(bf16[96,512]{1,0:T(8,128)(2,1)S(1)} %collective-permute-done.24.refs_4_), channel_id=1, source_target_pairs={{0,1},{1,0},{2,3},{3,2},{4,5},{5,4},{6,7},{7,6},{8,9},{9,8},{10,11... | collective-permute-start | bytes 294920 | tf_op jit(solution)/shard_map/ppermute | solution.py:24
  (11 other events, 63.0 us)

commit v7 on v6

--- a/solution.py
+++ b/solution.py
@@ -342,9 +342,16 @@
         before1, [VM] * 6, sent(2)[:1] + [((rows, panel), BF)],
     )(live, pick1, merged0, bulk0_other, land0, inv_mid)
     blocks1 = collect(raw1, spread1)
-    pivots1, pivot1, *bulk1 = after(
-        1, fs1, cs1, inv_mid, blocks1, panel // block, (top_head,), (code1, dinv_top) if shared else ())
+    pivots1, pivot1 = after(
+        1, fs1, cs1, inv_mid, blocks1, 0, (top_head,), (code1, dinv_top) if shared else ())
     others = [pivot1] + [swap(pivot1, "sub", m) for m in (1, 2, 3)]
+
+    def rest1(fs, cs, pivots, *outs):
+        for i, out in enumerate(outs):
+            lane = slice(i * block, (i + 1) * block)
+            out[...] = (cs[2 * n[2]:, lane].astype(F32) - dot(fs[2 * n[2]:], pivots[lane], NT)).astype(BF)
+
+    bulk1 = call(rest1, [VM] * 3, [((half, block), BF)] * (panel // block))(fs1, cs1, pivots1)
     bulk1_other = [swap(part, "sub", 2) for part in bulk1]
     raw2, = call(raised(n[2], 2, 0, shared), [VM] * 4, [((4 * n[2] + (2 * share if shared else 0), panel), BF)])(*others)
     spread2 = spread(raw2)

time: 69.8 us -> 70.1 us (level)
    pallas_call x16 -> x17, Pallas kernels: 12.2 us -> 12.5 us  [run(): made(*[pltpu.with_memory_space_constraint(a, pltpu.HBM) if spec is AN els...]
  transfers between devices with their start and end apart: 29 -> 29, of which waited for: 13 -> 13; matrix products, arithmetic and copies ran while one was open for 0% -> 0% of each run, Pallas kernels for 11% -> 12%
where the time goes in v7:
time: 70.1 us; the launch traced here: 70 us
  waiting for transfers between devices  34.2 us (49%)
  starting transfers between devices  23 us (33%)
  Pallas kernels  12.5 us (18%)
    ppermute x29, waiting for transfers between devices, swap(): lax.ppermute(value, axis, [(i, i ^ mask) for i in range(lax.axis_size(axi...  34.2 us
    ppermute x29, starting transfers between devices, swap(): lax.ppermute(value, axis, [(i, i ^ mask) for i in range(lax.axis_size(axi...  23 us
    pallas_call x17, Pallas kernels, run(): made(*[pltpu.with_memory_space_constraint(a, pltpu.HBM) if spec is AN els...  12.5 us
  transfers between devices with their start and end apart: 29, of which 13 were waited for; matrix products, arithmetic and copies ran while one was open for 0% of the time, Pallas kernels for 12%

profile of v7, /device:TPU:0, one launch (start us, length us, event | category | flops | bytes accessed | tf_op | source)
XLA Modules:
  0.0 70.0 jit_solution(2378782818447286028)
XLA Ops:
  0.0 1.1 %shard_map.91 = (bf16[176,512]{1,0:T(8,128)(2,1)S(1)}, s32[5,128]{1,0:T(8,128)S(1)}, s32[5,128]{1,0:T(8,128)S(1)}, bf16[64,512]{1,0:T(8,128)(2,1)S(1)}, bf16[16,512]{1,0:T(8,128)(2,1)S(1)}) custom-call(s32[5,128]{1,0:T(8,128)} %bitcast.10, s32[5,128]{1,0:T(8,128)} %bitcast.11, bf16[256,256]{1,0:T(8,128)(2,1)} %mid.1, bf16[640,1024]{1,0:T(8,128)(2,1)} %front_ref.3, ...), custom_call_target="tpu_custom_call" | custom-call | tf_op jit(solution)/shard_map/pallas_call | solution.py:39
  1.1 4.0 %collective-permute-start.5 = (bf16[64,512]{1,0:T(8,128)(2,1)S(1)}, bf16[64,512]{1,0:T(8,128)(2,1)S(1)}, u32[]{:S(2)}, u32[]{:S(2)}) collective-permute-start(bf16[64,512]{1,0:T(8,128)(2,1)S(1)} %get-tuple-element.36.refs_0_), channel_id=1, source_target_pairs={{0,6},{1,7},{2,4},{3,5},{4,2},{5,3},{6,0},{7,1},{8,14},{9,15},{10,... | collective-permute-start | bytes 196616 | tf_op jit(solution)/shard_map/ppermute | solution.py:24
  5.8 1.6 %collective-permute-done.5.refs_6_ = bf16[64,512]{1,0:T(8,128)(2,1)S(1)} collective-permute-done((bf16[64,512]{1,0:T(8,128)(2,1)S(1)}, bf16[64,512]{1,0:T(8,128)(2,1)S(1)}, u32[]{:S(2)}, u32[]{:S(2)}) %collective-permute-start.5) | collective-permute-done | bytes 65568 | tf_op jit(solution)/shard_map/ppermute | solution.py:24
  7.4 2.0 %collective-permute-done.3.refs_4_ = bf16[64,512]{1,0:T(8,128)(2,1)S(1)} collective-permute-done((bf16[64,512]{1,0:T(8,128)(2,1)S(1)}, bf16[64,512]{1,0:T(8,128)(2,1)S(1)}, u32[]{:S(2)}, u32[]{:S(2)}) %collective-permute-start.3) | collective-permute-done | bytes 65568 | tf_op jit(solution)/shard_map/ppermute | solution.py:24
  9.9 1.1 %shard_map.92 = (bf16[384,512]{1,0:T(8,128)(2,1)S(1)}, bf16[384,512]{1,0:T(8,128)(2,1)S(1)}, bf16[640,512]{1,0:T(8,128)(2,1)S(1)}) custom-call(s32[1,3]{1,0:T(1,128)S(1)} %bitcast.3, s32[5,128]{1,0:T(8,128)S(1)} %get-tuple-element.33.code.code_ref, bf16[640,1024]{1,0:T(8,128)(2,1)S(1)} %copy-done.1, bf16[512,256]{1,0:T(8,128)(2,1)S(1)} %copy-done.3), custom_call_target="tpu_custom_call" | custom-call | tf_op jit(solution)/shard_map/pallas_call | solution.py:39
  12.1 1.6 %collective-permute-start.7 = (bf16[320,512]{1,0:T(8,128)(2,1)S(1)}, bf16[320,512]{1,0:T(8,128)(2,1)S(1)}, u32[]{:S(2)}, u32[]{:S(2)}) collective-permute-start(bf16[320,512]{1,0:T(8,128)(2,1)S(1)} %shard_map.96), channel_id=1, source_target_pairs={{0,8},{8,0},{16,24},{24,16},{1,9},{9,1},{17,25},{25,17},{2,10},{10... | collective-permute-start | bytes 983048 | tf_op jit(solution)/shard_map/ppermute | solution.py:24
  14.2 1.6 %collective-permute-start.9 = (bf16[64,512]{1,0:T(8,128)(2,1)S(1)}, bf16[64,512]{1,0:T(8,128)(2,1)S(1)}, u32[]{:S(2)}, u32[]{:S(2)}) collective-permute-start(bf16[64,512]{1,0:T(8,128)(2,1)S(1)} %get-tuple-element.37.refs_1_), channel_id=1, source_target_pairs={{0,8},{8,0},{16,24},{24,16},{1,9},{9,1},{17,25},{25,17},{2,10},{10... | collective-permute-start | bytes 196616 | tf_op jit(solution)/shard_map/ppermute | solution.py:24
  16.5 10.2 %collective-permute-done.8.near_ref = bf16[176,512]{1,0:T(8,128)(2,1)S(1)} collective-permute-done((bf16[176,512]{1,0:T(8,128)(2,1)S(1)}, bf16[176,512]{1,0:T(8,128)(2,1)S(1)}, u32[]{:S(2)}, u32[]{:S(2)}) %collective-permute-start.8) | collective-permute-done | bytes 180256 | tf_op jit(solution)/shard_map/ppermute | solution.py:24
  27.6 1.6 %collective-permute-start.15 = (bf16[64,512]{1,0:T(8,128)(2,1)S(1)}, bf16[64,512]{1,0:T(8,128)(2,1)S(1)}, u32[]{:S(2)}, u32[]{:S(2)}) collective-permute-start(bf16[64,512]{1,0:T(8,128)(2,1)S(1)} %shard_map.99.refs_3_), channel_id=1, source_target_pairs={{0,6},{1,7},{2,4},{3,5},{4,2},{5,3},{6,0},{7,1},{8,14},{9,15},{10,... | collective-permute-start | bytes 196616 | tf_op jit(solution)/shard_map/ppermute | solution.py:24
  29.8 1.4 %collective-permute-start.11 = (bf16[64,512]{1,0:T(8,128)(2,1)S(1)}, bf16[64,512]{1,0:T(8,128)(2,1)S(1)}, u32[]{:S(2)}, u32[]{:S(2)}) collective-permute-start(bf16[64,512]{1,0:T(8,128)(2,1)S(1)} %shard_map.99.refs_3_), channel_id=1, source_target_pairs={{0,2},{1,3},{2,0},{3,1},{4,6},{5,7},{6,4},{7,5},{8,10},{9,11},{10,... | collective-permute-start | bytes 196616 | tf_op jit(solution)/shard_map/ppermute | solution.py:24
  31.1 2.4 %collective-permute-done.15.refs_9_ = bf16[64,512]{1,0:T(8,128)(2,1)S(1)} collective-permute-done((bf16[64,512]{1,0:T(8,128)(2,1)S(1)}, bf16[64,512]{1,0:T(8,128)(2,1)S(1)}, u32[]{:S(2)}, u32[]{:S(2)}) %collective-permute-start.15) | collective-permute-done | bytes 65568 | tf_op jit(solution)/shard_map/ppermute | solution.py:24
  34.3 1.1 %shard_map.95.merged = f32[640,512]{1,0:T(8,128)S(1)} custom-call(s32[1,3]{1,0:T(1,128)S(1)} %bitcast.5, s32[5,128]{1,0:T(8,128)S(1)} %get-tuple-element.33.code.code_ref, bf16[640,512]{1,0:T(8,128)(2,1)S(1)} %get-tuple-element.40.factor_ref, bf16[640,1024]{1,0:T(8,128)(2,1)S(1)} %copy-done.1, bf16[512,512]{1,0:T(8,128)(2,1)S(1)} %get-tuple-element.41.pivots_ref.pivots, ...), custom_call_target="tpu_custom_call" | custom-call | tf_op jit(solution)/shard_map/pallas_call | solution.py:39
  35.4 1.0 %shard_map.98 = (bf16[352,512]{1,0:T(8,128)(2,1)S(1)}, bf16[640,512]{1,0:T(8,128)(2,1)S(1)}) custom-call(s32[1,3]{1,0:T(1,128)S(1)} %bitcast.6, bf16[352,640]{1,0:T(8,128)(2,1)S(1)} %get-tuple-element.39.pick, f32[640,512]{1,0:T(8,128)S(1)} %shard_map.95.merged, bf16[320,512]{1,0:T(8,128)(2,1)S(1)} %collective-permute-done.7.got, ...), custom_call_target="tpu_custom_call" | custom-call | tf_op jit(solution)/shard_map/pallas_call | solution.py:39
  37.1 3.6 %collective-permute-start.20 = (bf16[48,512]{1,0:T(8,128)(2,1)S(1)}, bf16[48,512]{1,0:T(8,128)(2,1)S(1)}, u32[]{:S(2)}, u32[]{:S(2)}) collective-permute-start(bf16[48,512]{1,0:T(8,128)(2,1)S(1)} %get-tuple-element.54.refs_0_), channel_id=1, source_target_pairs={{0,24},{8,16},{16,8},{24,0},{1,25},{9,17},{17,9},{25,1},{2,26},{10... | collective-permute-start | bytes 147464 | tf_op jit(solution)/shard_map/ppermute | solution.py:24
  41.6 1.9 %collective-permute-done.20.refs_3_ = bf16[48,512]{1,0:T(8,128)(2,1)S(1)} collective-permute-done((bf16[48,512]{1,0:T(8,128)(2,1)S(1)}, bf16[48,512]{1,0:T(8,128)(2,1)S(1)}, u32[]{:S(2)}, u32[]{:S(2)}) %collective-permute-start.20) | collective-permute-done | bytes 49184 | tf_op jit(solution)/shard_map/ppermute | solution.py:24
  43.4 2.1 %collective-permute-done.19.refs_1_ = bf16[48,512]{1,0:T(8,128)(2,1)S(1)} collective-permute-done((bf16[48,512]{1,0:T(8,128)(2,1)S(1)}, bf16[48,512]{1,0:T(8,128)(2,1)S(1)}, u32[]{:S(2)}, u32[]{:S(2)}) %collective-permute-start.19) | collective-permute-done | bytes 49184 | tf_op jit(solution)/shard_map/ppermute | solution.py:24
  46.3 1.8 %collective-permute-start.26 = (bf16[96,512]{1,0:T(8,128)(2,1)S(1)}, bf16[96,512]{1,0:T(8,128)(2,1)S(1)}, u32[]{:S(2)}, u32[]{:S(2)}) collective-permute-start(bf16[96,512]{1,0:T(8,128)(2,1)S(1)} %shard_map.103.refs_0_), channel_id=1, source_target_pairs={{0,6},{1,7},{2,4},{3,5},{4,2},{5,3},{6,0},{7,1},{8,14},{9,15},{10,... | collective-permute-start | bytes 294920 | tf_op jit(solution)/shard_map/ppermute | solution.py:24
  48.6 1.3 %collective-permute-start.22 = (bf16[96,512]{1,0:T(8,128)(2,1)S(1)}, bf16[96,512]{1,0:T(8,128)(2,1)S(1)}, u32[]{:S(2)}, u32[]{:S(2)}) collective-permute-start(bf16[96,512]{1,0:T(8,128)(2,1)S(1)} %shard_map.103.refs_0_), channel_id=1, source_target_pairs={{0,2},{1,3},{2,0},{3,1},{4,6},{5,7},{6,4},{7,5},{8,10},{9,11},{10,... | collective-permute-start | bytes 294920 | tf_op jit(solution)/shard_map/ppermute | solution.py:24
  50.2 1.5 %collective-permute-start.28 = (bf16[320,256]{1,0:T(8,128)(2,1)S(1)}, bf16[320,256]{1,0:T(8,128)(2,1)S(1)}, u32[]{:S(2)}, u32[]{:S(2)}) collective-permute-start(bf16[320,256]{1,0:T(8,128)(2,1)S(1)} %get-tuple-element.58), channel_id=1, source_target_pairs={{0,16},{8,24},{16,0},{24,8},{1,17},{9,25},{17,1},{25,9},{2,18},{10... | collective-permute-start | bytes 491528 | tf_op jit(solution)/shard_map/ppermute | solution.py:24
  51.7 1.1 %collective-permute-done.26.refs_6_ = bf16[96,512]{1,0:T(8,128)(2,1)S(1)} collective-permute-done((bf16[96,512]{1,0:T(8,128)(2,1)S(1)}, bf16[96,512]{1,0:T(8,128)(2,1)S(1)}, u32[]{:S(2)}, u32[]{:S(2)}) %collective-permute-start.26) | collective-permute-done | bytes 98336 | tf_op jit(solution)/shard_map/ppermute | solution.py:24
  54.0 1.1 %shard_map.101.merged = f32[640,512]{1,0:T(8,128)S(1)} custom-call(s32[1,3]{1,0:T(1,128)S(1)} %bitcast.7, s32[5,128]{1,0:T(8,128)S(1)} %get-tuple-element.38.code.refs_1_.code_ref, bf16[640,512]{1,0:T(8,128)(2,1)S(1)} %get-tuple-element.46.factor_ref, bf16[640,1024]{1,0:T(8,128)(2,1)S(1)} %copy-done, ...), custom_call_target="tpu_custom_call" | custom-call | tf_op jit(solution)/shard_map/pallas_call | solution.py:39
  56.3 9.0 %collective-permute-done.28.got = bf16[320,256]{1,0:T(8,128)(2,1)S(1)} collective-permute-done((bf16[320,256]{1,0:T(8,128)(2,1)S(1)}, bf16[320,256]{1,0:T(8,128)(2,1)S(1)}, u32[]{:S(2)}, u32[]{:S(2)}) %collective-permute-start.28) | collective-permute-done | bytes 163872 | tf_op jit(solution)/shard_map/ppermute | solution.py:24
  66.1 2.3 %collective-permute-done.17.got = bf16[320,256]{1,0:T(8,128)(2,1)S(1)} collective-permute-done((bf16[320,256]{1,0:T(8,128)(2,1)S(1)}, bf16[320,256]{1,0:T(8,128)(2,1)S(1)}, u32[]{:S(2)}, u32[]{:S(2)}) %collective-permute-start.17) | collective-permute-done | bytes 163872 | tf_op jit(solution)/shard_map/ppermute | solution.py:24
  68.3 1.6 %shard_map.107 = bf16[640,512]{1,0:T(8,128)(2,1)} custom-call(s32[1,3]{1,0:T(1,128)S(1)} %bitcast.9, f32[640,512]{1,0:T(8,128)S(1)} %shard_map.101.merged, bf16[320,256]{1,0:T(8,128)(2,1)S(1)} %collective-permute-done.17.got, bf16[640,320]{1,0:T(8,128)(2,1)S(1)} %shard_map.104.land, bf16[512,256]{1,0:T(8,128)(2,1)S(1)} %get-tuple-element.56.inverse, ...), custom_call_target="tpu_custom_call" | custom-call | tf_op jit(solution)/shard_map/pallas_call | solution.py:39
  (63 shorter events, 12.0 us)
Async XLA Ops:
  1.1 6.2 %collective-permute-start.5 = (bf16[64,512]{1,0:T(8,128)(2,1)S(1)}, bf16[64,512]{1,0:T(8,128)(2,1)S(1)}, u32[]{:S(2)}, u32[]{:S(2)}) collective-permute-start(bf16[64,512]{1,0:T(8,128)(2,1)S(1)} %get-tuple-element.36.refs_0_), channel_id=1, source_target_pairs={{0,6},{1,7},{2,4},{3,5},{4,2},{5,3},{6,0},{7,1},{8,14},{9,15},{10,... | collective-permute-start | bytes 196616 | tf_op jit(solution)/shard_map/ppermute | solution.py:24
  5.1 4.3 %collective-permute-start.3 = (bf16[64,512]{1,0:T(8,128)(2,1)S(1)}, bf16[64,512]{1,0:T(8,128)(2,1)S(1)}, u32[]{:S(2)}, u32[]{:S(2)}) collective-permute-start(bf16[64,512]{1,0:T(8,128)(2,1)S(1)} %get-tuple-element.36.refs_0_), channel_id=1, source_target_pairs={{0,4},{1,5},{2,6},{3,7},{4,0},{5,1},{6,2},{7,3},{8,12},{9,13},{10,... | collective-permute-start | bytes 196616 | tf_op jit(solution)/shard_map/ppermute | solution.py:24
  5.6 4.3 %collective-permute-start.1 = (bf16[64,512]{1,0:T(8,128)(2,1)S(1)}, bf16[64,512]{1,0:T(8,128)(2,1)S(1)}, u32[]{:S(2)}, u32[]{:S(2)}) collective-permute-start(bf16[64,512]{1,0:T(8,128)(2,1)S(1)} %get-tuple-element.36.refs_0_), channel_id=1, source_target_pairs={{0,2},{1,3},{2,0},{3,1},{4,6},{5,7},{6,4},{7,5},{8,10},{9,11},{10,... | collective-permute-start | bytes 196616 | tf_op jit(solution)/shard_map/ppermute | solution.py:24
  5.8 5.2 %collective-permute-start = (bf16[64,512]{1,0:T(8,128)(2,1)S(1)}, bf16[64,512]{1,0:T(8,128)(2,1)S(1)}, u32[]{:S(2)}, u32[]{:S(2)}) collective-permute-start(bf16[64,512]{1,0:T(8,128)(2,1)S(1)} %get-tuple-element.36.refs_0_), channel_id=1, source_target_pairs={{0,1},{1,0},{2,3},{3,2},{4,5},{5,4},{6,7},{7,6},{8,9},{9,8},{10,11... | collective-permute-start | bytes 196616 | tf_op jit(solution)/shard_map/ppermute | solution.py:24
  7.4 3.6 %collective-permute-start.6 = (bf16[64,512]{1,0:T(8,128)(2,1)S(1)}, bf16[64,512]{1,0:T(8,128)(2,1)S(1)}, u32[]{:S(2)}, u32[]{:S(2)}) collective-permute-start(bf16[64,512]{1,0:T(8,128)(2,1)S(1)} %collective-permute-done.5.refs_6_), channel_id=1, source_target_pairs={{0,1},{1,0},{2,3},{3,2},{4,5},{5,4},{6,7},{7,6},{8,9},{9,8},{10,11... | collective-permute-start | bytes 196616 | tf_op jit(solution)/shard_map/ppermute | solution.py:24
  12.1 23.3 %collective-permute-start.7 = (bf16[320,512]{1,0:T(8,128)(2,1)S(1)}, bf16[320,512]{1,0:T(8,128)(2,1)S(1)}, u32[]{:S(2)}, u32[]{:S(2)}) collective-permute-start(bf16[320,512]{1,0:T(8,128)(2,1)S(1)} %shard_map.96), channel_id=1, source_target_pairs={{0,8},{8,0},{16,24},{24,16},{1,9},{9,1},{17,25},{25,17},{2,10},{10... | collective-permute-start | bytes 983048 | tf_op jit(solution)/shard_map/ppermute | solution.py:24
  13.8 12.9 %collective-permute-start.8 = (bf16[176,512]{1,0:T(8,128)(2,1)S(1)}, bf16[176,512]{1,0:T(8,128)(2,1)S(1)}, u32[]{:S(2)}, u32[]{:S(2)}) collective-permute-start(bf16[176,512]{1,0:T(8,128)(2,1)S(1)} %get-tuple-element.42.mine), channel_id=1, source_target_pairs={{0,8},{8,0},{16,24},{24,16},{1,9},{9,1},{17,25},{25,17},{2,10},{10... | collective-permute-start | bytes 540680 | tf_op jit(solution)/shard_map/ppermute | solution.py:24
  14.2 13.3 %collective-permute-start.9 = (bf16[64,512]{1,0:T(8,128)(2,1)S(1)}, bf16[64,512]{1,0:T(8,128)(2,1)S(1)}, u32[]{:S(2)}, u32[]{:S(2)}) collective-permute-start(bf16[64,512]{1,0:T(8,128)(2,1)S(1)} %get-tuple-element.37.refs_1_), channel_id=1, source_target_pairs={{0,8},{8,0},{16,24},{24,16},{1,9},{9,1},{17,25},{25,17},{2,10},{10... | collective-permute-start | bytes 196616 | tf_op jit(solution)/shard_map/ppermute | solution.py:24
  27.6 5.9 %collective-permute-start.15 = (bf16[64,512]{1,0:T(8,128)(2,1)S(1)}, bf16[64,512]{1,0:T(8,128)(2,1)S(1)}, u32[]{:S(2)}, u32[]{:S(2)}) collective-permute-start(bf16[64,512]{1,0:T(8,128)(2,1)S(1)} %shard_map.99.refs_3_), channel_id=1, source_target_pairs={{0,6},{1,7},{2,4},{3,5},{4,2},{5,3},{6,0},{7,1},{8,14},{9,15},{10,... | collective-permute-start | bytes 196616 | tf_op jit(solution)/shard_map/ppermute | solution.py:24
  29.1 4.7 %collective-permute-start.13 = (bf16[64,512]{1,0:T(8,128)(2,1)S(1)}, bf16[64,512]{1,0:T(8,128)(2,1)S(1)}, u32[]{:S(2)}, u32[]{:S(2)}) collective-permute-start(bf16[64,512]{1,0:T(8,128)(2,1)S(1)} %shard_map.99.refs_3_), channel_id=1, source_target_pairs={{0,4},{1,5},{2,6},{3,7},{4,0},{5,1},{6,2},{7,3},{8,12},{9,13},{10,... | collective-permute-start | bytes 196616 | tf_op jit(solution)/shard_map/ppermute | solution.py:24
  29.8 4.3 %collective-permute-start.11 = (bf16[64,512]{1,0:T(8,128)(2,1)S(1)}, bf16[64,512]{1,0:T(8,128)(2,1)S(1)}, u32[]{:S(2)}, u32[]{:S(2)}) collective-permute-start(bf16[64,512]{1,0:T(8,128)(2,1)S(1)} %shard_map.99.refs_3_), channel_id=1, source_target_pairs={{0,2},{1,3},{2,0},{3,1},{4,6},{5,7},{6,4},{7,5},{8,10},{9,11},{10,... | collective-permute-start | bytes 196616 | tf_op jit(solution)/shard_map/ppermute | solution.py:24
  31.1 5.3 %collective-permute-start.10 = (bf16[64,512]{1,0:T(8,128)(2,1)S(1)}, bf16[64,512]{1,0:T(8,128)(2,1)S(1)}, u32[]{:S(2)}, u32[]{:S(2)}) collective-permute-start(bf16[64,512]{1,0:T(8,128)(2,1)S(1)} %shard_map.99.refs_3_), channel_id=1, source_target_pairs={{0,1},{1,0},{2,3},{3,2},{4,5},{5,4},{6,7},{7,6},{8,9},{9,8},{10,11... | collective-permute-start | bytes 196616 | tf_op jit(solution)/shard_map/ppermute | solution.py:24
  33.5 2.9 %collective-permute-start.16 = (bf16[64,512]{1,0:T(8,128)(2,1)S(1)}, bf16[64,512]{1,0:T(8,128)(2,1)S(1)}, u32[]{:S(2)}, u32[]{:S(2)}) collective-permute-start(bf16[64,512]{1,0:T(8,128)(2,1)S(1)} %collective-permute-done.15.refs_9_), channel_id=1, source_target_pairs={{0,1},{1,0},{2,3},{3,2},{4,5},{5,4},{6,7},{7,6},{8,9},{9,8},{10,11... | collective-permute-start | bytes 196616 | tf_op jit(solution)/shard_map/ppermute | solution.py:24
  33.8 2.6 %collective-permute-start.14 = (bf16[64,512]{1,0:T(8,128)(2,1)S(1)}, bf16[64,512]{1,0:T(8,128)(2,1)S(1)}, u32[]{:S(2)}, u32[]{:S(2)}) collective-permute-start(bf16[64,512]{1,0:T(8,128)(2,1)S(1)} %collective-permute-done.13.refs_7_), channel_id=1, source_target_pairs={{0,1},{1,0},{2,3},{3,2},{4,5},{5,4},{6,7},{7,6},{8,9},{9,8},{10,11... | collective-permute-start | bytes 196616 | tf_op jit(solution)/shard_map/ppermute | solution.py:24
  37.1 6.3 %collective-permute-start.20 = (bf16[48,512]{1,0:T(8,128)(2,1)S(1)}, bf16[48,512]{1,0:T(8,128)(2,1)S(1)}, u32[]{:S(2)}, u32[]{:S(2)}) collective-permute-start(bf16[48,512]{1,0:T(8,128)(2,1)S(1)} %get-tuple-element.54.refs_0_), channel_id=1, source_target_pairs={{0,24},{8,16},{16,8},{24,0},{1,25},{9,17},{17,9},{25,1},{2,26},{10... | collective-permute-start | bytes 147464 | tf_op jit(solution)/shard_map/ppermute | solution.py:24
  40.7 4.8 %collective-permute-start.19 = (bf16[48,512]{1,0:T(8,128)(2,1)S(1)}, bf16[48,512]{1,0:T(8,128)(2,1)S(1)}, u32[]{:S(2)}, u32[]{:S(2)}) collective-permute-start(bf16[48,512]{1,0:T(8,128)(2,1)S(1)} %get-tuple-element.54.refs_0_), channel_id=1, source_target_pairs={{0,8},{8,0},{16,24},{24,16},{1,9},{9,1},{17,25},{25,17},{2,10},{10... | collective-permute-start | bytes 147464 | tf_op jit(solution)/shard_map/ppermute | solution.py:24
  40.7 5.5 %collective-permute-start.18 = (bf16[48,512]{1,0:T(8,128)(2,1)S(1)}, bf16[48,512]{1,0:T(8,128)(2,1)S(1)}, u32[]{:S(2)}, u32[]{:S(2)}) collective-permute-start(bf16[48,512]{1,0:T(8,128)(2,1)S(1)} %get-tuple-element.54.refs_0_), channel_id=1, source_target_pairs={{0,16},{8,24},{16,0},{24,8},{1,17},{9,25},{17,1},{25,9},{2,18},{10... | collective-permute-start | bytes 147464 | tf_op jit(solution)/shard_map/ppermute | solution.py:24
  46.3 6.5 %collective-permute-start.26 = (bf16[96,512]{1,0:T(8,128)(2,1)S(1)}, bf16[96,512]{1,0:T(8,128)(2,1)S(1)}, u32[]{:S(2)}, u32[]{:S(2)}) collective-permute-start(bf16[96,512]{1,0:T(8,128)(2,1)S(1)} %shard_map.103.refs_0_), channel_id=1, source_target_pairs={{0,6},{1,7},{2,4},{3,5},{4,2},{5,3},{6,0},{7,1},{8,14},{9,15},{10,... | collective-permute-start | bytes 294920 | tf_op jit(solution)/shard_map/ppermute | solution.py:24
  48.1 5.3 %collective-permute-start.24 = (bf16[96,512]{1,0:T(8,128)(2,1)S(1)}, bf16[96,512]{1,0:T(8,128)(2,1)S(1)}, u32[]{:S(2)}, u32[]{:S(2)}) collective-permute-start(bf16[96,512]{1,0:T(8,128)(2,1)S(1)} %shard_map.103.refs_0_), channel_id=1, source_target_pairs={{0,4},{1,5},{2,6},{3,7},{4,0},{5,1},{6,2},{7,3},{8,12},{9,13},{10,... | collective-permute-start | bytes 294920 | tf_op jit(solution)/shard_map/ppermute | solution.py:24
  48.6 4.8 %collective-permute-start.22 = (bf16[96,512]{1,0:T(8,128)(2,1)S(1)}, bf16[96,512]{1,0:T(8,128)(2,1)S(1)}, u32[]{:S(2)}, u32[]{:S(2)}) collective-permute-start(bf16[96,512]{1,0:T(8,128)(2,1)S(1)} %shard_map.103.refs_0_), channel_id=1, source_target_pairs={{0,2},{1,3},{2,0},{3,1},{4,6},{5,7},{6,4},{7,5},{8,10},{9,11},{10,... | collective-permute-start | bytes 294920 | tf_op jit(solution)/shard_map/ppermute | solution.py:24
  49.9 4.0 %collective-permute-start.21 = (bf16[96,512]{1,0:T(8,128)(2,1)S(1)}, bf16[96,512]{1,0:T(8,128)(2,1)S(1)}, u32[]{:S(2)}, u32[]{:S(2)}) collective-permute-start(bf16[96,512]{1,0:T(8,128)(2,1)S(1)} %shard_map.103.refs_0_), channel_id=1, source_target_pairs={{0,1},{1,0},{2,3},{3,2},{4,5},{5,4},{6,7},{7,6},{8,9},{9,8},{10,11... | collective-permute-start | bytes 294920 | tf_op jit(solution)/shard_map/ppermute | solution.py:24
  50.2 15.1 %collective-permute-start.28 = (bf16[320,256]{1,0:T(8,128)(2,1)S(1)}, bf16[320,256]{1,0:T(8,128)(2,1)S(1)}, u32[]{:S(2)}, u32[]{:S(2)}) collective-permute-start(bf16[320,256]{1,0:T(8,128)(2,1)S(1)} %get-tuple-element.58), channel_id=1, source_target_pairs={{0,16},{8,24},{16,0},{24,8},{1,17},{9,25},{17,1},{25,9},{2,18},{10... | collective-permute-start | bytes 491528 | tf_op jit(solution)/shard_map/ppermute | solution.py:24
  52.8 15.5 %collective-permute-start.17 = (bf16[320,256]{1,0:T(8,128)(2,1)S(1)}, bf16[320,256]{1,0:T(8,128)(2,1)S(1)}, u32[]{:S(2)}, u32[]{:S(2)}) collective-permute-start(bf16[320,256]{1,0:T(8,128)(2,1)S(1)} %get-tuple-element.53), channel_id=1, source_target_pairs={{0,16},{8,24},{16,0},{24,8},{1,17},{9,25},{17,1},{25,9},{2,18},{10... | collective-permute-start | bytes 491528 | tf_op jit(solution)/shard_map/ppermute | solution.py:24
  53.4 2.5 %collective-permute-start.25 = (bf16[96,512]{1,0:T(8,128)(2,1)S(1)}, bf16[96,512]{1,0:T(8,128)(2,1)S(1)}, u32[]{:S(2)}, u32[]{:S(2)}) collective-permute-start(bf16[96,512]{1,0:T(8,128)(2,1)S(1)} %collective-permute-done.24.refs_4_), channel_id=1, source_target_pairs={{0,1},{1,0},{2,3},{3,2},{4,5},{5,4},{6,7},{7,6},{8,9},{9,8},{10,11... | collective-permute-start | bytes 294920 | tf_op jit(solution)/shard_map/ppermute | solution.py:24
  (11 other events, 62.8 us)
